TPU v7x, 32 devices: a whole 2x2x4 slice. The times are simulated.
32 devices in a mesh: shot: 4 (over z), rcv: 8 (over y, x, core).
Axes of the slice: x: 2, y: 2, z: 4, core: 2. Of those that a mesh axis runs over, the one named last changes fastest.
Arguments:
- shot_side: bfloat16 [2, 2048, 1024], P(None, 'shot', 'rcv'), may hold values from -6 to 6
- rcv_side: bfloat16 [1024, 12288], P('shot', 'rcv'), may hold values from -0.125 to 0.125
Outputs:
- multiples: bfloat16 [2048, 12288], P('shot', 'rcv')
All inputs are finite; a program needn't handle non-finite values.
Results may differ from a plain program's by a relative error of at most 0.001.
Values may be sent and summed in bfloat16 or wider, within the bound.
No kernel may reach another device: no remote copies, remote signals or barrier semaphores. Data moves between devices by JAX's collectives and lax.ppermute only.
A program may use at most 64 MiB of HBM per device.

v0:
```python
import jax
import jax.numpy as jnp
from jax import lax
from jax.sharding import PartitionSpec as P

STEPS = 4


def passed_along(value, axis, steps):
    count = lax.axis_size(axis)
    pairs = [(source, (source + steps) % count) for source in range(count)]
    return lax.ppermute(value, axis, pairs)


def from_root(value, axis, root):
    mine = lax.axis_index(axis) == root
    return lax.psum(jnp.where(mine, value, jnp.zeros_like(value)), axis)


def complex_product(left, right):
    half = right.shape[1] // 2
    first = jnp.dot(left[0], right, preferred_element_type=jnp.float32)
    second = jnp.dot(left[1], right, preferred_element_type=jnp.float32)
    real_part = first[:, :half] - second[:, half:]
    imag_part = first[:, half:] + second[:, :half]
    return jnp.concatenate([real_part, imag_part], axis=1)


def turn_panel(panel):
    return passed_along(panel, "shot", 1)


def fetch_piece(shot_side, root):
    return from_root(shot_side, "rcv", root)


def on_device(shot_side, rcv_side):
    cycle_size = lax.axis_size("shot")
    pieces = lax.axis_size("rcv") // cycle_size
    shot_index = lax.axis_index("shot")
    total = jnp.zeros((shot_side.shape[1], rcv_side.shape[1]), jnp.float32)
    current = rcv_side
    for step in range(STEPS):
        if step > 0:
            current = turn_panel(current)
        block_id = (shot_index - step) % cycle_size
        gotten = [
            fetch_piece(shot_side, block_id * pieces + piece_id) for piece_id in range(pieces)
        ]
        total = total + complex_product(jnp.concatenate(gotten, axis=2), current)
    return total.astype(jnp.bfloat16)


def solution(mesh):
    return jax.shard_map(
        on_device,
        mesh=mesh,
        in_specs=(P(None, "shot", "rcv"), P("shot", "rcv")),
        out_specs=P("shot", "rcv"),
        check_vma=False,
    )
```

profile of v0, /device:TPU:0, one launch (start us, length us, event | category | flops | bytes accessed | tf_op | source)
XLA Modules:
  0.0 113.8 jit_solution(5330745418244322475)
XLA Ops:
  6.5 2.3 %broadcast_select_fusion = (bf16[2,512,128]{2,1,0:T(8,128)(2,1)}, bf16[2,512,128]{2,1,0:T(8,128)(2,1)}, bf16[2,512,128]{2,1,0:T(8,128)(2,1)}, bf16[2,512,128]{2,...) fusion(bf16[2,512,128]{2,1,0:T(8,128)(2,1)} %param.2, ...), kind=kLoop, calls=%fused_computation.28 | loop fusion | flops 1048576 | bytes 2359304 | tf_op jit(solution)/shard_map/jit(_where)/select_n | solution.py:17
  8.8 0.0 all-reduce.3.cloned.1.call-update
  8.8 1.1 copy-done
  10.0 3.0 %collective-permute-start = (bf16[256,1536]{1,0:T(8,128)(2,1)S(1)}, bf16[256,1536]{1,0:T(8,128)(2,1)S(1)}, u32[]{:S(2)}, u32[]{:S(2)}) collective-permute-start(bf16[256,1536]{1,0:T(8,128)(2,1)S(1)} %copy-done), channel_id=1, source_target_pairs={{0,8},{8,16},{16,24},{24,0},{1,9},{9,17},{17,25},{25,1},{2,10},{10... | collective-permute-start | bytes 2359304 | tf_op jit(solution)/shard_map/ppermute | solution.py:12
  13.0 19.6 %collective-permute-done = bf16[256,1536]{1,0:T(8,128)(2,1)S(1)} collective-permute-done((bf16[256,1536]{1,0:T(8,128)(2,1)S(1)}, bf16[256,1536]{1,0:T(8,128)(2,1)S(1)}, u32[]{:S(2)}, u32[]{:S(2)}) %collective-permute-start) | collective-permute-done | bytes 786464 | tf_op jit(solution)/shard_map/ppermute | solution.py:12
  32.5 44.5 %all-reduce.3.cloned.1.call-done = (bf16[2,512,128]{2,1,0:T(8,128)(2,1)}, bf16[2,512,128]{2,1,0:T(8,128)(2,1)}, bf16[2,512,128]{2,1,0:T(8,128)(2,1)}, bf16[2,512...) async-done(((bf16[2,512,128]{2,1,0:T(8,128)(2,1)}, ...) | async-done | bytes 2097168 | tf_op jit(solution)/shard_map/psum | solution.py:17
  77.0 1.0 constant_dynamic-update-slice_fusion.1
  78.0 1.0 constant_dynamic-update-slice_fusion
  79.0 0.6 fusion.9
  79.6 0.6 fusion.10
  80.2 0.3 copy-done.6
  80.6 0.0 copy-done.5
  80.7 0.0 copy-done.4
  80.8 0.5 copy-done.3
  81.2 0.1 constant_dynamic-update-slice_fusion.2
  81.3 0.0 copy-done.2
  81.3 0.1 constant_dynamic-update-slice_fusion.4
  81.4 0.6 fusion.7
  81.9 0.6 fusion.8
  82.5 0.4 copy-done.1
  82.9 0.1 constant_dynamic-update-slice_fusion.6
  83.0 0.4 slice_subtract_fusion.2
  83.3 0.4 slice_subtract_fusion.3
  83.8 1.5 %collective-permute-start.2 = (bf16[256,1536]{1,0:T(8,128)(2,1)S(1)}, bf16[256,1536]{1,0:T(8,128)(2,1)S(1)}, u32[]{:S(2)}, u32[]{:S(2)}) collective-permute-start(bf16[256,1536]{1,0:T(8,128)(2,1)S(1)} %collective-permute-done.1), channel_id=1, source_target_pairs={{0,8},{8,16},{16,24},{24,0},{1,9},{9,17},{17,25},{25,1},{2,10},{10... | collective-permute-start | bytes 2359304 | tf_op jit(solution)/shard_map/ppermute | solution.py:12
  85.3 0.6 fusion.5
  85.9 0.6 fusion.6
  86.4 0.4 slice_subtract_fusion.1
  86.8 17.1 %collective-permute-done.2 = bf16[256,1536]{1,0:T(8,128)(2,1)S(1)} collective-permute-done((bf16[256,1536]{1,0:T(8,128)(2,1)S(1)}, bf16[256,1536]{1,0:T(8,128)(2,1)S(1)}, u32[]{:S(2)}, u32[]{:S(2)}) %collective-permute-start.2) | collective-permute-done | bytes 786464 | tf_op jit(solution)/shard_map/ppermute | solution.py:12
  103.9 0.6 fusion.3
  104.5 0.6 fusion.4
  105.1 0.4 slice_subtract_fusion
  105.5 1.5 %fusion.2 = bf16[512,1536]{1,0:T(8,128)(2,1)} fusion(f32[512,768]{1,0:T(8,128)S(1)} %get-tuple-element.20, f32[512,768]{1,0:T(8,128)S(1)} %get-tuple-element.19, f32[512,768]{1,0:T(8,128)S(1)} %get-tuple-element.18, f32[512,768]{1,0:T(8,128)S(1)} %get-tuple-element.17, f32[512,768]{1,0:T(8,128)S(1)} %get-tuple-element.16, ...), kind=kLoop, calls=%fused_computation.3 | loop fusion | flops 6291456 | bytes 14155776 | tf_op jit(solution)/shard_map/convert_element_type | solution.py:51
  (13 shorter events, 0.2 us)
Async XLA Ops:
  6.5 70.5 %all-reduce.3.cloned.1.call-start = ((), (), s32[]{:S(2)}) async-start(), calls=%async_computation | async-start | bytes 4194304 | tf_op jit(solution)/shard_map/psum | solution.py:17
  8.8 1.1 copy-start
  10.0 22.6 %collective-permute-start = (bf16[256,1536]{1,0:T(8,128)(2,1)S(1)}, bf16[256,1536]{1,0:T(8,128)(2,1)S(1)}, u32[]{:S(2)}, u32[]{:S(2)}) collective-permute-start(bf16[256,1536]{1,0:T(8,128)(2,1)S(1)} %copy-done), channel_id=1, source_target_pairs={{0,8},{8,16},{16,24},{24,0},{1,9},{9,17},{17,25},{25,1},{2,10},{10... | collective-permute-start | bytes 2359304 | tf_op jit(solution)/shard_map/ppermute | solution.py:12
  32.5 51.2 %collective-permute-start.1 = (bf16[256,1536]{1,0:T(8,128)(2,1)S(1)}, bf16[256,1536]{1,0:T(8,128)(2,1)S(1)}, u32[]{:S(2)}, u32[]{:S(2)}) collective-permute-start(bf16[256,1536]{1,0:T(8,128)(2,1)S(1)} %collective-permute-done), channel_id=1, source_target_pairs={{0,8},{8,16},{16,24},{24,0},{1,9},{9,17},{17,25},{25,1},{2,10},{10... | collective-permute-start | bytes 2359304 | tf_op jit(solution)/shard_map/ppermute | solution.py:12
  79.6 1.0 copy-start.6
  79.6 1.0 copy-start.5
  79.6 1.1 copy-start.4
  80.2 1.0 copy-start.3
  80.2 1.1 copy-start.2
  81.9 1.0 copy-start.1
  83.8 20.2 %collective-permute-start.2 = (bf16[256,1536]{1,0:T(8,128)(2,1)S(1)}, bf16[256,1536]{1,0:T(8,128)(2,1)S(1)}, u32[]{:S(2)}, u32[]{:S(2)}) collective-permute-start(bf16[256,1536]{1,0:T(8,128)(2,1)S(1)} %collective-permute-done.1), channel_id=1, source_target_pairs={{0,8},{8,16},{16,24},{24,0},{1,9},{9,17},{17,25},{25,1},{2,10},{10... | collective-permute-start | bytes 2359304 | tf_op jit(solution)/shard_map/ppermute | solution.py:12
Sparse Core Ops, SparseCore 0:
  11.3 65.6 all-reduce.2
where the time goes:
time: 114 us
  waiting for transfers between devices  81.1 us (71%)
  between operations  13.5 us (12%)
  other arithmetic  5.35 us (5%)
  local copies, waits for them, and re-layouts  4.68 us (4%)
  matrix products  4.59 us (4%)
  starting transfers between devices  4.57 us (4%)
    psum x1, waiting for transfers between devices, from_root(): return lax.psum(jnp.where(mine, value, jnp.zeros_like(value)), axis)  44.5 us
    ppermute x3, waiting for transfers between devices, passed_along(): return lax.ppermute(value, axis, pairs)  36.6 us
    ppermute x3, starting transfers between devices, passed_along(): return lax.ppermute(value, axis, pairs)  4.56 us
    unnamed x18, local copies, waits for them, and re-layouts  3.48 us
    dot_general x4, matrix products, complex_product(): first = jnp.dot(left[0], right, preferred_element_type=jnp.float32)  2.3 us
    dot_general x4, matrix products, complex_product(): second = jnp.dot(left[1], right, preferred_element_type=jnp.float32)  2.29 us
  transfers between devices with their start and end apart: 4, of which 3 were waited for; matrix products, arithmetic and copies ran while one was open for 6% of the time, Pallas kernels for 0%

commit v1 on v0

--- a/solution.py
+++ b/solution.py
@@ -1,9 +1,12 @@
 import jax
 import jax.numpy as jnp
 from jax import lax
+from jax.experimental import pallas as pl
+from jax.experimental.pallas import tpu as pltpu
 from jax.sharding import PartitionSpec as P
 
 STEPS = 4
+VMEM_LIMIT = 16 * 1024 * 1024
 
 
 def passed_along(value, axis, steps):
@@ -26,15 +29,7 @@
     return jnp.concatenate([real_part, imag_part], axis=1)
 
 
-def turn_panel(panel):
-    return passed_along(panel, "shot", 1)
-
-
-def fetch_piece(shot_side, root):
-    return from_root(shot_side, "rcv", root)
-
-
-def on_device(shot_side, rcv_side):
+def ring_on_device(shot_side, rcv_side):
     cycle_size = lax.axis_size("shot")
     pieces = lax.axis_size("rcv") // cycle_size
     shot_index = lax.axis_index("shot")
@@ -42,18 +37,193 @@
     current = rcv_side
     for step in range(STEPS):
         if step > 0:
-            current = turn_panel(current)
+            current = passed_along(current, "shot", 1)
         block_id = (shot_index - step) % cycle_size
         gotten = [
-            fetch_piece(shot_side, block_id * pieces + piece_id) for piece_id in range(pieces)
+            from_root(shot_side, "rcv", block_id * pieces + piece_id)
+            for piece_id in range(pieces)
         ]
         total = total + complex_product(jnp.concatenate(gotten, axis=2), current)
     return total.astype(jnp.bfloat16)
 
 
+SWAP_OUTER = [(0, 1), (1, 0), (2, 3), (3, 2)]
+SWAP_INNER = [(1, 2), (2, 1)]
+OUTWARD = [(1, 0), (2, 3)]
+ACROSS = [(0, 2), (3, 1)]
+CHUNKS = 3
+
+
+def flipped(value, bit):
+    return lax.ppermute(value, "rcv", [(i, i ^ bit) for i in range(8)])
+
+
+def after(value, *others):
+    return lax.optimization_barrier((value, *others))[0]
+
+
+def over_shot(values, pairs):
+    return [lax.ppermute(value, "shot", pairs) for value in values]
+
+
+def kernel_call(kernel, out_shape, flops, count, **options):
+    return pl.pallas_call(
+        kernel,
+        out_shape=out_shape,
+        in_specs=[pl.BlockSpec(memory_space=pltpu.VMEM)] * count,
+        out_specs=options.pop("out_specs", pl.BlockSpec(memory_space=pltpu.VMEM)),
+        compiler_params=pltpu.CompilerParams(vmem_limit_bytes=VMEM_LIMIT),
+        cost_estimate=pl.CostEstimate(flops=flops, bytes_accessed=4 << 20, transcendentals=0),
+        **options,
+    )
+
+
+def stack_kernel(own, x, y, d, out):
+    rcv = lax.axis_index("rcv")
+    core0 = rcv % 2 == 0
+    here = rcv // 2
+
+    for rel, source in enumerate((own, x, y, d)):
+        blk = here ^ rel
+
+        def body(part, carry):
+            m, o = source[part], source[2 + part]
+            low = jnp.where(core0, m, o)
+            high = jnp.where(core0, o, m)
+            both = jnp.concatenate([low, high], axis=1)
+            out[blk, part, :, 0:256] = both
+            out[blk, 1 - part, :, 256:512] = jnp.where(part == 0, both, -both)
+            return carry
+
+        lax.fori_loop(0, 2, body, 0)
+
+
+def tall(right, at, width):
+    half = right.shape[1] // 2
+    return jnp.concatenate([right[:, at:at + width], right[:, half + at:half + at + width]], axis=0)
+
+
+def near_kernel(left, own, near, out):
+    z = lax.axis_index("shot")
+    half = own.shape[1] // 2
+    width = half // CHUNKS
+    for i in range(CHUNKS):
+        right = jnp.concatenate([tall(own, i * width, width), tall(near, i * width, width)], axis=0)
+
+        def body(part, carry):
+            rows = jnp.concatenate([left[z, part], left[z ^ 1, part]], axis=1)
+            out[CHUNKS * part + i] = jnp.dot(rows, right, preferred_element_type=jnp.float32)
+            return carry
+
+        lax.fori_loop(0, 2, body, 0)
+
+
+def far_block(which, z):
+    low = z < 2
+    return jnp.where(low, 2, 1) if which == 0 else jnp.where(low, 3, 0)
+
+
+def add_far(which, z, first, count, left, acc, from_inner, from_outer, out):
+    blk = far_block(which, z)
+    inner = (z == 1) | (z == 2)
+    half = from_inner.shape[1] // 2
+    width = half // count
+    for i in range(count):
+        right = jnp.where(inner, tall(from_inner, i * width, width), tall(from_outer, i * width, width))
+
+        def body(part, carry):
+            at = CHUNKS * part + first + i
+            total = acc[at] + jnp.dot(left[blk, part], right, preferred_element_type=jnp.float32)
+            out[at] = total.astype(out.dtype)
+            return carry
+
+        lax.fori_loop(0, 2, body, 0)
+
+
+def far_kernel(left, acc, from_inner, from_outer, out):
+    z = lax.axis_index("shot")
+    add_far(0, z, 0, CHUNKS, left, acc, from_inner, from_outer, out)
+
+
+def copies_out(buf, out, sem, chunks):
+    width = buf.shape[2]
+    return [
+        pltpu.make_async_copy(buf.at[at], out.at[:, pl.ds(at * width, width)], sem.at[at])
+        for at in chunks
+    ]
+
+
+def finish(first, left, acc, pairs, out, buf, sem):
+    z = lax.axis_index("shot")
+    for i, (from_inner, from_outer) in enumerate(pairs):
+        add_far(1, z, first + i, 1, left, acc, from_inner, from_outer, buf)
+    copies = copies_out(buf, out, sem, [CHUNKS * part + first + i for part in range(2) for i in range(len(pairs))])
+    for copy in copies:
+        copy.start()
+    for copy in copies:
+        copy.wait()
+
+
+def first_kernel(left, acc, inner_a, outer_a, inner_b, outer_b, out, buf, sem):
+    finish(0, left, acc, [(inner_a, outer_a), (inner_b, outer_b)], out, buf, sem)
+
+
+def last_kernel(left, acc, from_inner, from_outer, _, out, buf, sem):
+    finish(CHUNKS - 1, left, acc, [(from_inner, from_outer)], out, buf, sem)
+
+
+def cut(value):
+    half = value.shape[1] // 2
+    width = half // CHUNKS
+    return [
+        jnp.concatenate([value[:, at:at + width], value[:, half + at:half + at + width]], axis=1)
+        for at in range(0, half, width)
+    ]
+
+
+def line_on_device(shot_side, rcv_side):
+    shots, cols = shot_side.shape[1], rcv_side.shape[1]
+    width = cols // 2 // CHUNKS
+    m1, = over_shot([rcv_side], SWAP_INNER)
+    near, = over_shot([rcv_side], SWAP_OUTER)
+    m2, = over_shot([rcv_side], ACROSS)
+    s2, = over_shot([m1], OUTWARD)
+    m2 = cut(m2)
+    s3 = over_shot(m2, OUTWARD)
+
+    chip = jnp.concatenate([shot_side, flipped(shot_side, 1)])
+    x, y = flipped(chip, 2), flipped(chip, 4)
+    x, y, near, m1 = lax.optimization_barrier((x, y, near, m1))
+    d = flipped(x, 4)
+
+    left = kernel_call(stack_kernel, jax.ShapeDtypeStruct((4, 2, shots, 512), jnp.bfloat16), 1, 4)(chip, x, y, d)
+    block_flops = 8 * shots * 256 * (cols // 2)
+    acc_shape = jax.ShapeDtypeStruct((2 * CHUNKS, shots, width), jnp.float32)
+    acc = kernel_call(near_kernel, acc_shape, 2 * block_flops, 3)(left, rcv_side, near)
+    acc = kernel_call(far_kernel, acc_shape, block_flops, 4)(left, acc, m1, s2)
+
+    out_shape = jax.ShapeDtypeStruct((shots, cols), jnp.bfloat16)
+    scratch = [pltpu.VMEM((2 * CHUNKS, shots, width), jnp.bfloat16), pltpu.SemaphoreType.DMA((2 * CHUNKS,))]
+    in_place = pl.BlockSpec(memory_space=pl.ANY)
+    out = kernel_call(
+        first_kernel, out_shape, block_flops * 2 // 3, 6, out_specs=in_place, scratch_shapes=scratch
+    )(left, acc, m2[0], s3[0], m2[1], s3[1])
+    return pl.pallas_call(
+        last_kernel,
+        out_shape=out_shape,
+        in_specs=[pl.BlockSpec(memory_space=pltpu.VMEM)] * 4 + [in_place],
+        out_specs=in_place,
+        scratch_shapes=scratch,
+        input_output_aliases={4: 0},
+        compiler_params=pltpu.CompilerParams(vmem_limit_bytes=VMEM_LIMIT),
+        cost_estimate=pl.CostEstimate(flops=block_flops // 3, bytes_accessed=1 << 20, transcendentals=0),
+    )(left, acc, m2[2], s3[2], out)
+
+
 def solution(mesh):
+    line = mesh.shape["shot"] == 4 and mesh.shape["rcv"] == 8 and STEPS == 4
     return jax.shard_map(
-        on_device,
+        line_on_device if line else ring_on_device,
         mesh=mesh,
         in_specs=(P(None, "shot", "rcv"), P("shot", "rcv")),
         out_specs=P("shot", "rcv"),

time: 114 us -> 63.5 us (0.56)
  waiting for transfers between devices: 81.1 us -> 34.8 us
  starting transfers between devices: 4.57 us -> 18.3 us
  between operations: 13.5 us -> 0.16 us
  Pallas kernels: 0 us -> 8.87 us
  other arithmetic: 5.35 us -> 0.06 us
  matrix products: 4.59 us -> 0 us
  local copies, waits for them, and re-layouts: 4.68 us -> 1.06 us
    psum x1 -> x0, waiting for transfers between devices: 44.5 us -> none  [from_root(): return lax.psum(jnp.where(mine, value, jnp.zeros_like(value)), axis)]
    ppermute x3 -> x11, starting transfers between devices: 4.56 us -> 18.3 us  [the longest x7 13.3 us: over_shot(): return [lax.ppermute(value, 'shot', pairs) for value in values]]
    pallas_call x0 -> x5, Pallas kernels: none -> 8.87 us  [the longest x1 2.68 us: line_on_device(): kernel_call(near_kernel, acc_shape, 2 * block_flops, 3)]
    dot_general x8 -> x0, matrix products: 4.59 us -> none  [the longest x4 2.3 us: complex_product(): first = jnp.dot(left[0], right, preferred_element_type=jnp.float32)]
    unnamed x18 -> x3, local copies, waits for them, and re-layouts: 3.48 us -> 0.98 us
    select_n x1 -> x0, other arithmetic: 2.28 us -> none  [from_root(): return lax.psum(jnp.where(mine, value, jnp.zeros_like(value)), axis)]
    ppermute x3 -> x11, waiting for transfers between devices: 36.6 us -> 34.8 us  [the longest x7 24.1 us: over_shot(): return [lax.ppermute(value, 'shot', pairs) for value in values]]
    sub x4 -> x0, other arithmetic: 1.56 us -> none  [complex_product(): real_part = first[:, :half] - second[:, half:]]
  transfers between devices with their start and end apart: 4 -> 11, of which waited for: 3 -> 7; matrix products, arithmetic and copies ran while one was open for 6% -> 2% of each run, Pallas kernels for 0% -> 12%
where the time goes in v1:
time: 63.5 us; the launch traced here: 63.2 us
  waiting for transfers between devices  34.8 us (55%)
  starting transfers between devices  18.3 us (29%)
  Pallas kernels  8.87 us (14%)
  local copies, waits for them, and re-layouts  1.06 us (2%)
    ppermute x7, waiting for transfers between devices, over_shot(): return [lax.ppermute(value, 'shot', pairs) for value in values]  24.1 us
    ppermute x7, starting transfers between devices, over_shot(): return [lax.ppermute(value, 'shot', pairs) for value in values]  13.3 us
    ppermute x4, waiting for transfers between devices, flipped(): return lax.ppermute(value, 'rcv', [(i, i ^ bit) for i in range(8)])  10.7 us
    ppermute x4, starting transfers between devices, flipped(): return lax.ppermute(value, 'rcv', [(i, i ^ bit) for i in range(8)])  5.05 us
    pallas_call x1, Pallas kernels, line_on_device(): kernel_call(near_kernel, acc_shape, 2 * block_flops, 3)  2.68 us
    pallas_call x1, Pallas kernels, line_on_device(): kernel_call(first_kernel, out_shape, block_flops * 2 // 3, 6, out_specs=i...  2.26 us
    pallas_call x1, Pallas kernels, line_on_device(): acc = kernel_call(far_kernel, acc_shape, block_flops, 4)(left, acc, m1, s2)  1.87 us
    pallas_call x1, Pallas kernels, line_on_device(): pl.pallas_call(last_kernel, out_shape=out_shape, in_specs=[pl.BlockSpec(m...  1.47 us
  transfers between devices with their start and end apart: 11, of which 7 were waited for; matrix products, arithmetic and copies ran while one was open for 2% of the time, Pallas kernels for 12%

profile of v1, /device:TPU:0, one launch (start us, length us, event | category | flops | bytes accessed | tf_op | source)
XLA Modules:
  0.0 63.2 jit_solution(16792744229861110332)
XLA Ops:
  0.0 0.5 collective-permute-start
  0.5 0.7 %collective-permute-start.4 = (bf16[256,1536]{1,0:T(8,128)(2,1)}, bf16[256,1536]{1,0:T(8,128)(2,1)S(1)}, u32[]{:S(2)}, u32[]{:S(2)}) collective-permute-start(bf16[256,1536]{1,0:T(8,128)(2,1)} %own.1), channel_id=1, source_target_pairs={{8,16},{16,8},{9,17},{17,9},{10,18},{18,10},{11,19},{19,11},{12,20... | collective-permute-start | bytes 2359304 | tf_op jit(solution)/shard_map/ppermute | solution.py:66
  1.2 5.4 %collective-permute-start.3 = (bf16[256,1536]{1,0:T(8,128)(2,1)}, bf16[256,1536]{1,0:T(8,128)(2,1)S(1)}, u32[]{:S(2)}, u32[]{:S(2)}) collective-permute-start(bf16[256,1536]{1,0:T(8,128)(2,1)} %own.1), channel_id=1, source_target_pairs={{0,8},{8,0},{16,24},{24,16},{1,9},{9,1},{17,25},{25,17},{2,10},{10... | collective-permute-start | bytes 2359304 | tf_op jit(solution)/shard_map/ppermute | solution.py:66
  6.6 1.9 %collective-permute-start.7 = (bf16[256,1536]{1,0:T(8,128)(2,1)}, bf16[256,1536]{1,0:T(8,128)(2,1)S(1)}, u32[]{:S(2)}, u32[]{:S(2)}) collective-permute-start(bf16[256,1536]{1,0:T(8,128)(2,1)} %own.1), channel_id=1, source_target_pairs={{0,16},{24,8},{1,17},{25,9},{2,18},{26,10},{3,19},{27,11},{4,20},{... | collective-permute-start | bytes 2359304 | tf_op jit(solution)/shard_map/ppermute | solution.py:66
  8.4 1.0 %constant_dynamic-update-slice_fusion.1 = bf16[4,512,128]{2,1,0:T(8,128)(2,1)S(1)} fusion(bf16[2,512,128]{2,1,0:T(8,128)(2,1)} %param.2), kind=kLoop, calls=%fused_computation.4 | loop fusion | bytes 524288
  9.4 0.0 collective-permute-done
  9.5 1.6 %collective-permute-start.1 = (bf16[4,512,128]{2,1,0:T(8,128)(2,1)S(1)}, bf16[4,512,128]{2,1,0:T(8,128)(2,1)S(1)}, u32[]{:S(2)}, u32[]{:S(2)}) collective-permute-start(bf16[4,512,128]{2,1,0:T(8,128)(2,1)S(1)} %constant_dynamic-update-slice_fusion.own), channel_id=1, source_target_pairs={{0,2},{1,3},{2,0},{3,1},{4,6},{5,7},{6,4},{7,5},{8,10},{9,11},{10,... | collective-permute-start | bytes 1572872 | tf_op jit(solution)/shard_map/ppermute | solution.py:58
  11.0 1.5 %collective-permute-start.2 = (bf16[4,512,128]{2,1,0:T(8,128)(2,1)S(1)}, bf16[4,512,128]{2,1,0:T(8,128)(2,1)S(1)}, u32[]{:S(2)}, u32[]{:S(2)}) collective-permute-start(bf16[4,512,128]{2,1,0:T(8,128)(2,1)S(1)} %constant_dynamic-update-slice_fusion.own), channel_id=1, source_target_pairs={{0,4},{1,5},{2,6},{3,7},{4,0},{5,1},{6,2},{7,3},{8,12},{9,13},{10,... | collective-permute-start | bytes 1572872 | tf_op jit(solution)/shard_map/ppermute | solution.py:58
  12.5 0.0 collective-permute-done.4.from_inner
  12.5 1.3 %collective-permute-start.6 = (bf16[256,1536]{1,0:T(8,128)(2,1)S(1)}, bf16[256,1536]{1,0:T(8,128)(2,1)S(1)}, u32[]{:S(2)}, u32[]{:S(2)}) collective-permute-start(bf16[256,1536]{1,0:T(8,128)(2,1)S(1)} %collective-permute-done.4.from_inner), channel_id=1, source_target_pairs={{8,0},{16,24},{9,1},{17,25},{10,2},{18,26},{11,3},{19,27},{12,4},{... | collective-permute-start | bytes 2359304 | tf_op jit(solution)/shard_map/ppermute | solution.py:66
  13.8 9.5 %collective-permute-done.1.x = bf16[4,512,128]{2,1,0:T(8,128)(2,1)S(1)} collective-permute-done((bf16[4,512,128]{2,1,0:T(8,128)(2,1)S(1)}, bf16[4,512,128]{2,1,0:T(8,128)(2,1)S(1)}, u32[]{:S(2)}, u32[]{:S(2)}) %collective-permute-start.1) | collective-permute-done | bytes 524320 | tf_op jit(solution)/shard_map/ppermute | solution.py:58
  23.3 1.2 %collective-permute-done.2.y = bf16[4,512,128]{2,1,0:T(8,128)(2,1)S(1)} collective-permute-done((bf16[4,512,128]{2,1,0:T(8,128)(2,1)S(1)}, bf16[4,512,128]{2,1,0:T(8,128)(2,1)S(1)}, u32[]{:S(2)}, u32[]{:S(2)}) %collective-permute-start.2) | collective-permute-done | bytes 524320 | tf_op jit(solution)/shard_map/ppermute | solution.py:58
  24.5 0.3 collective-permute-done.3.near
  24.8 1.5 %collective-permute-start.5 = (bf16[4,512,128]{2,1,0:T(8,128)(2,1)S(1)}, bf16[4,512,128]{2,1,0:T(8,128)(2,1)S(1)}, u32[]{:S(2)}, u32[]{:S(2)}) collective-permute-start(bf16[4,512,128]{2,1,0:T(8,128)(2,1)S(1)} %collective-permute-done.1.x), channel_id=1, source_target_pairs={{0,4},{1,5},{2,6},{3,7},{4,0},{5,1},{6,2},{7,3},{8,12},{9,13},{10,... | collective-permute-start | bytes 1572872 | tf_op jit(solution)/shard_map/ppermute | solution.py:58
  26.3 14.6 %collective-permute-done.7 = bf16[256,1536]{1,0:T(8,128)(2,1)S(1)} collective-permute-done((bf16[256,1536]{1,0:T(8,128)(2,1)}, bf16[256,1536]{1,0:T(8,128)(2,1)S(1)}, u32[]{:S(2)}, u32[]{:S(2)}) %collective-permute-start.7) | collective-permute-done | bytes 786464 | tf_op jit(solution)/shard_map/ppermute | solution.py:66
  40.9 0.1 fusion
  41.0 1.3 %collective-permute-start.10 = (bf16[256,512]{1,0:T(8,128)(2,1)S(1)}, bf16[256,512]{1,0:T(8,128)(2,1)S(1)}, u32[]{:S(2)}, u32[]{:S(2)}) collective-permute-start(bf16[256,512]{1,0:T(8,128)(2,1)S(1)} %pad_maximum_fusion.2.inner_b), channel_id=1, source_target_pairs={{8,0},{16,24},{9,1},{17,25},{10,2},{18,26},{11,3},{19,27},{12,4},{... | collective-permute-start | bytes 786440 | tf_op jit(solution)/shard_map/ppermute | solution.py:66
  42.3 1.3 %collective-permute-start.9 = (bf16[256,512]{1,0:T(8,128)(2,1)S(1)}, bf16[256,512]{1,0:T(8,128)(2,1)S(1)}, u32[]{:S(2)}, u32[]{:S(2)}) collective-permute-start(bf16[256,512]{1,0:T(8,128)(2,1)S(1)} %pad_maximum_fusion.1.inner_a), channel_id=1, source_target_pairs={{8,0},{16,24},{9,1},{17,25},{10,2},{18,26},{11,3},{19,27},{12,4},{... | collective-permute-start | bytes 786440 | tf_op jit(solution)/shard_map/ppermute | solution.py:66
  43.7 0.0 copy-start
  43.7 1.4 %collective-permute-start.8 = (bf16[256,512]{1,0:T(8,128)(2,1)S(1)}, bf16[256,512]{1,0:T(8,128)(2,1)S(1)}, u32[]{:S(2)}, u32[]{:S(2)}) collective-permute-start(bf16[256,512]{1,0:T(8,128)(2,1)S(1)} %pad_maximum_fusion.from_inner), channel_id=1, source_target_pairs={{8,0},{16,24},{9,1},{17,25},{10,2},{18,26},{11,3},{19,27},{12,4},{... | collective-permute-start | bytes 786440 | tf_op jit(solution)/shard_map/ppermute | solution.py:66
  45.1 0.0 collective-permute-done.5.d
  45.1 0.6 shard_map.28.left
  45.7 0.0 copy-done
  45.7 2.7 %shard_map.29.acc = f32[6,512,256]{2,1,0:T(8,128)S(1)} custom-call(bf16[4,2,512,512]{3,2,1,0:T(8,128)(2,1)S(1)} %shard_map.28.left, bf16[256,1536]{1,0:T(8,128)(2,1)S(1)} %copy-done, bf16[256,1536]{1,0:T(8,128)(2,1)S(1)} %collective-permute-done.3.near), custom_call_target="tpu_custom_call" | custom-call | flops 1610612736 | bytes 4194304 | tf_op jit(solution)/shard_map/pallas_call | solution.py:202
  48.4 0.0 collective-permute-done.6.from_outer
  48.4 1.9 %shard_map.30.acc = f32[6,512,256]{2,1,0:T(8,128)S(1)} custom-call(bf16[4,2,512,512]{3,2,1,0:T(8,128)(2,1)S(1)} %shard_map.28.left, f32[6,512,256]{2,1,0:T(8,128)S(1)} %shard_map.29.acc, bf16[256,1536]{1,0:T(8,128)(2,1)S(1)} %collective-permute-done.4.from_inner, bf16[256,1536]{1,0:T(8,128)(2,1)S(1)} %collective-permute-done.6.from_outer), custom_call_target="tpu_custom_call" | custom-call | flops 805306368 | bytes 4194304 | tf_op jit(solution)/shard_map/pallas_call | solution.py:203
  50.3 1.8 %collective-permute-done.10.outer_b = bf16[256,512]{1,0:T(8,128)(2,1)S(1)} collective-permute-done((bf16[256,512]{1,0:T(8,128)(2,1)S(1)}, bf16[256,512]{1,0:T(8,128)(2,1)S(1)}, u32[]{:S(2)}, u32[]{:S(2)}) %collective-permute-start.10) | collective-permute-done | bytes 262176 | tf_op jit(solution)/shard_map/ppermute | solution.py:66
  52.2 5.6 %collective-permute-done.9.outer_a = bf16[256,512]{1,0:T(8,128)(2,1)S(1)} collective-permute-done((bf16[256,512]{1,0:T(8,128)(2,1)S(1)}, bf16[256,512]{1,0:T(8,128)(2,1)S(1)}, u32[]{:S(2)}, u32[]{:S(2)}) %collective-permute-start.9) | collective-permute-done | bytes 262176 | tf_op jit(solution)/shard_map/ppermute | solution.py:66
  57.8 2.3 %shard_map.31._ = bf16[512,1536]{1,0:T(8,128)(2,1)} custom-call(bf16[4,2,512,512]{3,2,1,0:T(8,128)(2,1)S(1)} %shard_map.28.left, f32[6,512,256]{2,1,0:T(8,128)S(1)} %shard_map.30.acc, bf16[256,512]{1,0:T(8,128)(2,1)S(1)} %pad_maximum_fusion.1.inner_a, bf16[256,512]{1,0:T(8,128)(2,1)S(1)} %collective-permute-done.9.outer_a, ...), custom_call_target="tpu_custom_call" | custom-call | flops 536870912 | bytes 4194304 | tf_op jit(solution)/shard_map/pallas_call | solution.py:208
  60.0 1.7 %collective-permute-done.8.from_outer = bf16[256,512]{1,0:T(8,128)(2,1)S(1)} collective-permute-done((bf16[256,512]{1,0:T(8,128)(2,1)S(1)}, bf16[256,512]{1,0:T(8,128)(2,1)S(1)}, u32[]{:S(2)}, u32[]{:S(2)}) %collective-permute-start.8) | collective-permute-done | bytes 262176 | tf_op jit(solution)/shard_map/ppermute | solution.py:66
  61.8 1.5 %shard_map.32 = bf16[512,1536]{1,0:T(8,128)(2,1)} custom-call(bf16[4,2,512,512]{3,2,1,0:T(8,128)(2,1)S(1)} %shard_map.28.left, f32[6,512,256]{2,1,0:T(8,128)S(1)} %shard_map.30.acc, bf16[256,512]{1,0:T(8,128)(2,1)S(1)} %pad_maximum_fusion.from_inner, bf16[256,512]{1,0:T(8,128)(2,1)S(1)} %collective-permute-done.8.from_outer, ...), custom_call_target="tpu_custom_call", output_to_operand_aliasing={{}: (4, {})} | custom-call | flops 268435456 | bytes 1048576 | tf_op jit(solution)/shard_map/pallas_call | solution.py:211
  (4 shorter events, 0.1 us)
Async XLA Ops:
  0.0 9.4 %collective-permute-start = (bf16[2,512,128]{2,1,0:T(8,128)(2,1)}, bf16[2,512,128]{2,1,0:T(8,128)(2,1)S(1)}, u32[]{:S(2)}, u32[]{:S(2)}) collective-permute-start(bf16[2,512,128]{2,1,0:T(8,128)(2,1)} %param.2), channel_id=1, source_target_pairs={{0,1},{1,0},{2,3},{3,2},{4,5},{5,4},{6,7},{7,6},{8,9},{9,8},{10,11... | collective-permute-start | bytes 786440 | tf_op jit(solution)/shard_map/ppermute | solution.py:58
  0.5 12.1 %collective-permute-start.4 = (bf16[256,1536]{1,0:T(8,128)(2,1)}, bf16[256,1536]{1,0:T(8,128)(2,1)S(1)}, u32[]{:S(2)}, u32[]{:S(2)}) collective-permute-start(bf16[256,1536]{1,0:T(8,128)(2,1)} %own.1), channel_id=1, source_target_pairs={{8,16},{16,8},{9,17},{17,9},{10,18},{18,10},{11,19},{19,11},{12,20... | collective-permute-start | bytes 2359304 | tf_op jit(solution)/shard_map/ppermute | solution.py:66
  1.2 23.6 %collective-permute-start.3 = (bf16[256,1536]{1,0:T(8,128)(2,1)}, bf16[256,1536]{1,0:T(8,128)(2,1)S(1)}, u32[]{:S(2)}, u32[]{:S(2)}) collective-permute-start(bf16[256,1536]{1,0:T(8,128)(2,1)} %own.1), channel_id=1, source_target_pairs={{0,8},{8,0},{16,24},{24,16},{1,9},{9,1},{17,25},{25,17},{2,10},{10... | collective-permute-start | bytes 2359304 | tf_op jit(solution)/shard_map/ppermute | solution.py:66
  6.6 34.4 %collective-permute-start.7 = (bf16[256,1536]{1,0:T(8,128)(2,1)}, bf16[256,1536]{1,0:T(8,128)(2,1)S(1)}, u32[]{:S(2)}, u32[]{:S(2)}) collective-permute-start(bf16[256,1536]{1,0:T(8,128)(2,1)} %own.1), channel_id=1, source_target_pairs={{0,16},{24,8},{1,17},{25,9},{2,18},{26,10},{3,19},{27,11},{4,20},{... | collective-permute-start | bytes 2359304 | tf_op jit(solution)/shard_map/ppermute | solution.py:66
  9.5 13.8 %collective-permute-start.1 = (bf16[4,512,128]{2,1,0:T(8,128)(2,1)S(1)}, bf16[4,512,128]{2,1,0:T(8,128)(2,1)S(1)}, u32[]{:S(2)}, u32[]{:S(2)}) collective-permute-start(bf16[4,512,128]{2,1,0:T(8,128)(2,1)S(1)} %constant_dynamic-update-slice_fusion.own), channel_id=1, source_target_pairs={{0,2},{1,3},{2,0},{3,1},{4,6},{5,7},{6,4},{7,5},{8,10},{9,11},{10,... | collective-permute-start | bytes 1572872 | tf_op jit(solution)/shard_map/ppermute | solution.py:58
  11.0 13.5 %collective-permute-start.2 = (bf16[4,512,128]{2,1,0:T(8,128)(2,1)S(1)}, bf16[4,512,128]{2,1,0:T(8,128)(2,1)S(1)}, u32[]{:S(2)}, u32[]{:S(2)}) collective-permute-start(bf16[4,512,128]{2,1,0:T(8,128)(2,1)S(1)} %constant_dynamic-update-slice_fusion.own), channel_id=1, source_target_pairs={{0,4},{1,5},{2,6},{3,7},{4,0},{5,1},{6,2},{7,3},{8,12},{9,13},{10,... | collective-permute-start | bytes 1572872 | tf_op jit(solution)/shard_map/ppermute | solution.py:58
  12.5 35.9 %collective-permute-start.6 = (bf16[256,1536]{1,0:T(8,128)(2,1)S(1)}, bf16[256,1536]{1,0:T(8,128)(2,1)S(1)}, u32[]{:S(2)}, u32[]{:S(2)}) collective-permute-start(bf16[256,1536]{1,0:T(8,128)(2,1)S(1)} %collective-permute-done.4.from_inner), channel_id=1, source_target_pairs={{8,0},{16,24},{9,1},{17,25},{10,2},{18,26},{11,3},{19,27},{12,4},{... | collective-permute-start | bytes 2359304 | tf_op jit(solution)/shard_map/ppermute | solution.py:66
  24.8 20.3 %collective-permute-start.5 = (bf16[4,512,128]{2,1,0:T(8,128)(2,1)S(1)}, bf16[4,512,128]{2,1,0:T(8,128)(2,1)S(1)}, u32[]{:S(2)}, u32[]{:S(2)}) collective-permute-start(bf16[4,512,128]{2,1,0:T(8,128)(2,1)S(1)} %collective-permute-done.1.x), channel_id=1, source_target_pairs={{0,4},{1,5},{2,6},{3,7},{4,0},{5,1},{6,2},{7,3},{8,12},{9,13},{10,... | collective-permute-start | bytes 1572872 | tf_op jit(solution)/shard_map/ppermute | solution.py:58
  41.0 11.1 %collective-permute-start.10 = (bf16[256,512]{1,0:T(8,128)(2,1)S(1)}, bf16[256,512]{1,0:T(8,128)(2,1)S(1)}, u32[]{:S(2)}, u32[]{:S(2)}) collective-permute-start(bf16[256,512]{1,0:T(8,128)(2,1)S(1)} %pad_maximum_fusion.2.inner_b), channel_id=1, source_target_pairs={{8,0},{16,24},{9,1},{17,25},{10,2},{18,26},{11,3},{19,27},{12,4},{... | collective-permute-start | bytes 786440 | tf_op jit(solution)/shard_map/ppermute | solution.py:66
  42.3 15.4 %collective-permute-start.9 = (bf16[256,512]{1,0:T(8,128)(2,1)S(1)}, bf16[256,512]{1,0:T(8,128)(2,1)S(1)}, u32[]{:S(2)}, u32[]{:S(2)}) collective-permute-start(bf16[256,512]{1,0:T(8,128)(2,1)S(1)} %pad_maximum_fusion.1.inner_a), channel_id=1, source_target_pairs={{8,0},{16,24},{9,1},{17,25},{10,2},{18,26},{11,3},{19,27},{12,4},{... | collective-permute-start | bytes 786440 | tf_op jit(solution)/shard_map/ppermute | solution.py:66
  43.7 2.1 %copy-start = (bf16[256,1536]{1,0:T(8,128)(2,1)S(1)}, bf16[256,1536]{1,0:T(8,128)(2,1)}, u32[]{:S(2)}) copy-start(bf16[256,1536]{1,0:T(8,128)(2,1)} %own.1) | copy-start | bytes 2359300
  43.7 18.1 %collective-permute-start.8 = (bf16[256,512]{1,0:T(8,128)(2,1)S(1)}, bf16[256,512]{1,0:T(8,128)(2,1)S(1)}, u32[]{:S(2)}, u32[]{:S(2)}) collective-permute-start(bf16[256,512]{1,0:T(8,128)(2,1)S(1)} %pad_maximum_fusion.from_inner), channel_id=1, source_target_pairs={{8,0},{16,24},{9,1},{17,25},{10,2},{18,26},{11,3},{19,27},{12,4},{... | collective-permute-start | bytes 786440 | tf_op jit(solution)/shard_map/ppermute | solution.py:66

commit v2 on v1

--- a/solution.py
+++ b/solution.py
@@ -48,7 +48,7 @@
 
 
 SWAP_OUTER = [(0, 1), (1, 0), (2, 3), (3, 2)]
-SWAP_INNER = [(1, 2), (2, 1)]
+SWAP_INNER = [(8 * z + q, 8 * (3 - z) + q if z in (1, 2) else 8 * z + (q ^ 1)) for z in range(4) for q in range(8)]
 OUTWARD = [(1, 0), (2, 3)]
 ACROSS = [(0, 2), (3, 1)]
 CHUNKS = 3
@@ -184,7 +184,7 @@
 def line_on_device(shot_side, rcv_side):
     shots, cols = shot_side.shape[1], rcv_side.shape[1]
     width = cols // 2 // CHUNKS
-    m1, = over_shot([rcv_side], SWAP_INNER)
+    m1 = lax.ppermute(rcv_side, ("shot", "rcv"), SWAP_INNER)
     near, = over_shot([rcv_side], SWAP_OUTER)
     m2, = over_shot([rcv_side], ACROSS)
     s2, = over_shot([m1], OUTWARD)

time: 63.5 us -> 61.5 us (0.969)
  waiting for transfers between devices: 34.8 us -> 33.2 us
    ppermute x7 -> x6, waiting for transfers between devices: 24.1 us -> 23 us  [over_shot(): return [lax.ppermute(value, 'shot', pairs) for value in values]]
    ppermute x7 -> x6, starting transfers between devices: 13.3 us -> 12.8 us  [over_shot(): return [lax.ppermute(value, 'shot', pairs) for value in values]]
  transfers between devices with their start and end apart: 11 -> 11, of which waited for: 7 -> 6; matrix products, arithmetic and copies ran while one was open for 2% -> 2% of each run, Pallas kernels for 12% -> 12%
where the time goes in v2:
time: 61.5 us; the launch traced here: 61.3 us
  waiting for transfers between devices  33.2 us (54%)
  starting transfers between devices  18 us (29%)
  Pallas kernels  8.85 us (14%)
  local copies, waits for them, and re-layouts  1.06 us (2%)
    ppermute x6, waiting for transfers between devices, over_shot(): return [lax.ppermute(value, 'shot', pairs) for value in values]  23 us
    ppermute x6, starting transfers between devices, over_shot(): return [lax.ppermute(value, 'shot', pairs) for value in values]  12.8 us
    ppermute x4, waiting for transfers between devices, flipped(): return lax.ppermute(value, 'rcv', [(i, i ^ bit) for i in range(8)])  10.2 us
    ppermute x4, starting transfers between devices, flipped(): return lax.ppermute(value, 'rcv', [(i, i ^ bit) for i in range(8)])  5.05 us
    pallas_call x1, Pallas kernels, line_on_device(): kernel_call(near_kernel, acc_shape, 2 * block_flops, 3)  2.69 us
    pallas_call x1, Pallas kernels, line_on_device(): kernel_call(first_kernel, out_shape, block_flops * 2 // 3, 6, out_specs=i...  2.25 us
    pallas_call x1, Pallas kernels, line_on_device(): acc = kernel_call(far_kernel, acc_shape, block_flops, 4)(left, acc, m1, s2)  1.87 us
    pallas_call x1, Pallas kernels, line_on_device(): pl.pallas_call(last_kernel, out_shape=out_shape, in_specs=[pl.BlockSpec(m...  1.46 us
  transfers between devices with their start and end apart: 11, of which 6 were waited for; matrix products, arithmetic and copies ran while one was open for 2% of the time, Pallas kernels for 12%

profile of v2, /device:TPU:0, one launch (start us, length us, event | category | flops | bytes accessed | tf_op | source)
XLA Modules:
  0.0 61.3 jit_solution(9116398201518186844)
XLA Ops:
  0.0 0.5 collective-permute-start
  0.5 0.1 collective-permute-start.4
  0.5 4.1 %collective-permute-start.3 = (bf16[256,1536]{1,0:T(8,128)(2,1)}, bf16[256,1536]{1,0:T(8,128)(2,1)S(1)}, u32[]{:S(2)}, u32[]{:S(2)}) collective-permute-start(bf16[256,1536]{1,0:T(8,128)(2,1)} %own.1), channel_id=1, source_target_pairs={{0,8},{8,0},{16,24},{24,16},{1,9},{9,1},{17,25},{25,17},{2,10},{10... | collective-permute-start | bytes 2359304 | tf_op jit(solution)/shard_map/ppermute | solution.py:66
  4.6 3.5 %collective-permute-start.7 = (bf16[256,1536]{1,0:T(8,128)(2,1)}, bf16[256,1536]{1,0:T(8,128)(2,1)S(1)}, u32[]{:S(2)}, u32[]{:S(2)}) collective-permute-start(bf16[256,1536]{1,0:T(8,128)(2,1)} %own.1), channel_id=1, source_target_pairs={{0,16},{24,8},{1,17},{25,9},{2,18},{26,10},{3,19},{27,11},{4,20},{... | collective-permute-start | bytes 2359304 | tf_op jit(solution)/shard_map/ppermute | solution.py:66
  8.1 1.0 %constant_dynamic-update-slice_fusion.1 = bf16[4,512,128]{2,1,0:T(8,128)(2,1)S(1)} fusion(bf16[2,512,128]{2,1,0:T(8,128)(2,1)} %param.2), kind=kLoop, calls=%fused_computation.4 | loop fusion | bytes 524288
  9.0 0.0 collective-permute-done
  9.1 1.6 %collective-permute-start.1 = (bf16[4,512,128]{2,1,0:T(8,128)(2,1)S(1)}, bf16[4,512,128]{2,1,0:T(8,128)(2,1)S(1)}, u32[]{:S(2)}, u32[]{:S(2)}) collective-permute-start(bf16[4,512,128]{2,1,0:T(8,128)(2,1)S(1)} %constant_dynamic-update-slice_fusion.own), channel_id=1, source_target_pairs={{0,2},{1,3},{2,0},{3,1},{4,6},{5,7},{6,4},{7,5},{8,10},{9,11},{10,... | collective-permute-start | bytes 1572872 | tf_op jit(solution)/shard_map/ppermute | solution.py:58
  10.7 1.5 %collective-permute-start.2 = (bf16[4,512,128]{2,1,0:T(8,128)(2,1)S(1)}, bf16[4,512,128]{2,1,0:T(8,128)(2,1)S(1)}, u32[]{:S(2)}, u32[]{:S(2)}) collective-permute-start(bf16[4,512,128]{2,1,0:T(8,128)(2,1)S(1)} %constant_dynamic-update-slice_fusion.own), channel_id=1, source_target_pairs={{0,4},{1,5},{2,6},{3,7},{4,0},{5,1},{6,2},{7,3},{8,12},{9,13},{10,... | collective-permute-start | bytes 1572872 | tf_op jit(solution)/shard_map/ppermute | solution.py:58
  12.2 0.0 collective-permute-done.4.from_inner
  12.2 1.3 %collective-permute-start.6 = (bf16[256,1536]{1,0:T(8,128)(2,1)S(1)}, bf16[256,1536]{1,0:T(8,128)(2,1)S(1)}, u32[]{:S(2)}, u32[]{:S(2)}) collective-permute-start(bf16[256,1536]{1,0:T(8,128)(2,1)S(1)} %collective-permute-done.4.from_inner), channel_id=1, source_target_pairs={{8,0},{16,24},{9,1},{17,25},{10,2},{18,26},{11,3},{19,27},{12,4},{... | collective-permute-start | bytes 2359304 | tf_op jit(solution)/shard_map/ppermute | solution.py:66
  13.5 9.0 %collective-permute-done.1.x = bf16[4,512,128]{2,1,0:T(8,128)(2,1)S(1)} collective-permute-done((bf16[4,512,128]{2,1,0:T(8,128)(2,1)S(1)}, bf16[4,512,128]{2,1,0:T(8,128)(2,1)S(1)}, u32[]{:S(2)}, u32[]{:S(2)}) %collective-permute-start.1) | collective-permute-done | bytes 524320 | tf_op jit(solution)/shard_map/ppermute | solution.py:58
  22.4 1.2 %collective-permute-done.2.y = bf16[4,512,128]{2,1,0:T(8,128)(2,1)S(1)} collective-permute-done((bf16[4,512,128]{2,1,0:T(8,128)(2,1)S(1)}, bf16[4,512,128]{2,1,0:T(8,128)(2,1)S(1)}, u32[]{:S(2)}, u32[]{:S(2)}) %collective-permute-start.2) | collective-permute-done | bytes 524320 | tf_op jit(solution)/shard_map/ppermute | solution.py:58
  23.7 0.0 collective-permute-done.3.near
  23.7 1.5 %collective-permute-start.5 = (bf16[4,512,128]{2,1,0:T(8,128)(2,1)S(1)}, bf16[4,512,128]{2,1,0:T(8,128)(2,1)S(1)}, u32[]{:S(2)}, u32[]{:S(2)}) collective-permute-start(bf16[4,512,128]{2,1,0:T(8,128)(2,1)S(1)} %collective-permute-done.1.x), channel_id=1, source_target_pairs={{0,4},{1,5},{2,6},{3,7},{4,0},{5,1},{6,2},{7,3},{8,12},{9,13},{10,... | collective-permute-start | bytes 1572872 | tf_op jit(solution)/shard_map/ppermute | solution.py:58
  25.2 13.8 %collective-permute-done.7 = bf16[256,1536]{1,0:T(8,128)(2,1)S(1)} collective-permute-done((bf16[256,1536]{1,0:T(8,128)(2,1)}, bf16[256,1536]{1,0:T(8,128)(2,1)S(1)}, u32[]{:S(2)}, u32[]{:S(2)}) %collective-permute-start.7) | collective-permute-done | bytes 786464 | tf_op jit(solution)/shard_map/ppermute | solution.py:66
  39.0 0.1 fusion
  39.0 1.3 %collective-permute-start.10 = (bf16[256,512]{1,0:T(8,128)(2,1)S(1)}, bf16[256,512]{1,0:T(8,128)(2,1)S(1)}, u32[]{:S(2)}, u32[]{:S(2)}) collective-permute-start(bf16[256,512]{1,0:T(8,128)(2,1)S(1)} %pad_maximum_fusion.2.inner_b), channel_id=1, source_target_pairs={{8,0},{16,24},{9,1},{17,25},{10,2},{18,26},{11,3},{19,27},{12,4},{... | collective-permute-start | bytes 786440 | tf_op jit(solution)/shard_map/ppermute | solution.py:66
  40.4 1.3 %collective-permute-start.9 = (bf16[256,512]{1,0:T(8,128)(2,1)S(1)}, bf16[256,512]{1,0:T(8,128)(2,1)S(1)}, u32[]{:S(2)}, u32[]{:S(2)}) collective-permute-start(bf16[256,512]{1,0:T(8,128)(2,1)S(1)} %pad_maximum_fusion.1.inner_a), channel_id=1, source_target_pairs={{8,0},{16,24},{9,1},{17,25},{10,2},{18,26},{11,3},{19,27},{12,4},{... | collective-permute-start | bytes 786440 | tf_op jit(solution)/shard_map/ppermute | solution.py:66
  41.7 0.0 copy-start
  41.7 1.4 %collective-permute-start.8 = (bf16[256,512]{1,0:T(8,128)(2,1)S(1)}, bf16[256,512]{1,0:T(8,128)(2,1)S(1)}, u32[]{:S(2)}, u32[]{:S(2)}) collective-permute-start(bf16[256,512]{1,0:T(8,128)(2,1)S(1)} %pad_maximum_fusion.from_inner), channel_id=1, source_target_pairs={{8,0},{16,24},{9,1},{17,25},{10,2},{18,26},{11,3},{19,27},{12,4},{... | collective-permute-start | bytes 786440 | tf_op jit(solution)/shard_map/ppermute | solution.py:66
  43.1 0.0 collective-permute-done.5.d
  43.2 0.6 shard_map.28.left
  43.8 0.0 copy-done
  43.8 2.7 %shard_map.29.acc = f32[6,512,256]{2,1,0:T(8,128)S(1)} custom-call(bf16[4,2,512,512]{3,2,1,0:T(8,128)(2,1)S(1)} %shard_map.28.left, bf16[256,1536]{1,0:T(8,128)(2,1)S(1)} %copy-done, bf16[256,1536]{1,0:T(8,128)(2,1)S(1)} %collective-permute-done.3.near), custom_call_target="tpu_custom_call" | custom-call | flops 1610612736 | bytes 4194304 | tf_op jit(solution)/shard_map/pallas_call | solution.py:202
  46.5 0.0 collective-permute-done.6.from_outer
  46.5 1.9 %shard_map.30.acc = f32[6,512,256]{2,1,0:T(8,128)S(1)} custom-call(bf16[4,2,512,512]{3,2,1,0:T(8,128)(2,1)S(1)} %shard_map.28.left, f32[6,512,256]{2,1,0:T(8,128)S(1)} %shard_map.29.acc, bf16[256,1536]{1,0:T(8,128)(2,1)S(1)} %collective-permute-done.4.from_inner, bf16[256,1536]{1,0:T(8,128)(2,1)S(1)} %collective-permute-done.6.from_outer), custom_call_target="tpu_custom_call" | custom-call | flops 805306368 | bytes 4194304 | tf_op jit(solution)/shard_map/pallas_call | solution.py:203
  48.3 1.8 %collective-permute-done.10.outer_b = bf16[256,512]{1,0:T(8,128)(2,1)S(1)} collective-permute-done((bf16[256,512]{1,0:T(8,128)(2,1)S(1)}, bf16[256,512]{1,0:T(8,128)(2,1)S(1)}, u32[]{:S(2)}, u32[]{:S(2)}) %collective-permute-start.10) | collective-permute-done | bytes 262176 | tf_op jit(solution)/shard_map/ppermute | solution.py:66
  50.2 5.6 %collective-permute-done.9.outer_a = bf16[256,512]{1,0:T(8,128)(2,1)S(1)} collective-permute-done((bf16[256,512]{1,0:T(8,128)(2,1)S(1)}, bf16[256,512]{1,0:T(8,128)(2,1)S(1)}, u32[]{:S(2)}, u32[]{:S(2)}) %collective-permute-start.9) | collective-permute-done | bytes 262176 | tf_op jit(solution)/shard_map/ppermute | solution.py:66
  55.8 2.2 %shard_map.31._ = bf16[512,1536]{1,0:T(8,128)(2,1)} custom-call(bf16[4,2,512,512]{3,2,1,0:T(8,128)(2,1)S(1)} %shard_map.28.left, f32[6,512,256]{2,1,0:T(8,128)S(1)} %shard_map.30.acc, bf16[256,512]{1,0:T(8,128)(2,1)S(1)} %pad_maximum_fusion.1.inner_a, bf16[256,512]{1,0:T(8,128)(2,1)S(1)} %collective-permute-done.9.outer_a, ...), custom_call_target="tpu_custom_call" | custom-call | flops 536870912 | bytes 4194304 | tf_op jit(solution)/shard_map/pallas_call | solution.py:208
  58.1 1.7 %collective-permute-done.8.from_outer = bf16[256,512]{1,0:T(8,128)(2,1)S(1)} collective-permute-done((bf16[256,512]{1,0:T(8,128)(2,1)S(1)}, bf16[256,512]{1,0:T(8,128)(2,1)S(1)}, u32[]{:S(2)}, u32[]{:S(2)}) %collective-permute-start.8) | collective-permute-done | bytes 262176 | tf_op jit(solution)/shard_map/ppermute | solution.py:66
  59.8 1.5 %shard_map.32 = bf16[512,1536]{1,0:T(8,128)(2,1)} custom-call(bf16[4,2,512,512]{3,2,1,0:T(8,128)(2,1)S(1)} %shard_map.28.left, f32[6,512,256]{2,1,0:T(8,128)S(1)} %shard_map.30.acc, bf16[256,512]{1,0:T(8,128)(2,1)S(1)} %pad_maximum_fusion.from_inner, bf16[256,512]{1,0:T(8,128)(2,1)S(1)} %collective-permute-done.8.from_outer, ...), custom_call_target="tpu_custom_call", output_to_operand_aliasing={{}: (4, {})} | custom-call | flops 268435456 | bytes 1048576 | tf_op jit(solution)/shard_map/pallas_call | solution.py:211
  (4 shorter events, 0.1 us)
Async XLA Ops:
  0.0 9.1 %collective-permute-start = (bf16[2,512,128]{2,1,0:T(8,128)(2,1)}, bf16[2,512,128]{2,1,0:T(8,128)(2,1)S(1)}, u32[]{:S(2)}, u32[]{:S(2)}) collective-permute-start(bf16[2,512,128]{2,1,0:T(8,128)(2,1)} %param.2), channel_id=1, source_target_pairs={{0,1},{1,0},{2,3},{3,2},{4,5},{5,4},{6,7},{7,6},{8,9},{9,8},{10,11... | collective-permute-start | bytes 786440 | tf_op jit(solution)/shard_map/ppermute | solution.py:58
  0.5 11.7 %collective-permute-start.4 = (bf16[256,1536]{1,0:T(8,128)(2,1)}, bf16[256,1536]{1,0:T(8,128)(2,1)S(1)}, u32[]{:S(2)}, u32[]{:S(2)}) collective-permute-start(bf16[256,1536]{1,0:T(8,128)(2,1)} %own.1), channel_id=1, source_target_pairs={{0,1},{1,0},{2,3},{3,2},{4,5},{5,4},{6,7},{7,6},{8,16},{9,17},{10,... | collective-permute-start | bytes 2359304 | tf_op jit(solution)/shard_map/ppermute | solution.py:187
  0.5 23.1 %collective-permute-start.3 = (bf16[256,1536]{1,0:T(8,128)(2,1)}, bf16[256,1536]{1,0:T(8,128)(2,1)S(1)}, u32[]{:S(2)}, u32[]{:S(2)}) collective-permute-start(bf16[256,1536]{1,0:T(8,128)(2,1)} %own.1), channel_id=1, source_target_pairs={{0,8},{8,0},{16,24},{24,16},{1,9},{9,1},{17,25},{25,17},{2,10},{10... | collective-permute-start | bytes 2359304 | tf_op jit(solution)/shard_map/ppermute | solution.py:66
  4.6 34.4 %collective-permute-start.7 = (bf16[256,1536]{1,0:T(8,128)(2,1)}, bf16[256,1536]{1,0:T(8,128)(2,1)S(1)}, u32[]{:S(2)}, u32[]{:S(2)}) collective-permute-start(bf16[256,1536]{1,0:T(8,128)(2,1)} %own.1), channel_id=1, source_target_pairs={{0,16},{24,8},{1,17},{25,9},{2,18},{26,10},{3,19},{27,11},{4,20},{... | collective-permute-start | bytes 2359304 | tf_op jit(solution)/shard_map/ppermute | solution.py:66
  9.1 13.3 %collective-permute-start.1 = (bf16[4,512,128]{2,1,0:T(8,128)(2,1)S(1)}, bf16[4,512,128]{2,1,0:T(8,128)(2,1)S(1)}, u32[]{:S(2)}, u32[]{:S(2)}) collective-permute-start(bf16[4,512,128]{2,1,0:T(8,128)(2,1)S(1)} %constant_dynamic-update-slice_fusion.own), channel_id=1, source_target_pairs={{0,2},{1,3},{2,0},{3,1},{4,6},{5,7},{6,4},{7,5},{8,10},{9,11},{10,... | collective-permute-start | bytes 1572872 | tf_op jit(solution)/shard_map/ppermute | solution.py:58
  10.7 13.0 %collective-permute-start.2 = (bf16[4,512,128]{2,1,0:T(8,128)(2,1)S(1)}, bf16[4,512,128]{2,1,0:T(8,128)(2,1)S(1)}, u32[]{:S(2)}, u32[]{:S(2)}) collective-permute-start(bf16[4,512,128]{2,1,0:T(8,128)(2,1)S(1)} %constant_dynamic-update-slice_fusion.own), channel_id=1, source_target_pairs={{0,4},{1,5},{2,6},{3,7},{4,0},{5,1},{6,2},{7,3},{8,12},{9,13},{10,... | collective-permute-start | bytes 1572872 | tf_op jit(solution)/shard_map/ppermute | solution.py:58
  12.2 34.3 %collective-permute-start.6 = (bf16[256,1536]{1,0:T(8,128)(2,1)S(1)}, bf16[256,1536]{1,0:T(8,128)(2,1)S(1)}, u32[]{:S(2)}, u32[]{:S(2)}) collective-permute-start(bf16[256,1536]{1,0:T(8,128)(2,1)S(1)} %collective-permute-done.4.from_inner), channel_id=1, source_target_pairs={{8,0},{16,24},{9,1},{17,25},{10,2},{18,26},{11,3},{19,27},{12,4},{... | collective-permute-start | bytes 2359304 | tf_op jit(solution)/shard_map/ppermute | solution.py:66
  23.7 19.5 %collective-permute-start.5 = (bf16[4,512,128]{2,1,0:T(8,128)(2,1)S(1)}, bf16[4,512,128]{2,1,0:T(8,128)(2,1)S(1)}, u32[]{:S(2)}, u32[]{:S(2)}) collective-permute-start(bf16[4,512,128]{2,1,0:T(8,128)(2,1)S(1)} %collective-permute-done.1.x), channel_id=1, source_target_pairs={{0,4},{1,5},{2,6},{3,7},{4,0},{5,1},{6,2},{7,3},{8,12},{9,13},{10,... | collective-permute-start | bytes 1572872 | tf_op jit(solution)/shard_map/ppermute | solution.py:58
  39.0 11.1 %collective-permute-start.10 = (bf16[256,512]{1,0:T(8,128)(2,1)S(1)}, bf16[256,512]{1,0:T(8,128)(2,1)S(1)}, u32[]{:S(2)}, u32[]{:S(2)}) collective-permute-start(bf16[256,512]{1,0:T(8,128)(2,1)S(1)} %pad_maximum_fusion.2.inner_b), channel_id=1, source_target_pairs={{8,0},{16,24},{9,1},{17,25},{10,2},{18,26},{11,3},{19,27},{12,4},{... | collective-permute-start | bytes 786440 | tf_op jit(solution)/shard_map/ppermute | solution.py:66
  40.4 15.4 %collective-permute-start.9 = (bf16[256,512]{1,0:T(8,128)(2,1)S(1)}, bf16[256,512]{1,0:T(8,128)(2,1)S(1)}, u32[]{:S(2)}, u32[]{:S(2)}) collective-permute-start(bf16[256,512]{1,0:T(8,128)(2,1)S(1)} %pad_maximum_fusion.1.inner_a), channel_id=1, source_target_pairs={{8,0},{16,24},{9,1},{17,25},{10,2},{18,26},{11,3},{19,27},{12,4},{... | collective-permute-start | bytes 786440 | tf_op jit(solution)/shard_map/ppermute | solution.py:66
  41.7 2.1 %copy-start = (bf16[256,1536]{1,0:T(8,128)(2,1)S(1)}, bf16[256,1536]{1,0:T(8,128)(2,1)}, u32[]{:S(2)}) copy-start(bf16[256,1536]{1,0:T(8,128)(2,1)} %own.1) | copy-start | bytes 2359300
  41.7 18.1 %collective-permute-start.8 = (bf16[256,512]{1,0:T(8,128)(2,1)S(1)}, bf16[256,512]{1,0:T(8,128)(2,1)S(1)}, u32[]{:S(2)}, u32[]{:S(2)}) collective-permute-start(bf16[256,512]{1,0:T(8,128)(2,1)S(1)} %pad_maximum_fusion.from_inner), channel_id=1, source_target_pairs={{8,0},{16,24},{9,1},{17,25},{10,2},{18,26},{11,3},{19,27},{12,4},{... | collective-permute-start | bytes 786440 | tf_op jit(solution)/shard_map/ppermute | solution.py:66

commit v3 on v2

v3 whole, which is shorter than its diff:
```python
import jax
import jax.numpy as jnp
from jax import lax
from jax.experimental import pallas as pl
from jax.experimental.pallas import tpu as pltpu
from jax.sharding import PartitionSpec as P

STEPS = 4
VMEM_LIMIT = 16 * 1024 * 1024


def passed_along(value, axis, steps):
    count = lax.axis_size(axis)
    pairs = [(source, (source + steps) % count) for source in range(count)]
    return lax.ppermute(value, axis, pairs)


def from_root(value, axis, root):
    mine = lax.axis_index(axis) == root
    return lax.psum(jnp.where(mine, value, jnp.zeros_like(value)), axis)


def complex_product(left, right):
    half = right.shape[1] // 2
    first = jnp.dot(left[0], right, preferred_element_type=jnp.float32)
    second = jnp.dot(left[1], right, preferred_element_type=jnp.float32)
    real_part = first[:, :half] - second[:, half:]
    imag_part = first[:, half:] + second[:, :half]
    return jnp.concatenate([real_part, imag_part], axis=1)


def ring_on_device(shot_side, rcv_side):
    cycle_size = lax.axis_size("shot")
    pieces = lax.axis_size("rcv") // cycle_size
    shot_index = lax.axis_index("shot")
    total = jnp.zeros((shot_side.shape[1], rcv_side.shape[1]), jnp.float32)
    current = rcv_side
    for step in range(STEPS):
        if step > 0:
            current = passed_along(current, "shot", 1)
        block_id = (shot_index - step) % cycle_size
        gotten = [
            from_root(shot_side, "rcv", block_id * pieces + piece_id)
            for piece_id in range(pieces)
        ]
        total = total + complex_product(jnp.concatenate(gotten, axis=2), current)
    return total.astype(jnp.bfloat16)


SWAP_OUTER = [(0, 1), (1, 0), (2, 3), (3, 2)]
SWAP_INNER = [(8 * z + q, 8 * (3 - z) + q if z in (1, 2) else 8 * z + (q ^ 1)) for z in range(4) for q in range(8)]
OUTWARD = [(1, 0), (2, 3)]
ACROSS = [(0, 2), (3, 1)]
CHUNKS = 3


def after(value, *others):
    return lax.optimization_barrier((value, *others))[0]


def flipped(value, bit):
    return lax.ppermute(value, "rcv", [(i, i ^ bit) for i in range(8)])


def over_shot(value, pairs):
    return lax.ppermute(value, "shot", pairs)


def kernel_call(kernel, out_shape, flops, count, **options):
    return pl.pallas_call(
        kernel,
        out_shape=out_shape,
        in_specs=[pl.BlockSpec(memory_space=pltpu.VMEM)] * count,
        out_specs=options.pop("out_specs", pl.BlockSpec(memory_space=pltpu.VMEM)),
        compiler_params=pltpu.CompilerParams(vmem_limit_bytes=VMEM_LIMIT),
        cost_estimate=pl.CostEstimate(flops=flops, bytes_accessed=4 << 20, transcendentals=0),
        **options,
    )


def stack_kernel(own, x, y, d, out):
    rcv = lax.axis_index("rcv")
    core0 = rcv % 2 == 0
    here = rcv // 2

    for rel, source in enumerate((own, x, y, d)):
        blk = here ^ rel

        def body(part, carry):
            m, o = source[part], source[2 + part]
            low = jnp.where(core0, m, o)
            high = jnp.where(core0, o, m)
            both = jnp.concatenate([low, high], axis=1)
            out[blk, part, :, 0:256] = both
            out[blk, 1 - part, :, 256:512] = jnp.where(part == 0, both, -both)
            return carry

        lax.fori_loop(0, 2, body, 0)


def tall(right, at, width):
    half = right.shape[1] // 2
    return jnp.concatenate([right[:, at:at + width], right[:, half + at:half + at + width]], axis=0)


def far_block(which, z):
    low = z < 2
    return jnp.where(low, 2, 1) if which == 0 else jnp.where(low, 3, 0)


def is_inner(z):
    return (z == 1) | (z == 2)


def most_kernel(left, own, near, from_inner, from_outer, out):
    z = lax.axis_index("shot")
    inner = is_inner(z)
    blk = far_block(0, z)
    width = own.shape[1] // 2 // CHUNKS
    for i in range(CHUNKS):
        at = i * width
        far = jnp.where(inner, tall(from_inner, at, width), tall(from_outer, at, width))
        right = jnp.concatenate([tall(own, at, width), tall(near, at, width), far], axis=0)

        def body(part, carry):
            rows = jnp.concatenate([left[z, part], left[z ^ 1, part], left[blk, part]], axis=1)
            out[CHUNKS * part + i] = jnp.dot(rows, right, preferred_element_type=jnp.float32)
            return carry

        lax.fori_loop(0, 2, body, 0)


def finish(first, pairs, left, acc, out, buf, sem):
    z = lax.axis_index("shot")
    inner = is_inner(z)
    blk = far_block(1, z)
    rows, width = acc.shape[1] // 2, acc.shape[2]
    copies = []
    for i, (from_inner, from_outer) in enumerate(pairs):
        right = jnp.where(inner, tall(from_inner, 0, width), tall(from_outer, 0, width))
        for part in range(2):
            slab = CHUNKS * part + first + i
            for r in range(2):
                these = pl.ds(r * rows, rows)
                total = acc[slab, these] + jnp.dot(left[blk, part, these], right, preferred_element_type=jnp.float32)
                buf[slab, these] = total.astype(buf.dtype)
                copy = pltpu.make_async_copy(
                    buf.at[slab, these], out.at[these, pl.ds(slab * width, width)], sem.at[2 * slab + r]
                )
                copy.start()
                copies.append(copy)
    for copy in copies:
        copy.wait()


def first_kernel(left, acc, inner_a, outer_a, inner_b, outer_b, out, buf, sem):
    finish(0, [(inner_a, outer_a), (inner_b, outer_b)], left, acc, out, buf, sem)


def last_kernel(left, acc, from_inner, from_outer, _, out, buf, sem):
    finish(CHUNKS - 1, [(from_inner, from_outer)], left, acc, out, buf, sem)


def cut(value, parts, total=CHUNKS):
    half = value.shape[1] // 2
    width = half // total
    out, at = [], 0
    for count in parts:
        low, high = at * width, (at + count) * width
        out.append(value if count == total else jnp.concatenate([value[:, low:high], value[:, half + low:half + high]], axis=1))
        at += count
    return out


def line_on_device(shot_side, rcv_side):
    shots, cols = shot_side.shape[1], rcv_side.shape[1]
    width = cols // 2 // CHUNKS

    near = over_shot(rcv_side, SWAP_OUTER)
    mid = lax.ppermute(rcv_side, ("shot", "rcv"), SWAP_INNER)

    core = flipped(shot_side, 1)
    chip = jnp.concatenate([shot_side, core])
    x, y = flipped(chip, 2), flipped(chip, 4)
    diag = flipped(after(x, y, near, mid), 4)

    outer_mid = over_shot(mid, OUTWARD)
    across_a, across_b = cut(rcv_side, (2, 1))
    across_a = over_shot(after(across_a, core), ACROSS)
    across_b = over_shot(across_b, ACROSS)
    inner = cut(across_a, (1, 1), 2) + [across_b]
    outer_a = over_shot(inner[0], OUTWARD)
    outer_b = over_shot(after(inner[1], near, diag), OUTWARD)
    outer_c = over_shot(after(inner[2], near, outer_a), OUTWARD)

    left = kernel_call(stack_kernel, jax.ShapeDtypeStruct((4, 2, shots, 512), jnp.bfloat16), 1, 4)(chip, x, y, diag)
    block_flops = 8 * shots * 256 * (cols // 2)
    acc_shape = jax.ShapeDtypeStruct((2 * CHUNKS, shots, width), jnp.float32)
    acc = kernel_call(most_kernel, acc_shape, 3 * block_flops, 5)(left, rcv_side, near, mid, outer_mid)

    out_shape = jax.ShapeDtypeStruct((shots, cols), jnp.bfloat16)
    scratch = [pltpu.VMEM((2 * CHUNKS, shots, width), jnp.bfloat16), pltpu.SemaphoreType.DMA((4 * CHUNKS,))]
    in_place = pl.BlockSpec(memory_space=pl.ANY)
    out = kernel_call(
        first_kernel, out_shape, block_flops * 2 // 3, 6, out_specs=in_place, scratch_shapes=scratch
    )(left, acc, inner[0], outer_a, inner[1], outer_b)
    return pl.pallas_call(
        last_kernel,
        out_shape=out_shape,
        in_specs=[pl.BlockSpec(memory_space=pltpu.VMEM)] * 4 + [in_place],
        out_specs=in_place,
        scratch_shapes=scratch,
        input_output_aliases={4: 0},
        compiler_params=pltpu.CompilerParams(vmem_limit_bytes=VMEM_LIMIT),
        cost_estimate=pl.CostEstimate(flops=block_flops // 3, bytes_accessed=1 << 20, transcendentals=0),
    )(left, acc, inner[2], outer_c, out)


def solution(mesh):
    line = mesh.shape["shot"] == 4 and mesh.shape["rcv"] == 8 and STEPS == 4
    return jax.shard_map(
        line_on_device if line else ring_on_device,
        mesh=mesh,
        in_specs=(P(None, "shot", "rcv"), P("shot", "rcv")),
        out_specs=P("shot", "rcv"),
        check_vma=False,
    )
```

time: 61.5 us -> 58.8 us (0.956)
  waiting for transfers between devices: 33.2 us -> 25.5 us
  starting transfers between devices: 18 us -> 23.6 us
  Pallas kernels: 8.85 us -> 7 us
  local copies, waits for them, and re-layouts: 1.06 us -> 2.13 us
    ppermute x7 -> x8, waiting for transfers between devices: 23 us -> 14.8 us  [the longest x7 14.8 us: over_shot(): return lax.ppermute(value, 'shot', pairs)]
    ppermute x7 -> x8, starting transfers between devices: 12.9 us -> 19 us  [the longest x7 18.5 us: over_shot(): return lax.ppermute(value, 'shot', pairs)]
    slice x1 -> x3, local copies, waits for them, and re-layouts: 0.05 us -> 1.12 us  [cut(): value[:, low:high]]
    pallas_call x2 -> x1, Pallas kernels: 4.55 us -> 3.61 us  [line_on_device(): kernel_call(most_kernel, acc_shape, 3 * block_flops, 5)]
    pallas_call x1, Pallas kernels: 2.25 us -> 1.54 us  [line_on_device(): kernel_call(first_kernel, out_shape, block_flops * 2 // 3, 6, out_specs=i...]
  transfers between devices with their start and end apart: 11 -> 12, of which waited for: 6 -> 6; matrix products, arithmetic and copies ran while one was open for 2% -> 4% of each run, Pallas kernels for 12% -> 10%
where the time goes in v3:
time: 58.8 us; the launch traced here: 58.6 us
  waiting for transfers between devices  25.5 us (43%)
  starting transfers between devices  23.6 us (40%)
  Pallas kernels  7 us (12%)
  local copies, waits for them, and re-layouts  2.13 us (4%)
    ppermute x7, starting transfers between devices, over_shot(): return lax.ppermute(value, 'shot', pairs)  18.5 us
    ppermute x7, waiting for transfers between devices, over_shot(): return lax.ppermute(value, 'shot', pairs)  14.8 us
    ppermute x4, waiting for transfers between devices, flipped(): return lax.ppermute(value, 'rcv', [(i, i ^ bit) for i in range(8)])  10.7 us
    ppermute x4, starting transfers between devices, flipped(): return lax.ppermute(value, 'rcv', [(i, i ^ bit) for i in range(8)])  4.66 us
    pallas_call x1, Pallas kernels, line_on_device(): kernel_call(most_kernel, acc_shape, 3 * block_flops, 5)  3.61 us
    pallas_call x1, Pallas kernels, line_on_device(): kernel_call(first_kernel, out_shape, block_flops * 2 // 3, 6, out_specs=i...  1.54 us
    pallas_call x1, Pallas kernels, line_on_device(): pl.pallas_call(last_kernel, out_shape=out_shape, in_specs=[pl.BlockSpec(m...  1.26 us
  transfers between devices with their start and end apart: 12, of which 6 were waited for; matrix products, arithmetic and copies ran while one was open for 4% of the time, Pallas kernels for 10%

profile of v3, /device:TPU:0, one launch (start us, length us, event | category | flops | bytes accessed | tf_op | source)
XLA Modules:
  0.0 58.6 jit_solution(10783970918431097012)
XLA Ops:
  0.0 0.5 collective-permute-start.4
  0.5 4.1 %collective-permute-start.3 = (bf16[256,1536]{1,0:T(8,128)(2,1)}, bf16[256,1536]{1,0:T(8,128)(2,1)S(1)}, u32[]{:S(2)}, u32[]{:S(2)}) collective-permute-start(bf16[256,1536]{1,0:T(8,128)(2,1)} %own.1), channel_id=1, source_target_pairs={{0,8},{8,0},{16,24},{24,16},{1,9},{9,1},{17,25},{25,17},{2,10},{10... | collective-permute-start | bytes 2359304 | tf_op jit(solution)/shard_map/ppermute | solution.py:66
  4.6 0.0 collective-permute-start
  4.6 1.1 %fusion = (bf16[256,512]{1,0:T(8,128)(2,1)S(1)}, bf16[256,512]{1,0:T(8,128)(2,1)S(1)}) fusion(bf16[256,1536]{1,0:T(8,128)(2,1)} %own.1), kind=kLoop, calls=%fused_computation.6 | loop fusion | bytes 1048576 | tf_op jit(solution)/shard_map/slice | solution.py:170
  5.7 1.0 %constant_dynamic-update-slice_fusion.1 = bf16[4,512,128]{2,1,0:T(8,128)(2,1)S(1)} fusion(bf16[2,512,128]{2,1,0:T(8,128)(2,1)} %param.2), kind=kLoop, calls=%fused_computation.5 | loop fusion | bytes 524288
  6.6 0.0 collective-permute-done
  6.7 1.6 %collective-permute-start.1 = (bf16[4,512,128]{2,1,0:T(8,128)(2,1)S(1)}, bf16[4,512,128]{2,1,0:T(8,128)(2,1)S(1)}, u32[]{:S(2)}, u32[]{:S(2)}) collective-permute-start(bf16[4,512,128]{2,1,0:T(8,128)(2,1)S(1)} %constant_dynamic-update-slice_fusion.own), channel_id=1, source_target_pairs={{0,2},{1,3},{2,0},{3,1},{4,6},{5,7},{6,4},{7,5},{8,10},{9,11},{10,... | collective-permute-start | bytes 1572872 | tf_op jit(solution)/shard_map/ppermute | solution.py:62
  8.3 1.5 %collective-permute-start.2 = (bf16[4,512,128]{2,1,0:T(8,128)(2,1)S(1)}, bf16[4,512,128]{2,1,0:T(8,128)(2,1)S(1)}, u32[]{:S(2)}, u32[]{:S(2)}) collective-permute-start(bf16[4,512,128]{2,1,0:T(8,128)(2,1)S(1)} %constant_dynamic-update-slice_fusion.own), channel_id=1, source_target_pairs={{0,4},{1,5},{2,6},{3,7},{4,0},{5,1},{6,2},{7,3},{8,12},{9,13},{10,... | collective-permute-start | bytes 1572872 | tf_op jit(solution)/shard_map/ppermute | solution.py:62
  9.8 0.1 pad_maximum_fusion
  9.8 3.2 %collective-permute-start.8 = (bf16[256,1024]{1,0:T(8,128)(2,1)S(1)}, bf16[256,1024]{1,0:T(8,128)(2,1)S(1)}, u32[]{:S(2)}, u32[]{:S(2)}) collective-permute-start(bf16[256,1024]{1,0:T(8,128)(2,1)S(1)} %pad_maximum_fusion), channel_id=1, source_target_pairs={{0,16},{24,8},{1,17},{25,9},{2,18},{26,10},{3,19},{27,11},{4,20},{... | collective-permute-start | bytes 1572872 | tf_op jit(solution)/shard_map/ppermute | solution.py:66
  13.0 0.0 collective-permute-done.4.from_inner
  13.0 1.3 %collective-permute-start.6 = (bf16[256,1536]{1,0:T(8,128)(2,1)S(1)}, bf16[256,1536]{1,0:T(8,128)(2,1)S(1)}, u32[]{:S(2)}, u32[]{:S(2)}) collective-permute-start(bf16[256,1536]{1,0:T(8,128)(2,1)S(1)} %collective-permute-done.4.from_inner), channel_id=1, source_target_pairs={{8,0},{16,24},{9,1},{17,25},{10,2},{18,26},{11,3},{19,27},{12,4},{... | collective-permute-start | bytes 2359304 | tf_op jit(solution)/shard_map/ppermute | solution.py:66
  14.3 0.0 copy-done
  14.4 6.7 %collective-permute-done.1.x = bf16[4,512,128]{2,1,0:T(8,128)(2,1)S(1)} collective-permute-done((bf16[4,512,128]{2,1,0:T(8,128)(2,1)S(1)}, bf16[4,512,128]{2,1,0:T(8,128)(2,1)S(1)}, u32[]{:S(2)}, u32[]{:S(2)}) %collective-permute-start.1) | collective-permute-done | bytes 524320 | tf_op jit(solution)/shard_map/ppermute | solution.py:62
  21.1 6.0 %collective-permute-start.7 = (bf16[256,512]{1,0:T(8,128)(2,1)S(1)}, bf16[256,512]{1,0:T(8,128)(2,1)S(1)}, u32[]{:S(2)}, u32[]{:S(2)}) collective-permute-start(bf16[256,512]{1,0:T(8,128)(2,1)S(1)} %pad_maximum_fusion.1), channel_id=1, source_target_pairs={{0,16},{24,8},{1,17},{25,9},{2,18},{26,10},{3,19},{27,11},{4,20},{... | collective-permute-start | bytes 786440 | tf_op jit(solution)/shard_map/ppermute | solution.py:66
  27.1 0.0 collective-permute-done.2.y
  27.2 0.0 collective-permute-done.3.near
  27.2 1.6 %collective-permute-start.5 = (bf16[4,512,128]{2,1,0:T(8,128)(2,1)S(1)}, bf16[4,512,128]{2,1,0:T(8,128)(2,1)S(1)}, u32[]{:S(2)}, u32[]{:S(2)}) collective-permute-start(bf16[4,512,128]{2,1,0:T(8,128)(2,1)S(1)} %collective-permute-done.1.x), channel_id=1, source_target_pairs={{0,4},{1,5},{2,6},{3,7},{4,0},{5,1},{6,2},{7,3},{8,12},{9,13},{10,... | collective-permute-start | bytes 1572872 | tf_op jit(solution)/shard_map/ppermute | solution.py:62
  28.8 5.3 %collective-permute-done.8 = bf16[256,1024]{1,0:T(8,128)(2,1)S(1)} collective-permute-done((bf16[256,1024]{1,0:T(8,128)(2,1)S(1)}, bf16[256,1024]{1,0:T(8,128)(2,1)S(1)}, u32[]{:S(2)}, u32[]{:S(2)}) %collective-permute-start.8) | collective-permute-done | bytes 524320 | tf_op jit(solution)/shard_map/ppermute | solution.py:66
  34.1 1.3 %collective-permute-start.9 = (bf16[256,512]{1,0:T(8,128)(2,1)S(1)}, bf16[256,512]{1,0:T(8,128)(2,1)S(1)}, u32[]{:S(2)}, u32[]{:S(2)}) collective-permute-start(bf16[256,512]{1,0:T(8,128)(2,1)S(1)} %pad_maximum_fusion.2.inner_a), channel_id=1, source_target_pairs={{8,0},{16,24},{9,1},{17,25},{10,2},{18,26},{11,3},{19,27},{12,4},{... | collective-permute-start | bytes 786440 | tf_op jit(solution)/shard_map/ppermute | solution.py:66
  35.4 4.0 %collective-permute-done.5.d = bf16[4,512,128]{2,1,0:T(8,128)(2,1)S(1)} collective-permute-done((bf16[4,512,128]{2,1,0:T(8,128)(2,1)S(1)}, bf16[4,512,128]{2,1,0:T(8,128)(2,1)S(1)}, u32[]{:S(2)}, u32[]{:S(2)}) %collective-permute-start.5) | collective-permute-done | bytes 524320 | tf_op jit(solution)/shard_map/ppermute | solution.py:62
  39.5 1.3 %collective-permute-start.11 = (bf16[256,512]{1,0:T(8,128)(2,1)S(1)}, bf16[256,512]{1,0:T(8,128)(2,1)S(1)}, u32[]{:S(2)}, u32[]{:S(2)}) collective-permute-start(bf16[256,512]{1,0:T(8,128)(2,1)S(1)} %pad_maximum_fusion.3.inner_b), channel_id=1, source_target_pairs={{8,0},{16,24},{9,1},{17,25},{10,2},{18,26},{11,3},{19,27},{12,4},{... | collective-permute-start | bytes 786440 | tf_op jit(solution)/shard_map/ppermute | solution.py:66
  40.8 0.0 collective-permute-done.7.from_inner
  40.8 7.1 %collective-permute-done.9.outer_a = bf16[256,512]{1,0:T(8,128)(2,1)S(1)} collective-permute-done((bf16[256,512]{1,0:T(8,128)(2,1)S(1)}, bf16[256,512]{1,0:T(8,128)(2,1)S(1)}, u32[]{:S(2)}, u32[]{:S(2)}) %collective-permute-start.9) | collective-permute-done | bytes 262176 | tf_op jit(solution)/shard_map/ppermute | solution.py:66
  47.9 1.3 %collective-permute-start.10 = (bf16[256,512]{1,0:T(8,128)(2,1)S(1)}, bf16[256,512]{1,0:T(8,128)(2,1)S(1)}, u32[]{:S(2)}, u32[]{:S(2)}) collective-permute-start(bf16[256,512]{1,0:T(8,128)(2,1)S(1)} %collective-permute-done.7.from_inner), channel_id=1, source_target_pairs={{8,0},{16,24},{9,1},{17,25},{10,2},{18,26},{11,3},{19,27},{12,4},{... | collective-permute-start | bytes 786440 | tf_op jit(solution)/shard_map/ppermute | solution.py:66
  49.1 0.6 %shard_map.28.left = bf16[4,2,512,512]{3,2,1,0:T(8,128)(2,1)S(1)} custom-call(bf16[4,512,128]{2,1,0:T(8,128)(2,1)S(1)} %constant_dynamic-update-slice_fusion.own, bf16[4,512,128]{2,1,0:T(8,128)(2,1)S(1)} %collective-permute-done.1.x, bf16[4,512,128]{2,1,0:T(8,128)(2,1)S(1)} %collective-permute-done.2.y, bf16[4,512,128]{2,1,0:T(8,128)(2,1)S(1)} %collective-permute-done.5.d), custom_call_target="tpu_custom_call" | custom-call | flops 1 | bytes 4194304 | tf_op jit(solution)/shard_map/pallas_call | solution.py:196
  49.7 0.0 collective-permute-done.6.from_outer
  49.8 3.6 %shard_map.29.acc = f32[6,512,256]{2,1,0:T(8,128)S(1)} custom-call(bf16[4,2,512,512]{3,2,1,0:T(8,128)(2,1)S(1)} %shard_map.28.left, bf16[256,1536]{1,0:T(8,128)(2,1)S(1)} %copy-done, bf16[256,1536]{1,0:T(8,128)(2,1)S(1)} %collective-permute-done.3.near, bf16[256,1536]{1,0:T(8,128)(2,1)S(1)} %collective-permute-done.4.from_inner, ...), custom_call_target="tpu_custom_call" | custom-call | flops 2415919104 | bytes 4194304 | tf_op jit(solution)/shard_map/pallas_call | solution.py:199
  53.4 0.1 collective-permute-done.11.outer_b
  53.5 1.5 %shard_map.30._ = bf16[512,1536]{1,0:T(8,128)(2,1)} custom-call(bf16[4,2,512,512]{3,2,1,0:T(8,128)(2,1)S(1)} %shard_map.28.left, f32[6,512,256]{2,1,0:T(8,128)S(1)} %shard_map.29.acc, bf16[256,512]{1,0:T(8,128)(2,1)S(1)} %pad_maximum_fusion.2.inner_a, bf16[256,512]{1,0:T(8,128)(2,1)S(1)} %collective-permute-done.9.outer_a, ...), custom_call_target="tpu_custom_call" | custom-call | flops 536870912 | bytes 4194304 | tf_op jit(solution)/shard_map/pallas_call | solution.py:204
  55.0 2.3 %collective-permute-done.10.from_outer = bf16[256,512]{1,0:T(8,128)(2,1)S(1)} collective-permute-done((bf16[256,512]{1,0:T(8,128)(2,1)S(1)}, bf16[256,512]{1,0:T(8,128)(2,1)S(1)}, u32[]{:S(2)}, u32[]{:S(2)}) %collective-permute-start.10) | collective-permute-done | bytes 262176 | tf_op jit(solution)/shard_map/ppermute | solution.py:66
  57.3 1.3 %shard_map.31 = bf16[512,1536]{1,0:T(8,128)(2,1)} custom-call(bf16[4,2,512,512]{3,2,1,0:T(8,128)(2,1)S(1)} %shard_map.28.left, f32[6,512,256]{2,1,0:T(8,128)S(1)} %shard_map.29.acc, bf16[256,512]{1,0:T(8,128)(2,1)S(1)} %collective-permute-done.7.from_inner, bf16[256,512]{1,0:T(8,128)(2,1)S(1)} %collective-permute-done.10.from_outer, ...), custom_call_target="tpu_custom_call", output_to_operand_aliasing={{}: (4, {})} | custom-call | flops 268435456 | bytes 1048576 | tf_op jit(solution)/shard_map/pallas_call | solution.py:207
  (7 shorter events, 0.2 us)
Async XLA Ops:
  0.0 14.3 %copy-start = (bf16[256,1536]{1,0:T(8,128)(2,1)S(1)}, bf16[256,1536]{1,0:T(8,128)(2,1)}, u32[]{:S(2)}) copy-start(bf16[256,1536]{1,0:T(8,128)(2,1)} %own.1) | copy-start | bytes 2359300
  0.0 13.0 %collective-permute-start.4 = (bf16[256,1536]{1,0:T(8,128)(2,1)}, bf16[256,1536]{1,0:T(8,128)(2,1)S(1)}, u32[]{:S(2)}, u32[]{:S(2)}) collective-permute-start(bf16[256,1536]{1,0:T(8,128)(2,1)} %own.1), channel_id=1, source_target_pairs={{0,1},{1,0},{2,3},{3,2},{4,5},{5,4},{6,7},{7,6},{8,16},{9,17},{10,... | collective-permute-start | bytes 2359304 | tf_op jit(solution)/shard_map/ppermute | solution.py:180
  0.5 26.7 %collective-permute-start.3 = (bf16[256,1536]{1,0:T(8,128)(2,1)}, bf16[256,1536]{1,0:T(8,128)(2,1)S(1)}, u32[]{:S(2)}, u32[]{:S(2)}) collective-permute-start(bf16[256,1536]{1,0:T(8,128)(2,1)} %own.1), channel_id=1, source_target_pairs={{0,8},{8,0},{16,24},{24,16},{1,9},{9,1},{17,25},{25,17},{2,10},{10... | collective-permute-start | bytes 2359304 | tf_op jit(solution)/shard_map/ppermute | solution.py:66
  4.6 2.0 %collective-permute-start = (bf16[2,512,128]{2,1,0:T(8,128)(2,1)}, bf16[2,512,128]{2,1,0:T(8,128)(2,1)S(1)}, u32[]{:S(2)}, u32[]{:S(2)}) collective-permute-start(bf16[2,512,128]{2,1,0:T(8,128)(2,1)} %param.2), channel_id=1, source_target_pairs={{0,1},{1,0},{2,3},{3,2},{4,5},{5,4},{6,7},{7,6},{8,9},{9,8},{10,11... | collective-permute-start | bytes 786440 | tf_op jit(solution)/shard_map/ppermute | solution.py:62
  6.7 14.4 %collective-permute-start.1 = (bf16[4,512,128]{2,1,0:T(8,128)(2,1)S(1)}, bf16[4,512,128]{2,1,0:T(8,128)(2,1)S(1)}, u32[]{:S(2)}, u32[]{:S(2)}) collective-permute-start(bf16[4,512,128]{2,1,0:T(8,128)(2,1)S(1)} %constant_dynamic-update-slice_fusion.own), channel_id=1, source_target_pairs={{0,2},{1,3},{2,0},{3,1},{4,6},{5,7},{6,4},{7,5},{8,10},{9,11},{10,... | collective-permute-start | bytes 1572872 | tf_op jit(solution)/shard_map/ppermute | solution.py:62
  8.3 18.9 %collective-permute-start.2 = (bf16[4,512,128]{2,1,0:T(8,128)(2,1)S(1)}, bf16[4,512,128]{2,1,0:T(8,128)(2,1)S(1)}, u32[]{:S(2)}, u32[]{:S(2)}) collective-permute-start(bf16[4,512,128]{2,1,0:T(8,128)(2,1)S(1)} %constant_dynamic-update-slice_fusion.own), channel_id=1, source_target_pairs={{0,4},{1,5},{2,6},{3,7},{4,0},{5,1},{6,2},{7,3},{8,12},{9,13},{10,... | collective-permute-start | bytes 1572872 | tf_op jit(solution)/shard_map/ppermute | solution.py:62
  9.8 24.2 %collective-permute-start.8 = (bf16[256,1024]{1,0:T(8,128)(2,1)S(1)}, bf16[256,1024]{1,0:T(8,128)(2,1)S(1)}, u32[]{:S(2)}, u32[]{:S(2)}) collective-permute-start(bf16[256,1024]{1,0:T(8,128)(2,1)S(1)} %pad_maximum_fusion), channel_id=1, source_target_pairs={{0,16},{24,8},{1,17},{25,9},{2,18},{26,10},{3,19},{27,11},{4,20},{... | collective-permute-start | bytes 1572872 | tf_op jit(solution)/shard_map/ppermute | solution.py:66
  13.0 36.7 %collective-permute-start.6 = (bf16[256,1536]{1,0:T(8,128)(2,1)S(1)}, bf16[256,1536]{1,0:T(8,128)(2,1)S(1)}, u32[]{:S(2)}, u32[]{:S(2)}) collective-permute-start(bf16[256,1536]{1,0:T(8,128)(2,1)S(1)} %collective-permute-done.4.from_inner), channel_id=1, source_target_pairs={{8,0},{16,24},{9,1},{17,25},{10,2},{18,26},{11,3},{19,27},{12,4},{... | collective-permute-start | bytes 2359304 | tf_op jit(solution)/shard_map/ppermute | solution.py:66
  21.1 19.7 %collective-permute-start.7 = (bf16[256,512]{1,0:T(8,128)(2,1)S(1)}, bf16[256,512]{1,0:T(8,128)(2,1)S(1)}, u32[]{:S(2)}, u32[]{:S(2)}) collective-permute-start(bf16[256,512]{1,0:T(8,128)(2,1)S(1)} %pad_maximum_fusion.1), channel_id=1, source_target_pairs={{0,16},{24,8},{1,17},{25,9},{2,18},{26,10},{3,19},{27,11},{4,20},{... | collective-permute-start | bytes 786440 | tf_op jit(solution)/shard_map/ppermute | solution.py:66
  27.2 12.3 %collective-permute-start.5 = (bf16[4,512,128]{2,1,0:T(8,128)(2,1)S(1)}, bf16[4,512,128]{2,1,0:T(8,128)(2,1)S(1)}, u32[]{:S(2)}, u32[]{:S(2)}) collective-permute-start(bf16[4,512,128]{2,1,0:T(8,128)(2,1)S(1)} %collective-permute-done.1.x), channel_id=1, source_target_pairs={{0,4},{1,5},{2,6},{3,7},{4,0},{5,1},{6,2},{7,3},{8,12},{9,13},{10,... | collective-permute-start | bytes 1572872 | tf_op jit(solution)/shard_map/ppermute | solution.py:62
  34.1 13.8 %collective-permute-start.9 = (bf16[256,512]{1,0:T(8,128)(2,1)S(1)}, bf16[256,512]{1,0:T(8,128)(2,1)S(1)}, u32[]{:S(2)}, u32[]{:S(2)}) collective-permute-start(bf16[256,512]{1,0:T(8,128)(2,1)S(1)} %pad_maximum_fusion.2.inner_a), channel_id=1, source_target_pairs={{8,0},{16,24},{9,1},{17,25},{10,2},{18,26},{11,3},{19,27},{12,4},{... | collective-permute-start | bytes 786440 | tf_op jit(solution)/shard_map/ppermute | solution.py:66
  39.5 14.0 %collective-permute-start.11 = (bf16[256,512]{1,0:T(8,128)(2,1)S(1)}, bf16[256,512]{1,0:T(8,128)(2,1)S(1)}, u32[]{:S(2)}, u32[]{:S(2)}) collective-permute-start(bf16[256,512]{1,0:T(8,128)(2,1)S(1)} %pad_maximum_fusion.3.inner_b), channel_id=1, source_target_pairs={{8,0},{16,24},{9,1},{17,25},{10,2},{18,26},{11,3},{19,27},{12,4},{... | collective-permute-start | bytes 786440 | tf_op jit(solution)/shard_map/ppermute | solution.py:66
  47.9 9.4 %collective-permute-start.10 = (bf16[256,512]{1,0:T(8,128)(2,1)S(1)}, bf16[256,512]{1,0:T(8,128)(2,1)S(1)}, u32[]{:S(2)}, u32[]{:S(2)}) collective-permute-start(bf16[256,512]{1,0:T(8,128)(2,1)S(1)} %collective-permute-done.7.from_inner), channel_id=1, source_target_pairs={{8,0},{16,24},{9,1},{17,25},{10,2},{18,26},{11,3},{19,27},{12,4},{... | collective-permute-start | bytes 786440 | tf_op jit(solution)/shard_map/ppermute | solution.py:66

commit v4 on v3

--- a/solution.py
+++ b/solution.py
@@ -112,14 +112,15 @@
     return (z == 1) | (z == 2)
 
 
-def most_kernel(left, own, near, from_inner, from_outer, out):
+def most_kernel(left, own, near, inner_a, outer_a, inner_b, outer_b, out):
     z = lax.axis_index("shot")
     inner = is_inner(z)
     blk = far_block(0, z)
     width = own.shape[1] // 2 // CHUNKS
     for i in range(CHUNKS):
         at = i * width
-        far = jnp.where(inner, tall(from_inner, at, width), tall(from_outer, at, width))
+        first, second, start = (inner_a, outer_a, at) if i < 2 else (inner_b, outer_b, 0)
+        far = jnp.where(inner, tall(first, start, width), tall(second, start, width))
         right = jnp.concatenate([tall(own, at, width), tall(near, at, width), far], axis=0)
 
         def body(part, carry):
@@ -177,33 +178,36 @@
     width = cols // 2 // CHUNKS
 
     near = over_shot(rcv_side, SWAP_OUTER)
-    mid = lax.ppermute(rcv_side, ("shot", "rcv"), SWAP_INNER)
+    mid_a, mid_b = (lax.ppermute(piece, ("shot", "rcv"), SWAP_INNER) for piece in cut(rcv_side, (2, 1)))
 
     core = flipped(shot_side, 1)
     chip = jnp.concatenate([shot_side, core])
     x, y = flipped(chip, 2), flipped(chip, 4)
-    diag = flipped(after(x, y, near, mid), 4)
-
-    outer_mid = over_shot(mid, OUTWARD)
-    across_a, across_b = cut(rcv_side, (2, 1))
-    across_a = over_shot(after(across_a, core), ACROSS)
-    across_b = over_shot(across_b, ACROSS)
-    inner = cut(across_a, (1, 1), 2) + [across_b]
-    outer_a = over_shot(inner[0], OUTWARD)
-    outer_b = over_shot(after(inner[1], near, diag), OUTWARD)
-    outer_c = over_shot(after(inner[2], near, outer_a), OUTWARD)
+    diag = flipped(after(x, mid_a, mid_b), 4)
+
+    outer_mid_a = over_shot(mid_a, OUTWARD)
+    outer_mid_b = over_shot(after(mid_b, near, x, y, core), OUTWARD)
+    across = cut(rcv_side, (1, 1, 1))
+    inner_a = over_shot(after(across[0], near, mid_b, y), ACROSS)
+    inner_b = over_shot(after(across[1], mid_b, near, core), ACROSS)
+    inner_c = over_shot(after(across[2], near, core), ACROSS)
+    outer_a = over_shot(inner_a, OUTWARD)
+    outer_b = over_shot(inner_b, OUTWARD)
+    outer_c = over_shot(after(inner_c, diag, mid_a, outer_mid_a, outer_mid_b), OUTWARD)
 
     left = kernel_call(stack_kernel, jax.ShapeDtypeStruct((4, 2, shots, 512), jnp.bfloat16), 1, 4)(chip, x, y, diag)
     block_flops = 8 * shots * 256 * (cols // 2)
     acc_shape = jax.ShapeDtypeStruct((2 * CHUNKS, shots, width), jnp.float32)
-    acc = kernel_call(most_kernel, acc_shape, 3 * block_flops, 5)(left, rcv_side, near, mid, outer_mid)
+    acc = kernel_call(most_kernel, acc_shape, 3 * block_flops, 7)(
+        left, rcv_side, near, mid_a, outer_mid_a, mid_b, outer_mid_b
+    )
 
     out_shape = jax.ShapeDtypeStruct((shots, cols), jnp.bfloat16)
     scratch = [pltpu.VMEM((2 * CHUNKS, shots, width), jnp.bfloat16), pltpu.SemaphoreType.DMA((4 * CHUNKS,))]
     in_place = pl.BlockSpec(memory_space=pl.ANY)
     out = kernel_call(
         first_kernel, out_shape, block_flops * 2 // 3, 6, out_specs=in_place, scratch_shapes=scratch
-    )(left, acc, inner[0], outer_a, inner[1], outer_b)
+    )(left, acc, inner_a, outer_a, inner_b, outer_b)
     return pl.pallas_call(
         last_kernel,
         out_shape=out_shape,
@@ -213,13 +217,24 @@
         input_output_aliases={4: 0},
         compiler_params=pltpu.CompilerParams(vmem_limit_bytes=VMEM_LIMIT),
         cost_estimate=pl.CostEstimate(flops=block_flops // 3, bytes_accessed=1 << 20, transcendentals=0),
-    )(left, acc, inner[2], outer_c, out)
+    )(left, acc, inner_c, outer_c, out)
+
+
+def on_device(shot_side, rcv_side):
+    line = (
+        STEPS == 4
+        and lax.axis_size("shot") == 4
+        and lax.axis_size("rcv") == 8
+        and shot_side.shape[2] == 128
+        and rcv_side.shape[0] == 256
+        and rcv_side.shape[1] % (2 * CHUNKS * 128) == 0
+    )
+    return (line_on_device if line else ring_on_device)(shot_side, rcv_side)
 
 
 def solution(mesh):
-    line = mesh.shape["shot"] == 4 and mesh.shape["rcv"] == 8 and STEPS == 4
     return jax.shard_map(
-        line_on_device if line else ring_on_device,
+        on_device,
         mesh=mesh,
         in_specs=(P(None, "shot", "rcv"), P("shot", "rcv")),
         out_specs=P("shot", "rcv"),

time: 58.8 us -> 58.6 us (level)
  waiting for transfers between devices: 25.5 us -> 20.3 us
  starting transfers between devices: 23.6 us -> 28.6 us
    ppermute x7 -> x9, starting transfers between devices: 18.5 us -> 23.2 us  [over_shot(): return lax.ppermute(value, 'shot', pairs)]
    ppermute x7 -> x9, waiting for transfers between devices: 14.8 us -> 10.6 us  [over_shot(): return lax.ppermute(value, 'shot', pairs)]
    ppermute x4, waiting for transfers between devices: 10.7 us -> 9.42 us  [flipped(): return lax.ppermute(value, 'rcv', [(i, i ^ bit) for i in range(8)])]
  transfers between devices with their start and end apart: 12 -> 15, of which waited for: 6 -> 8; matrix products, arithmetic and copies ran while one was open for 4% -> 4% of each run, Pallas kernels for 10% -> 10%
where the time goes in v4:
time: 58.6 us; the launch traced here: 58.3 us
  starting transfers between devices  28.6 us (49%)
  waiting for transfers between devices  20.3 us (35%)
  Pallas kernels  7.04 us (12%)
  local copies, waits for them, and re-layouts  2.12 us (4%)
    ppermute x9, starting transfers between devices, over_shot(): return lax.ppermute(value, 'shot', pairs)  23.2 us
    ppermute x9, waiting for transfers between devices, over_shot(): return lax.ppermute(value, 'shot', pairs)  10.6 us
    ppermute x4, waiting for transfers between devices, flipped(): return lax.ppermute(value, 'rcv', [(i, i ^ bit) for i in range(8)])  9.42 us
    ppermute x4, starting transfers between devices, flipped(): return lax.ppermute(value, 'rcv', [(i, i ^ bit) for i in range(8)])  5.11 us
    pallas_call x1, Pallas kernels, line_on_device(): kernel_call(most_kernel, acc_shape, 3 * block_flops, 7)  3.64 us
    pallas_call x1, Pallas kernels, line_on_device(): kernel_call(first_kernel, out_shape, block_flops * 2 // 3, 6, out_specs=i...  1.54 us
    pallas_call x1, Pallas kernels, line_on_device(): pl.pallas_call(last_kernel, out_shape=out_shape, in_specs=[pl.BlockSpec(m...  1.26 us
  transfers between devices with their start and end apart: 15, of which 8 were waited for; matrix products, arithmetic and copies ran while one was open for 4% of the time, Pallas kernels for 10%

profile of v4, /device:TPU:0, one launch (start us, length us, event | category | flops | bytes accessed | tf_op | source)
XLA Modules:
  0.0 58.3 jit_solution(6408109917533756469)
XLA Ops:
  0.0 0.5 collective-permute-start
  0.5 2.6 %collective-permute-start.6 = (bf16[256,1536]{1,0:T(8,128)(2,1)}, bf16[256,1536]{1,0:T(8,128)(2,1)S(1)}, u32[]{:S(2)}, u32[]{:S(2)}) collective-permute-start(bf16[256,1536]{1,0:T(8,128)(2,1)} %own.1), channel_id=1, source_target_pairs={{0,8},{8,0},{16,24},{24,16},{1,9},{9,1},{17,25},{25,17},{2,10},{10... | collective-permute-start | bytes 2359304 | tf_op jit(solution)/shard_map/ppermute | solution.py:66
  3.1 1.1 %fusion.1 = (bf16[256,512]{1,0:T(8,128)(2,1)S(1)}, bf16[256,512]{1,0:T(8,128)(2,1)S(1)}) fusion(bf16[256,1536]{1,0:T(8,128)(2,1)} %own.1), kind=kLoop, calls=%fused_computation.7 | loop fusion | bytes 1048576 | tf_op jit(solution)/shard_map/slice | solution.py:171
  4.2 0.1 pad_maximum_fusion
  4.2 0.2 collective-permute-start.3
  4.5 1.0 %constant_dynamic-update-slice_fusion.1 = bf16[4,512,128]{2,1,0:T(8,128)(2,1)S(1)} fusion(bf16[2,512,128]{2,1,0:T(8,128)(2,1)} %param.2), kind=kLoop, calls=%fused_computation.5 | loop fusion | bytes 524288
  5.4 0.0 collective-permute-done
  5.5 1.6 %collective-permute-start.1 = (bf16[4,512,128]{2,1,0:T(8,128)(2,1)S(1)}, bf16[4,512,128]{2,1,0:T(8,128)(2,1)S(1)}, u32[]{:S(2)}, u32[]{:S(2)}) collective-permute-start(bf16[4,512,128]{2,1,0:T(8,128)(2,1)S(1)} %constant_dynamic-update-slice_fusion.own), channel_id=1, source_target_pairs={{0,2},{1,3},{2,0},{3,1},{4,6},{5,7},{6,4},{7,5},{8,10},{9,11},{10,... | collective-permute-start | bytes 1572872 | tf_op jit(solution)/shard_map/ppermute | solution.py:62
  7.0 0.1 fusion
  7.1 1.6 %collective-permute-start.2 = (bf16[4,512,128]{2,1,0:T(8,128)(2,1)S(1)}, bf16[4,512,128]{2,1,0:T(8,128)(2,1)S(1)}, u32[]{:S(2)}, u32[]{:S(2)}) collective-permute-start(bf16[4,512,128]{2,1,0:T(8,128)(2,1)S(1)} %constant_dynamic-update-slice_fusion.own), channel_id=1, source_target_pairs={{0,4},{1,5},{2,6},{3,7},{4,0},{5,1},{6,2},{7,3},{8,12},{9,13},{10,... | collective-permute-start | bytes 1572872 | tf_op jit(solution)/shard_map/ppermute | solution.py:62
  8.7 0.1 collective-permute-start.4
  8.8 1.3 %collective-permute-start.7 = (bf16[256,1024]{1,0:T(8,128)(2,1)S(1)}, bf16[256,1024]{1,0:T(8,128)(2,1)S(1)}, u32[]{:S(2)}, u32[]{:S(2)}) collective-permute-start(bf16[256,1024]{1,0:T(8,128)(2,1)S(1)} %collective-permute-done.3.inner_a), channel_id=1, source_target_pairs={{8,0},{16,24},{9,1},{17,25},{10,2},{18,26},{11,3},{19,27},{12,4},{... | collective-permute-start | bytes 1572872 | tf_op jit(solution)/shard_map/ppermute | solution.py:66
  10.1 0.2 collective-permute-done.4.inner_b
  10.3 9.4 %collective-permute-done.1.x = bf16[4,512,128]{2,1,0:T(8,128)(2,1)S(1)} collective-permute-done((bf16[4,512,128]{2,1,0:T(8,128)(2,1)S(1)}, bf16[4,512,128]{2,1,0:T(8,128)(2,1)S(1)}, u32[]{:S(2)}, u32[]{:S(2)}) %collective-permute-start.1) | collective-permute-done | bytes 524320 | tf_op jit(solution)/shard_map/ppermute | solution.py:62
  19.7 1.5 %collective-permute-start.5 = (bf16[4,512,128]{2,1,0:T(8,128)(2,1)S(1)}, bf16[4,512,128]{2,1,0:T(8,128)(2,1)S(1)}, u32[]{:S(2)}, u32[]{:S(2)}) collective-permute-start(bf16[4,512,128]{2,1,0:T(8,128)(2,1)S(1)} %collective-permute-done.1.x), channel_id=1, source_target_pairs={{0,4},{1,5},{2,6},{3,7},{4,0},{5,1},{6,2},{7,3},{8,12},{9,13},{10,... | collective-permute-start | bytes 1572872 | tf_op jit(solution)/shard_map/ppermute | solution.py:62
  21.3 0.2 collective-permute-done.6.near
  21.5 8.6 %collective-permute-start.11 = (bf16[256,512]{1,0:T(8,128)(2,1)S(1)}, bf16[256,512]{1,0:T(8,128)(2,1)S(1)}, u32[]{:S(2)}, u32[]{:S(2)}) collective-permute-start(bf16[256,512]{1,0:T(8,128)(2,1)S(1)} %pad_maximum_fusion.2), channel_id=1, source_target_pairs={{0,16},{24,8},{1,17},{25,9},{2,18},{26,10},{3,19},{27,11},{4,20},{... | collective-permute-start | bytes 786440 | tf_op jit(solution)/shard_map/ppermute | solution.py:66
  30.0 1.3 %collective-permute-start.13 = (bf16[256,512]{1,0:T(8,128)(2,1)S(1)}, bf16[256,512]{1,0:T(8,128)(2,1)S(1)}, u32[]{:S(2)}, u32[]{:S(2)}) collective-permute-start(bf16[256,512]{1,0:T(8,128)(2,1)S(1)} %pad_maximum_fusion.3), channel_id=1, source_target_pairs={{0,16},{24,8},{1,17},{25,9},{2,18},{26,10},{3,19},{27,11},{4,20},{... | collective-permute-start | bytes 786440 | tf_op jit(solution)/shard_map/ppermute | solution.py:66
  31.3 1.3 %collective-permute-start.8 = (bf16[256,512]{1,0:T(8,128)(2,1)S(1)}, bf16[256,512]{1,0:T(8,128)(2,1)S(1)}, u32[]{:S(2)}, u32[]{:S(2)}) collective-permute-start(bf16[256,512]{1,0:T(8,128)(2,1)S(1)} %collective-permute-done.4.inner_b), channel_id=1, source_target_pairs={{8,0},{16,24},{9,1},{17,25},{10,2},{18,26},{11,3},{19,27},{12,4},{... | collective-permute-start | bytes 786440 | tf_op jit(solution)/shard_map/ppermute | solution.py:66
  32.6 0.1 collective-permute-done.7.outer_a
  32.7 4.2 %collective-permute-start.9 = (bf16[256,512]{1,0:T(8,128)(2,1)S(1)}, bf16[256,512]{1,0:T(8,128)(2,1)S(1)}, u32[]{:S(2)}, u32[]{:S(2)}) collective-permute-start(bf16[256,512]{1,0:T(8,128)(2,1)S(1)} %pad_maximum_fusion.1), channel_id=1, source_target_pairs={{0,16},{24,8},{1,17},{25,9},{2,18},{26,10},{3,19},{27,11},{4,20},{... | collective-permute-start | bytes 786440 | tf_op jit(solution)/shard_map/ppermute | solution.py:66
  37.0 1.3 %collective-permute-start.12 = (bf16[256,512]{1,0:T(8,128)(2,1)S(1)}, bf16[256,512]{1,0:T(8,128)(2,1)S(1)}, u32[]{:S(2)}, u32[]{:S(2)}) collective-permute-start(bf16[256,512]{1,0:T(8,128)(2,1)S(1)} %collective-permute-done.11.inner_a), channel_id=1, source_target_pairs={{8,0},{16,24},{9,1},{17,25},{10,2},{18,26},{11,3},{19,27},{12,4},{... | collective-permute-start | bytes 786440 | tf_op jit(solution)/shard_map/ppermute | solution.py:66
  38.3 4.1 %collective-permute-done.13.inner_b = bf16[256,512]{1,0:T(8,128)(2,1)S(1)} collective-permute-done((bf16[256,512]{1,0:T(8,128)(2,1)S(1)}, bf16[256,512]{1,0:T(8,128)(2,1)S(1)}, u32[]{:S(2)}, u32[]{:S(2)}) %collective-permute-start.13) | collective-permute-done | bytes 262176 | tf_op jit(solution)/shard_map/ppermute | solution.py:66
  42.4 1.3 %collective-permute-start.14 = (bf16[256,512]{1,0:T(8,128)(2,1)S(1)}, bf16[256,512]{1,0:T(8,128)(2,1)S(1)}, u32[]{:S(2)}, u32[]{:S(2)}) collective-permute-start(bf16[256,512]{1,0:T(8,128)(2,1)S(1)} %collective-permute-done.13.inner_b), channel_id=1, source_target_pairs={{8,0},{16,24},{9,1},{17,25},{10,2},{18,26},{11,3},{19,27},{12,4},{... | collective-permute-start | bytes 786440 | tf_op jit(solution)/shard_map/ppermute | solution.py:66
  43.7 2.3 %collective-permute-done.9.from_inner = bf16[256,512]{1,0:T(8,128)(2,1)S(1)} collective-permute-done((bf16[256,512]{1,0:T(8,128)(2,1)S(1)}, bf16[256,512]{1,0:T(8,128)(2,1)S(1)}, u32[]{:S(2)}, u32[]{:S(2)}) %collective-permute-start.9) | collective-permute-done | bytes 262176 | tf_op jit(solution)/shard_map/ppermute | solution.py:66
  46.0 1.3 %collective-permute-start.10 = (bf16[256,512]{1,0:T(8,128)(2,1)S(1)}, bf16[256,512]{1,0:T(8,128)(2,1)S(1)}, u32[]{:S(2)}, u32[]{:S(2)}) collective-permute-start(bf16[256,512]{1,0:T(8,128)(2,1)S(1)} %collective-permute-done.9.from_inner), channel_id=1, source_target_pairs={{8,0},{16,24},{9,1},{17,25},{10,2},{18,26},{11,3},{19,27},{12,4},{... | collective-permute-start | bytes 786440 | tf_op jit(solution)/shard_map/ppermute | solution.py:66
  47.3 0.6 %shard_map.28.left = bf16[4,2,512,512]{3,2,1,0:T(8,128)(2,1)S(1)} custom-call(bf16[4,512,128]{2,1,0:T(8,128)(2,1)S(1)} %constant_dynamic-update-slice_fusion.own, bf16[4,512,128]{2,1,0:T(8,128)(2,1)S(1)} %collective-permute-done.1.x, bf16[4,512,128]{2,1,0:T(8,128)(2,1)S(1)} %collective-permute-done.2.y, bf16[4,512,128]{2,1,0:T(8,128)(2,1)S(1)} %collective-permute-done.5.d), custom_call_target="tpu_custom_call" | custom-call | flops 1 | bytes 4194304 | tf_op jit(solution)/shard_map/pallas_call | solution.py:198
  47.9 3.6 %shard_map.29.acc = f32[6,512,256]{2,1,0:T(8,128)S(1)} custom-call(bf16[4,2,512,512]{3,2,1,0:T(8,128)(2,1)S(1)} %shard_map.28.left, bf16[256,1536]{1,0:T(8,128)(2,1)S(1)} %copy-done, bf16[256,1536]{1,0:T(8,128)(2,1)S(1)} %collective-permute-done.6.near, bf16[256,1024]{1,0:T(8,128)(2,1)S(1)} %collective-permute-done.3.inner_a, ...), custom_call_target="tpu_custom_call" | custom-call | flops 2415919104 | bytes 4194304 | tf_op jit(solution)/shard_map/pallas_call | solution.py:201
  51.6 2.2 %collective-permute-done.14.outer_b = bf16[256,512]{1,0:T(8,128)(2,1)S(1)} collective-permute-done((bf16[256,512]{1,0:T(8,128)(2,1)S(1)}, bf16[256,512]{1,0:T(8,128)(2,1)S(1)}, u32[]{:S(2)}, u32[]{:S(2)}) %collective-permute-start.14) | collective-permute-done | bytes 262176 | tf_op jit(solution)/shard_map/ppermute | solution.py:66
  53.7 1.5 %shard_map.30._ = bf16[512,1536]{1,0:T(8,128)(2,1)} custom-call(bf16[4,2,512,512]{3,2,1,0:T(8,128)(2,1)S(1)} %shard_map.28.left, f32[6,512,256]{2,1,0:T(8,128)S(1)} %shard_map.29.acc, bf16[256,512]{1,0:T(8,128)(2,1)S(1)} %collective-permute-done.11.inner_a, bf16[256,512]{1,0:T(8,128)(2,1)S(1)} %collective-permute-done.12.outer_a, ...), custom_call_target="tpu_custom_call" | custom-call | flops 536870912 | bytes 4194304 | tf_op jit(solution)/shard_map/pallas_call | solution.py:208
  55.3 1.8 %collective-permute-done.10.from_outer = bf16[256,512]{1,0:T(8,128)(2,1)S(1)} collective-permute-done((bf16[256,512]{1,0:T(8,128)(2,1)S(1)}, bf16[256,512]{1,0:T(8,128)(2,1)S(1)}, u32[]{:S(2)}, u32[]{:S(2)}) %collective-permute-start.10) | collective-permute-done | bytes 262176 | tf_op jit(solution)/shard_map/ppermute | solution.py:66
  57.1 1.3 %shard_map.31 = bf16[512,1536]{1,0:T(8,128)(2,1)} custom-call(bf16[4,2,512,512]{3,2,1,0:T(8,128)(2,1)S(1)} %shard_map.28.left, f32[6,512,256]{2,1,0:T(8,128)S(1)} %shard_map.29.acc, bf16[256,512]{1,0:T(8,128)(2,1)S(1)} %collective-permute-done.9.from_inner, bf16[256,512]{1,0:T(8,128)(2,1)S(1)} %collective-permute-done.10.from_outer, ...), custom_call_target="tpu_custom_call", output_to_operand_aliasing={{}: (4, {})} | custom-call | flops 268435456 | bytes 1048576 | tf_op jit(solution)/shard_map/pallas_call | solution.py:211
  (12 shorter events, 0.1 us)
Async XLA Ops:
  0.0 7.0 %copy-start = (bf16[256,1536]{1,0:T(8,128)(2,1)S(1)}, bf16[256,1536]{1,0:T(8,128)(2,1)}, u32[]{:S(2)}) copy-start(bf16[256,1536]{1,0:T(8,128)(2,1)} %own.1) | copy-start | bytes 2359300
  0.0 5.4 %collective-permute-start = (bf16[2,512,128]{2,1,0:T(8,128)(2,1)}, bf16[2,512,128]{2,1,0:T(8,128)(2,1)S(1)}, u32[]{:S(2)}, u32[]{:S(2)}) collective-permute-start(bf16[2,512,128]{2,1,0:T(8,128)(2,1)} %param.2), channel_id=1, source_target_pairs={{0,1},{1,0},{2,3},{3,2},{4,5},{5,4},{6,7},{7,6},{8,9},{9,8},{10,11... | collective-permute-start | bytes 786440 | tf_op jit(solution)/shard_map/ppermute | solution.py:62
  0.5 21.0 %collective-permute-start.6 = (bf16[256,1536]{1,0:T(8,128)(2,1)}, bf16[256,1536]{1,0:T(8,128)(2,1)S(1)}, u32[]{:S(2)}, u32[]{:S(2)}) collective-permute-start(bf16[256,1536]{1,0:T(8,128)(2,1)} %own.1), channel_id=1, source_target_pairs={{0,8},{8,0},{16,24},{24,16},{1,9},{9,1},{17,25},{25,17},{2,10},{10... | collective-permute-start | bytes 2359304 | tf_op jit(solution)/shard_map/ppermute | solution.py:66
  4.2 4.6 %collective-permute-start.3 = (bf16[256,1024]{1,0:T(8,128)(2,1)S(1)}, bf16[256,1024]{1,0:T(8,128)(2,1)S(1)}, u32[]{:S(2)}, u32[]{:S(2)}) collective-permute-start(bf16[256,1024]{1,0:T(8,128)(2,1)S(1)} %pad_maximum_fusion), channel_id=1, source_target_pairs={{0,1},{1,0},{2,3},{3,2},{4,5},{5,4},{6,7},{7,6},{8,16},{9,17},{10,... | collective-permute-start | bytes 1572872 | tf_op jit(solution)/shard_map/ppermute | solution.py:181
  5.5 14.2 %collective-permute-start.1 = (bf16[4,512,128]{2,1,0:T(8,128)(2,1)S(1)}, bf16[4,512,128]{2,1,0:T(8,128)(2,1)S(1)}, u32[]{:S(2)}, u32[]{:S(2)}) collective-permute-start(bf16[4,512,128]{2,1,0:T(8,128)(2,1)S(1)} %constant_dynamic-update-slice_fusion.own), channel_id=1, source_target_pairs={{0,2},{1,3},{2,0},{3,1},{4,6},{5,7},{6,4},{7,5},{8,10},{9,11},{10,... | collective-permute-start | bytes 1572872 | tf_op jit(solution)/shard_map/ppermute | solution.py:62
  7.1 14.4 %collective-permute-start.2 = (bf16[4,512,128]{2,1,0:T(8,128)(2,1)S(1)}, bf16[4,512,128]{2,1,0:T(8,128)(2,1)S(1)}, u32[]{:S(2)}, u32[]{:S(2)}) collective-permute-start(bf16[4,512,128]{2,1,0:T(8,128)(2,1)S(1)} %constant_dynamic-update-slice_fusion.own), channel_id=1, source_target_pairs={{0,4},{1,5},{2,6},{3,7},{4,0},{5,1},{6,2},{7,3},{8,12},{9,13},{10,... | collective-permute-start | bytes 1572872 | tf_op jit(solution)/shard_map/ppermute | solution.py:62
  8.7 1.6 %collective-permute-start.4 = (bf16[256,512]{1,0:T(8,128)(2,1)S(1)}, bf16[256,512]{1,0:T(8,128)(2,1)S(1)}, u32[]{:S(2)}, u32[]{:S(2)}) collective-permute-start(bf16[256,512]{1,0:T(8,128)(2,1)S(1)} %pad_maximum_fusion.1), channel_id=1, source_target_pairs={{0,1},{1,0},{2,3},{3,2},{4,5},{5,4},{6,7},{7,6},{8,16},{9,17},{10,... | collective-permute-start | bytes 786440 | tf_op jit(solution)/shard_map/ppermute | solution.py:181
  8.8 23.9 %collective-permute-start.7 = (bf16[256,1024]{1,0:T(8,128)(2,1)S(1)}, bf16[256,1024]{1,0:T(8,128)(2,1)S(1)}, u32[]{:S(2)}, u32[]{:S(2)}) collective-permute-start(bf16[256,1024]{1,0:T(8,128)(2,1)S(1)} %collective-permute-done.3.inner_a), channel_id=1, source_target_pairs={{8,0},{16,24},{9,1},{17,25},{10,2},{18,26},{11,3},{19,27},{12,4},{... | collective-permute-start | bytes 1572872 | tf_op jit(solution)/shard_map/ppermute | solution.py:66
  19.7 26.3 %collective-permute-start.5 = (bf16[4,512,128]{2,1,0:T(8,128)(2,1)S(1)}, bf16[4,512,128]{2,1,0:T(8,128)(2,1)S(1)}, u32[]{:S(2)}, u32[]{:S(2)}) collective-permute-start(bf16[4,512,128]{2,1,0:T(8,128)(2,1)S(1)} %collective-permute-done.1.x), channel_id=1, source_target_pairs={{0,4},{1,5},{2,6},{3,7},{4,0},{5,1},{6,2},{7,3},{8,12},{9,13},{10,... | collective-permute-start | bytes 1572872 | tf_op jit(solution)/shard_map/ppermute | solution.py:62
  21.5 15.5 %collective-permute-start.11 = (bf16[256,512]{1,0:T(8,128)(2,1)S(1)}, bf16[256,512]{1,0:T(8,128)(2,1)S(1)}, u32[]{:S(2)}, u32[]{:S(2)}) collective-permute-start(bf16[256,512]{1,0:T(8,128)(2,1)S(1)} %pad_maximum_fusion.2), channel_id=1, source_target_pairs={{0,16},{24,8},{1,17},{25,9},{2,18},{26,10},{3,19},{27,11},{4,20},{... | collective-permute-start | bytes 786440 | tf_op jit(solution)/shard_map/ppermute | solution.py:66
  30.0 12.3 %collective-permute-start.13 = (bf16[256,512]{1,0:T(8,128)(2,1)S(1)}, bf16[256,512]{1,0:T(8,128)(2,1)S(1)}, u32[]{:S(2)}, u32[]{:S(2)}) collective-permute-start(bf16[256,512]{1,0:T(8,128)(2,1)S(1)} %pad_maximum_fusion.3), channel_id=1, source_target_pairs={{0,16},{24,8},{1,17},{25,9},{2,18},{26,10},{3,19},{27,11},{4,20},{... | collective-permute-start | bytes 786440 | tf_op jit(solution)/shard_map/ppermute | solution.py:66
  31.3 12.3 %collective-permute-start.8 = (bf16[256,512]{1,0:T(8,128)(2,1)S(1)}, bf16[256,512]{1,0:T(8,128)(2,1)S(1)}, u32[]{:S(2)}, u32[]{:S(2)}) collective-permute-start(bf16[256,512]{1,0:T(8,128)(2,1)S(1)} %collective-permute-done.4.inner_b), channel_id=1, source_target_pairs={{8,0},{16,24},{9,1},{17,25},{10,2},{18,26},{11,3},{19,27},{12,4},{... | collective-permute-start | bytes 786440 | tf_op jit(solution)/shard_map/ppermute | solution.py:66
  32.7 13.3 %collective-permute-start.9 = (bf16[256,512]{1,0:T(8,128)(2,1)S(1)}, bf16[256,512]{1,0:T(8,128)(2,1)S(1)}, u32[]{:S(2)}, u32[]{:S(2)}) collective-permute-start(bf16[256,512]{1,0:T(8,128)(2,1)S(1)} %pad_maximum_fusion.1), channel_id=1, source_target_pairs={{0,16},{24,8},{1,17},{25,9},{2,18},{26,10},{3,19},{27,11},{4,20},{... | collective-permute-start | bytes 786440 | tf_op jit(solution)/shard_map/ppermute | solution.py:66
  37.0 14.6 %collective-permute-start.12 = (bf16[256,512]{1,0:T(8,128)(2,1)S(1)}, bf16[256,512]{1,0:T(8,128)(2,1)S(1)}, u32[]{:S(2)}, u32[]{:S(2)}) collective-permute-start(bf16[256,512]{1,0:T(8,128)(2,1)S(1)} %collective-permute-done.11.inner_a), channel_id=1, source_target_pairs={{8,0},{16,24},{9,1},{17,25},{10,2},{18,26},{11,3},{19,27},{12,4},{... | collective-permute-start | bytes 786440 | tf_op jit(solution)/shard_map/ppermute | solution.py:66
  42.4 11.3 %collective-permute-start.14 = (bf16[256,512]{1,0:T(8,128)(2,1)S(1)}, bf16[256,512]{1,0:T(8,128)(2,1)S(1)}, u32[]{:S(2)}, u32[]{:S(2)}) collective-permute-start(bf16[256,512]{1,0:T(8,128)(2,1)S(1)} %collective-permute-done.13.inner_b), channel_id=1, source_target_pairs={{8,0},{16,24},{9,1},{17,25},{10,2},{18,26},{11,3},{19,27},{12,4},{... | collective-permute-start | bytes 786440 | tf_op jit(solution)/shard_map/ppermute | solution.py:66
  46.0 11.1 %collective-permute-start.10 = (bf16[256,512]{1,0:T(8,128)(2,1)S(1)}, bf16[256,512]{1,0:T(8,128)(2,1)S(1)}, u32[]{:S(2)}, u32[]{:S(2)}) collective-permute-start(bf16[256,512]{1,0:T(8,128)(2,1)S(1)} %collective-permute-done.9.from_inner), channel_id=1, source_target_pairs={{8,0},{16,24},{9,1},{17,25},{10,2},{18,26},{11,3},{19,27},{12,4},{... | collective-permute-start | bytes 786440 | tf_op jit(solution)/shard_map/ppermute | solution.py:66

commit v5 on v4

--- a/solution.py
+++ b/solution.py
@@ -112,15 +112,14 @@
     return (z == 1) | (z == 2)
 
 
-def most_kernel(left, own, near, inner_a, outer_a, inner_b, outer_b, out):
+def most_kernel(left, own, near, from_inner, from_outer, out):
     z = lax.axis_index("shot")
     inner = is_inner(z)
     blk = far_block(0, z)
     width = own.shape[1] // 2 // CHUNKS
     for i in range(CHUNKS):
         at = i * width
-        first, second, start = (inner_a, outer_a, at) if i < 2 else (inner_b, outer_b, 0)
-        far = jnp.where(inner, tall(first, start, width), tall(second, start, width))
+        far = jnp.where(inner, tall(from_inner, at, width), tall(from_outer, at, width))
         right = jnp.concatenate([tall(own, at, width), tall(near, at, width), far], axis=0)
 
         def body(part, carry):
@@ -178,29 +177,26 @@
     width = cols // 2 // CHUNKS
 
     near = over_shot(rcv_side, SWAP_OUTER)
-    mid_a, mid_b = (lax.ppermute(piece, ("shot", "rcv"), SWAP_INNER) for piece in cut(rcv_side, (2, 1)))
+    mid = lax.ppermute(rcv_side, ("shot", "rcv"), SWAP_INNER)
 
     core = flipped(shot_side, 1)
     chip = jnp.concatenate([shot_side, core])
-    x, y = flipped(chip, 2), flipped(chip, 4)
-    diag = flipped(after(x, mid_a, mid_b), 4)
-
-    outer_mid_a = over_shot(mid_a, OUTWARD)
-    outer_mid_b = over_shot(after(mid_b, near, x, y, core), OUTWARD)
+    x, y = flipped(after(chip, core), 2), flipped(chip, 4)
+    diag = flipped(after(x, y, near, mid), 4)
+
+    outer_mid = over_shot(after(mid, core), OUTWARD)
     across = cut(rcv_side, (1, 1, 1))
-    inner_a = over_shot(after(across[0], near, mid_b, y), ACROSS)
-    inner_b = over_shot(after(across[1], mid_b, near, core), ACROSS)
-    inner_c = over_shot(after(across[2], near, core), ACROSS)
-    outer_a = over_shot(inner_a, OUTWARD)
-    outer_b = over_shot(inner_b, OUTWARD)
-    outer_c = over_shot(after(inner_c, diag, mid_a, outer_mid_a, outer_mid_b), OUTWARD)
+    inner_a = over_shot(across[0], ACROSS)
+    inner_b = over_shot(across[1], ACROSS)
+    inner_c = over_shot(after(across[2], inner_a), ACROSS)
+    outer_a = over_shot(after(inner_a, mid), OUTWARD)
+    outer_b = over_shot(after(inner_b, near, outer_mid), OUTWARD)
+    outer_c = over_shot(inner_c, OUTWARD)
 
     left = kernel_call(stack_kernel, jax.ShapeDtypeStruct((4, 2, shots, 512), jnp.bfloat16), 1, 4)(chip, x, y, diag)
     block_flops = 8 * shots * 256 * (cols // 2)
     acc_shape = jax.ShapeDtypeStruct((2 * CHUNKS, shots, width), jnp.float32)
-    acc = kernel_call(most_kernel, acc_shape, 3 * block_flops, 7)(
-        left, rcv_side, near, mid_a, outer_mid_a, mid_b, outer_mid_b
-    )
+    acc = kernel_call(most_kernel, acc_shape, 3 * block_flops, 5)(left, rcv_side, near, mid, outer_mid)
 
     out_shape = jax.ShapeDtypeStruct((shots, cols), jnp.bfloat16)
     scratch = [pltpu.VMEM((2 * CHUNKS, shots, width), jnp.bfloat16), pltpu.SemaphoreType.DMA((4 * CHUNKS,))]

time: 58.6 us -> 58.9 us (level)
  starting transfers between devices: 28.6 us -> 37.8 us
  waiting for transfers between devices: 20.3 us -> 11.2 us
    ppermute x9 -> x8, starting transfers between devices: 23.2 us -> 32.6 us  [over_shot(): return lax.ppermute(value, 'shot', pairs)]
    ppermute x4, waiting for transfers between devices: 9.42 us -> 0.01 us  [flipped(): return lax.ppermute(value, 'rcv', [(i, i ^ bit) for i in range(8)])]
    ppermute x9 -> x8, waiting for transfers between devices: 10.6 us -> 11.2 us  [over_shot(): return lax.ppermute(value, 'shot', pairs)]
    slice x2 -> x1, local copies, waits for them, and re-layouts: 1.12 us -> 1.27 us  [cut(): value[:, low:high]]
  transfers between devices with their start and end apart: 15 -> 13, of which waited for: 8 -> 5; matrix products, arithmetic and copies ran while one was open for 4% -> 4% of each run, Pallas kernels for 10% -> 10%
where the time goes in v5:
time: 58.9 us; the launch traced here: 58.6 us
  starting transfers between devices  37.8 us (64%)
  waiting for transfers between devices  11.2 us (19%)
  Pallas kernels  7 us (12%)
  local copies, waits for them, and re-layouts  2.28 us (4%)
    ppermute x8, starting transfers between devices, over_shot(): return lax.ppermute(value, 'shot', pairs)  32.6 us
    ppermute x8, waiting for transfers between devices, over_shot(): return lax.ppermute(value, 'shot', pairs)  11.2 us
    ppermute x4, starting transfers between devices, flipped(): return lax.ppermute(value, 'rcv', [(i, i ^ bit) for i in range(8)])  4.72 us
    pallas_call x1, Pallas kernels, line_on_device(): kernel_call(most_kernel, acc_shape, 3 * block_flops, 5)  3.61 us
    pallas_call x1, Pallas kernels, line_on_device(): kernel_call(first_kernel, out_shape, block_flops * 2 // 3, 6, out_specs=i...  1.54 us
    slice x1, local copies, waits for them, and re-layouts, cut(): value[:, low:high]  1.27 us
    pallas_call x1, Pallas kernels, line_on_device(): pl.pallas_call(last_kernel, out_shape=out_shape, in_specs=[pl.BlockSpec(m...  1.26 us
  transfers between devices with their start and end apart: 13, of which 5 were waited for; matrix products, arithmetic and copies ran while one was open for 4% of the time, Pallas kernels for 10%

profile of v5, /device:TPU:0, one launch (start us, length us, event | category | flops | bytes accessed | tf_op | source)
XLA Modules:
  0.0 58.6 jit_solution(4443456579816742546)
XLA Ops:
  0.0 0.5 collective-permute-start.4
  0.5 0.1 collective-permute-start
  0.5 4.1 %collective-permute-start.3 = (bf16[256,1536]{1,0:T(8,128)(2,1)}, bf16[256,1536]{1,0:T(8,128)(2,1)S(1)}, u32[]{:S(2)}, u32[]{:S(2)}) collective-permute-start(bf16[256,1536]{1,0:T(8,128)(2,1)} %own.1), channel_id=1, source_target_pairs={{0,8},{8,0},{16,24},{24,16},{1,9},{9,1},{17,25},{25,17},{2,10},{10... | collective-permute-start | bytes 2359304 | tf_op jit(solution)/shard_map/ppermute | solution.py:66
  4.6 1.0 %constant_dynamic-update-slice_fusion.1 = bf16[4,512,128]{2,1,0:T(8,128)(2,1)S(1)} fusion(bf16[2,512,128]{2,1,0:T(8,128)(2,1)} %param.2), kind=kLoop, calls=%fused_computation.4 | loop fusion | bytes 524288
  5.6 0.0 collective-permute-done
  5.6 1.6 %collective-permute-start.1 = (bf16[4,512,128]{2,1,0:T(8,128)(2,1)S(1)}, bf16[4,512,128]{2,1,0:T(8,128)(2,1)S(1)}, u32[]{:S(2)}, u32[]{:S(2)}) collective-permute-start(bf16[4,512,128]{2,1,0:T(8,128)(2,1)S(1)} %constant_dynamic-update-slice_fusion.own), channel_id=1, source_target_pairs={{0,2},{1,3},{2,0},{3,1},{4,6},{5,7},{6,4},{7,5},{8,10},{9,11},{10,... | collective-permute-start | bytes 1572872 | tf_op jit(solution)/shard_map/ppermute | solution.py:62
  7.2 1.5 %collective-permute-start.2 = (bf16[4,512,128]{2,1,0:T(8,128)(2,1)S(1)}, bf16[4,512,128]{2,1,0:T(8,128)(2,1)S(1)}, u32[]{:S(2)}, u32[]{:S(2)}) collective-permute-start(bf16[4,512,128]{2,1,0:T(8,128)(2,1)S(1)} %constant_dynamic-update-slice_fusion.own), channel_id=1, source_target_pairs={{0,4},{1,5},{2,6},{3,7},{4,0},{5,1},{6,2},{7,3},{8,12},{9,13},{10,... | collective-permute-start | bytes 1572872 | tf_op jit(solution)/shard_map/ppermute | solution.py:62
  8.7 0.0 collective-permute-done.4.from_inner
  8.7 1.3 %collective-permute-start.6 = (bf16[256,1536]{1,0:T(8,128)(2,1)S(1)}, bf16[256,1536]{1,0:T(8,128)(2,1)S(1)}, u32[]{:S(2)}, u32[]{:S(2)}) collective-permute-start(bf16[256,1536]{1,0:T(8,128)(2,1)S(1)} %collective-permute-done.4.from_inner), channel_id=1, source_target_pairs={{8,0},{16,24},{9,1},{17,25},{10,2},{18,26},{11,3},{19,27},{12,4},{... | collective-permute-start | bytes 2359304 | tf_op jit(solution)/shard_map/ppermute | solution.py:66
  10.0 1.3 %fusion = (bf16[256,256]{1,0:T(8,128)(2,1)S(1)}, bf16[256,256]{1,0:T(8,128)(2,1)S(1)}, bf16[256,256]{1,0:T(8,128)(2,1)S(1)}, bf16[256,256]{1,0:T(8,128)(2,1)S(1)...) fusion(bf16[256,1536]{1,0:T(8,128)(2,1)} %own.1), kind=kLoop, calls=%fused_computation.5 | loop fusion | bytes 1572864 | tf_op jit(solution)/shard_map/slice | solution.py:170
  11.3 16.8 %collective-permute-start.7 = (bf16[256,512]{1,0:T(8,128)(2,1)S(1)}, bf16[256,512]{1,0:T(8,128)(2,1)S(1)}, u32[]{:S(2)}, u32[]{:S(2)}) collective-permute-start(bf16[256,512]{1,0:T(8,128)(2,1)S(1)} %pad_maximum_fusion.1), channel_id=1, source_target_pairs={{0,16},{24,8},{1,17},{25,9},{2,18},{26,10},{3,19},{27,11},{4,20},{... | collective-permute-start | bytes 786440 | tf_op jit(solution)/shard_map/ppermute | solution.py:66
  28.1 0.0 collective-permute-done.1.x
  28.1 0.0 collective-permute-done.2.y
  28.1 0.0 collective-permute-done.3.near
  28.1 1.6 %collective-permute-start.5 = (bf16[4,512,128]{2,1,0:T(8,128)(2,1)S(1)}, bf16[4,512,128]{2,1,0:T(8,128)(2,1)S(1)}, u32[]{:S(2)}, u32[]{:S(2)}) collective-permute-start(bf16[4,512,128]{2,1,0:T(8,128)(2,1)S(1)} %collective-permute-done.1.x), channel_id=1, source_target_pairs={{0,4},{1,5},{2,6},{3,7},{4,0},{5,1},{6,2},{7,3},{8,12},{9,13},{10,... | collective-permute-start | bytes 1572872 | tf_op jit(solution)/shard_map/ppermute | solution.py:62
  29.7 1.3 %collective-permute-start.11 = (bf16[256,512]{1,0:T(8,128)(2,1)S(1)}, bf16[256,512]{1,0:T(8,128)(2,1)S(1)}, u32[]{:S(2)}, u32[]{:S(2)}) collective-permute-start(bf16[256,512]{1,0:T(8,128)(2,1)S(1)} %pad_maximum_fusion.2), channel_id=1, source_target_pairs={{0,16},{24,8},{1,17},{25,9},{2,18},{26,10},{3,19},{27,11},{4,20},{... | collective-permute-start | bytes 786440 | tf_op jit(solution)/shard_map/ppermute | solution.py:66
  31.1 0.0 copy-start
  31.1 3.7 %collective-permute-done.7.inner_a = bf16[256,512]{1,0:T(8,128)(2,1)S(1)} collective-permute-done((bf16[256,512]{1,0:T(8,128)(2,1)S(1)}, bf16[256,512]{1,0:T(8,128)(2,1)S(1)}, u32[]{:S(2)}, u32[]{:S(2)}) %collective-permute-start.7) | collective-permute-done | bytes 262176 | tf_op jit(solution)/shard_map/ppermute | solution.py:66
  34.8 5.3 %collective-permute-start.8 = (bf16[256,512]{1,0:T(8,128)(2,1)S(1)}, bf16[256,512]{1,0:T(8,128)(2,1)S(1)}, u32[]{:S(2)}, u32[]{:S(2)}) collective-permute-start(bf16[256,512]{1,0:T(8,128)(2,1)S(1)} %pad_maximum_fusion), channel_id=1, source_target_pairs={{0,16},{24,8},{1,17},{25,9},{2,18},{26,10},{3,19},{27,11},{4,20},{... | collective-permute-start | bytes 786440 | tf_op jit(solution)/shard_map/ppermute | solution.py:66
  40.1 1.3 %collective-permute-start.10 = (bf16[256,512]{1,0:T(8,128)(2,1)S(1)}, bf16[256,512]{1,0:T(8,128)(2,1)S(1)}, u32[]{:S(2)}, u32[]{:S(2)}) collective-permute-start(bf16[256,512]{1,0:T(8,128)(2,1)S(1)} %collective-permute-done.7.inner_a), channel_id=1, source_target_pairs={{8,0},{16,24},{9,1},{17,25},{10,2},{18,26},{11,3},{19,27},{12,4},{... | collective-permute-start | bytes 786440 | tf_op jit(solution)/shard_map/ppermute | solution.py:66
  41.4 0.0 collective-permute-done.11.inner_b
  41.4 0.0 collective-permute-done.6.from_outer
  41.4 1.3 %collective-permute-start.12 = (bf16[256,512]{1,0:T(8,128)(2,1)S(1)}, bf16[256,512]{1,0:T(8,128)(2,1)S(1)}, u32[]{:S(2)}, u32[]{:S(2)}) collective-permute-start(bf16[256,512]{1,0:T(8,128)(2,1)S(1)} %collective-permute-done.11.inner_b), channel_id=1, source_target_pairs={{8,0},{16,24},{9,1},{17,25},{10,2},{18,26},{11,3},{19,27},{12,4},{... | collective-permute-start | bytes 786440 | tf_op jit(solution)/shard_map/ppermute | solution.py:66
  42.7 1.2 %collective-permute-done.8.from_inner = bf16[256,512]{1,0:T(8,128)(2,1)S(1)} collective-permute-done((bf16[256,512]{1,0:T(8,128)(2,1)S(1)}, bf16[256,512]{1,0:T(8,128)(2,1)S(1)}, u32[]{:S(2)}, u32[]{:S(2)}) %collective-permute-start.8) | collective-permute-done | bytes 262176 | tf_op jit(solution)/shard_map/ppermute | solution.py:66
  44.0 1.3 %collective-permute-start.9 = (bf16[256,512]{1,0:T(8,128)(2,1)S(1)}, bf16[256,512]{1,0:T(8,128)(2,1)S(1)}, u32[]{:S(2)}, u32[]{:S(2)}) collective-permute-start(bf16[256,512]{1,0:T(8,128)(2,1)S(1)} %collective-permute-done.8.from_inner), channel_id=1, source_target_pairs={{8,0},{16,24},{9,1},{17,25},{10,2},{18,26},{11,3},{19,27},{12,4},{... | collective-permute-start | bytes 786440 | tf_op jit(solution)/shard_map/ppermute | solution.py:66
  45.3 0.6 %shard_map.28.left = bf16[4,2,512,512]{3,2,1,0:T(8,128)(2,1)S(1)} custom-call(bf16[4,512,128]{2,1,0:T(8,128)(2,1)S(1)} %constant_dynamic-update-slice_fusion.own, bf16[4,512,128]{2,1,0:T(8,128)(2,1)S(1)} %collective-permute-done.1.x, bf16[4,512,128]{2,1,0:T(8,128)(2,1)S(1)} %collective-permute-done.2.y, bf16[4,512,128]{2,1,0:T(8,128)(2,1)S(1)} %collective-permute-done.5.d), custom_call_target="tpu_custom_call" | custom-call | flops 1 | bytes 4194304 | tf_op jit(solution)/shard_map/pallas_call | solution.py:196
  45.9 3.6 %shard_map.29.acc = f32[6,512,256]{2,1,0:T(8,128)S(1)} custom-call(bf16[4,2,512,512]{3,2,1,0:T(8,128)(2,1)S(1)} %shard_map.28.left, bf16[256,1536]{1,0:T(8,128)(2,1)S(1)} %copy-done, bf16[256,1536]{1,0:T(8,128)(2,1)S(1)} %collective-permute-done.3.near, bf16[256,1536]{1,0:T(8,128)(2,1)S(1)} %collective-permute-done.4.from_inner, ...), custom_call_target="tpu_custom_call" | custom-call | flops 2415919104 | bytes 4194304 | tf_op jit(solution)/shard_map/pallas_call | solution.py:199
  49.5 1.7 %collective-permute-done.10.outer_a = bf16[256,512]{1,0:T(8,128)(2,1)S(1)} collective-permute-done((bf16[256,512]{1,0:T(8,128)(2,1)S(1)}, bf16[256,512]{1,0:T(8,128)(2,1)S(1)}, u32[]{:S(2)}, u32[]{:S(2)}) %collective-permute-start.10) | collective-permute-done | bytes 262176 | tf_op jit(solution)/shard_map/ppermute | solution.py:66
  51.3 3.2 %collective-permute-done.12.outer_b = bf16[256,512]{1,0:T(8,128)(2,1)S(1)} collective-permute-done((bf16[256,512]{1,0:T(8,128)(2,1)S(1)}, bf16[256,512]{1,0:T(8,128)(2,1)S(1)}, u32[]{:S(2)}, u32[]{:S(2)}) %collective-permute-start.12) | collective-permute-done | bytes 262176 | tf_op jit(solution)/shard_map/ppermute | solution.py:66
  54.5 1.5 %shard_map.30._ = bf16[512,1536]{1,0:T(8,128)(2,1)} custom-call(bf16[4,2,512,512]{3,2,1,0:T(8,128)(2,1)S(1)} %shard_map.28.left, f32[6,512,256]{2,1,0:T(8,128)S(1)} %shard_map.29.acc, bf16[256,512]{1,0:T(8,128)(2,1)S(1)} %collective-permute-done.7.inner_a, bf16[256,512]{1,0:T(8,128)(2,1)S(1)} %collective-permute-done.10.outer_a, ...), custom_call_target="tpu_custom_call" | custom-call | flops 536870912 | bytes 4194304 | tf_op jit(solution)/shard_map/pallas_call | solution.py:204
  56.0 1.3 %collective-permute-done.9.from_outer = bf16[256,512]{1,0:T(8,128)(2,1)S(1)} collective-permute-done((bf16[256,512]{1,0:T(8,128)(2,1)S(1)}, bf16[256,512]{1,0:T(8,128)(2,1)S(1)}, u32[]{:S(2)}, u32[]{:S(2)}) %collective-permute-start.9) | collective-permute-done | bytes 262176 | tf_op jit(solution)/shard_map/ppermute | solution.py:66
  57.3 1.3 %shard_map.31 = bf16[512,1536]{1,0:T(8,128)(2,1)} custom-call(bf16[4,2,512,512]{3,2,1,0:T(8,128)(2,1)S(1)} %shard_map.28.left, f32[6,512,256]{2,1,0:T(8,128)S(1)} %shard_map.29.acc, bf16[256,512]{1,0:T(8,128)(2,1)S(1)} %collective-permute-done.8.from_inner, bf16[256,512]{1,0:T(8,128)(2,1)S(1)} %collective-permute-done.9.from_outer, ...), custom_call_target="tpu_custom_call", output_to_operand_aliasing={{}: (4, {})} | custom-call | flops 268435456 | bytes 1048576 | tf_op jit(solution)/shard_map/pallas_call | solution.py:207
  (6 shorter events, 0.1 us)
Async XLA Ops:
  0.0 8.7 %collective-permute-start.4 = (bf16[256,1536]{1,0:T(8,128)(2,1)}, bf16[256,1536]{1,0:T(8,128)(2,1)S(1)}, u32[]{:S(2)}, u32[]{:S(2)}) collective-permute-start(bf16[256,1536]{1,0:T(8,128)(2,1)} %own.1), channel_id=1, source_target_pairs={{0,1},{1,0},{2,3},{3,2},{4,5},{5,4},{6,7},{7,6},{8,16},{9,17},{10,... | collective-permute-start | bytes 2359304 | tf_op jit(solution)/shard_map/ppermute | solution.py:180
  0.5 5.1 %collective-permute-start = (bf16[2,512,128]{2,1,0:T(8,128)(2,1)}, bf16[2,512,128]{2,1,0:T(8,128)(2,1)S(1)}, u32[]{:S(2)}, u32[]{:S(2)}) collective-permute-start(bf16[2,512,128]{2,1,0:T(8,128)(2,1)} %param.2), channel_id=1, source_target_pairs={{0,1},{1,0},{2,3},{3,2},{4,5},{5,4},{6,7},{7,6},{8,9},{9,8},{10,11... | collective-permute-start | bytes 786440 | tf_op jit(solution)/shard_map/ppermute | solution.py:62
  0.5 27.6 %collective-permute-start.3 = (bf16[256,1536]{1,0:T(8,128)(2,1)}, bf16[256,1536]{1,0:T(8,128)(2,1)S(1)}, u32[]{:S(2)}, u32[]{:S(2)}) collective-permute-start(bf16[256,1536]{1,0:T(8,128)(2,1)} %own.1), channel_id=1, source_target_pairs={{0,8},{8,0},{16,24},{24,16},{1,9},{9,1},{17,25},{25,17},{2,10},{10... | collective-permute-start | bytes 2359304 | tf_op jit(solution)/shard_map/ppermute | solution.py:66
  5.6 22.5 %collective-permute-start.1 = (bf16[4,512,128]{2,1,0:T(8,128)(2,1)S(1)}, bf16[4,512,128]{2,1,0:T(8,128)(2,1)S(1)}, u32[]{:S(2)}, u32[]{:S(2)}) collective-permute-start(bf16[4,512,128]{2,1,0:T(8,128)(2,1)S(1)} %constant_dynamic-update-slice_fusion.own), channel_id=1, source_target_pairs={{0,2},{1,3},{2,0},{3,1},{4,6},{5,7},{6,4},{7,5},{8,10},{9,11},{10,... | collective-permute-start | bytes 1572872 | tf_op jit(solution)/shard_map/ppermute | solution.py:62
  7.2 20.9 %collective-permute-start.2 = (bf16[4,512,128]{2,1,0:T(8,128)(2,1)S(1)}, bf16[4,512,128]{2,1,0:T(8,128)(2,1)S(1)}, u32[]{:S(2)}, u32[]{:S(2)}) collective-permute-start(bf16[4,512,128]{2,1,0:T(8,128)(2,1)S(1)} %constant_dynamic-update-slice_fusion.own), channel_id=1, source_target_pairs={{0,4},{1,5},{2,6},{3,7},{4,0},{5,1},{6,2},{7,3},{8,12},{9,13},{10,... | collective-permute-start | bytes 1572872 | tf_op jit(solution)/shard_map/ppermute | solution.py:62
  8.7 32.7 %collective-permute-start.6 = (bf16[256,1536]{1,0:T(8,128)(2,1)S(1)}, bf16[256,1536]{1,0:T(8,128)(2,1)S(1)}, u32[]{:S(2)}, u32[]{:S(2)}) collective-permute-start(bf16[256,1536]{1,0:T(8,128)(2,1)S(1)} %collective-permute-done.4.from_inner), channel_id=1, source_target_pairs={{8,0},{16,24},{9,1},{17,25},{10,2},{18,26},{11,3},{19,27},{12,4},{... | collective-permute-start | bytes 2359304 | tf_op jit(solution)/shard_map/ppermute | solution.py:66
  11.3 23.5 %collective-permute-start.7 = (bf16[256,512]{1,0:T(8,128)(2,1)S(1)}, bf16[256,512]{1,0:T(8,128)(2,1)S(1)}, u32[]{:S(2)}, u32[]{:S(2)}) collective-permute-start(bf16[256,512]{1,0:T(8,128)(2,1)S(1)} %pad_maximum_fusion.1), channel_id=1, source_target_pairs={{0,16},{24,8},{1,17},{25,9},{2,18},{26,10},{3,19},{27,11},{4,20},{... | collective-permute-start | bytes 786440 | tf_op jit(solution)/shard_map/ppermute | solution.py:66
  28.1 17.2 %collective-permute-start.5 = (bf16[4,512,128]{2,1,0:T(8,128)(2,1)S(1)}, bf16[4,512,128]{2,1,0:T(8,128)(2,1)S(1)}, u32[]{:S(2)}, u32[]{:S(2)}) collective-permute-start(bf16[4,512,128]{2,1,0:T(8,128)(2,1)S(1)} %collective-permute-done.1.x), channel_id=1, source_target_pairs={{0,4},{1,5},{2,6},{3,7},{4,0},{5,1},{6,2},{7,3},{8,12},{9,13},{10,... | collective-permute-start | bytes 1572872 | tf_op jit(solution)/shard_map/ppermute | solution.py:62
  29.7 11.7 %collective-permute-start.11 = (bf16[256,512]{1,0:T(8,128)(2,1)S(1)}, bf16[256,512]{1,0:T(8,128)(2,1)S(1)}, u32[]{:S(2)}, u32[]{:S(2)}) collective-permute-start(bf16[256,512]{1,0:T(8,128)(2,1)S(1)} %pad_maximum_fusion.2), channel_id=1, source_target_pairs={{0,16},{24,8},{1,17},{25,9},{2,18},{26,10},{3,19},{27,11},{4,20},{... | collective-permute-start | bytes 786440 | tf_op jit(solution)/shard_map/ppermute | solution.py:66
  31.1 14.8 %copy-start = (bf16[256,1536]{1,0:T(8,128)(2,1)S(1)}, bf16[256,1536]{1,0:T(8,128)(2,1)}, u32[]{:S(2)}) copy-start(bf16[256,1536]{1,0:T(8,128)(2,1)} %own.1) | copy-start | bytes 2359300
  34.8 9.2 %collective-permute-start.8 = (bf16[256,512]{1,0:T(8,128)(2,1)S(1)}, bf16[256,512]{1,0:T(8,128)(2,1)S(1)}, u32[]{:S(2)}, u32[]{:S(2)}) collective-permute-start(bf16[256,512]{1,0:T(8,128)(2,1)S(1)} %pad_maximum_fusion), channel_id=1, source_target_pairs={{0,16},{24,8},{1,17},{25,9},{2,18},{26,10},{3,19},{27,11},{4,20},{... | collective-permute-start | bytes 786440 | tf_op jit(solution)/shard_map/ppermute | solution.py:66
  40.1 11.1 %collective-permute-start.10 = (bf16[256,512]{1,0:T(8,128)(2,1)S(1)}, bf16[256,512]{1,0:T(8,128)(2,1)S(1)}, u32[]{:S(2)}, u32[]{:S(2)}) collective-permute-start(bf16[256,512]{1,0:T(8,128)(2,1)S(1)} %collective-permute-done.7.inner_a), channel_id=1, source_target_pairs={{8,0},{16,24},{9,1},{17,25},{10,2},{18,26},{11,3},{19,27},{12,4},{... | collective-permute-start | bytes 786440 | tf_op jit(solution)/shard_map/ppermute | solution.py:66
  41.4 13.1 %collective-permute-start.12 = (bf16[256,512]{1,0:T(8,128)(2,1)S(1)}, bf16[256,512]{1,0:T(8,128)(2,1)S(1)}, u32[]{:S(2)}, u32[]{:S(2)}) collective-permute-start(bf16[256,512]{1,0:T(8,128)(2,1)S(1)} %collective-permute-done.11.inner_b), channel_id=1, source_target_pairs={{8,0},{16,24},{9,1},{17,25},{10,2},{18,26},{11,3},{19,27},{12,4},{... | collective-permute-start | bytes 786440 | tf_op jit(solution)/shard_map/ppermute | solution.py:66
  44.0 13.3 %collective-permute-start.9 = (bf16[256,512]{1,0:T(8,128)(2,1)S(1)}, bf16[256,512]{1,0:T(8,128)(2,1)S(1)}, u32[]{:S(2)}, u32[]{:S(2)}) collective-permute-start(bf16[256,512]{1,0:T(8,128)(2,1)S(1)} %collective-permute-done.8.from_inner), channel_id=1, source_target_pairs={{8,0},{16,24},{9,1},{17,25},{10,2},{18,26},{11,3},{19,27},{12,4},{... | collective-permute-start | bytes 786440 | tf_op jit(solution)/shard_map/ppermute | solution.py:66

commit v6 on v4

--- a/solution.py
+++ b/solution.py
@@ -186,11 +186,11 @@
     diag = flipped(after(x, mid_a, mid_b), 4)
 
     outer_mid_a = over_shot(mid_a, OUTWARD)
-    outer_mid_b = over_shot(after(mid_b, near, x, y, core), OUTWARD)
+    outer_mid_b = over_shot(after(mid_b, near), OUTWARD)
     across = cut(rcv_side, (1, 1, 1))
     inner_a = over_shot(after(across[0], near, mid_b, y), ACROSS)
-    inner_b = over_shot(after(across[1], mid_b, near, core), ACROSS)
-    inner_c = over_shot(after(across[2], near, core), ACROSS)
+    inner_b = over_shot(after(across[1], mid_b, near, y), ACROSS)
+    inner_c = over_shot(after(across[2], mid_b, near, y), ACROSS)
     outer_a = over_shot(inner_a, OUTWARD)
     outer_b = over_shot(inner_b, OUTWARD)
     outer_c = over_shot(after(inner_c, diag, mid_a, outer_mid_a, outer_mid_b), OUTWARD)

time: 58.6 us -> 58.6 us (level)
  no operation moved by 1% of the time
where the time goes in v6:
time: 58.6 us; the launch traced here: 58.3 us
  starting transfers between devices  28.6 us (49%)
  waiting for transfers between devices  20.3 us (35%)
  Pallas kernels  7.04 us (12%)
  local copies, waits for them, and re-layouts  2.12 us (4%)
    ppermute x9, starting transfers between devices, over_shot(): return lax.ppermute(value, 'shot', pairs)  23.2 us
    ppermute x9, waiting for transfers between devices, over_shot(): return lax.ppermute(value, 'shot', pairs)  10.6 us
    ppermute x4, waiting for transfers between devices, flipped(): return lax.ppermute(value, 'rcv', [(i, i ^ bit) for i in range(8)])  9.42 us
    ppermute x4, starting transfers between devices, flipped(): return lax.ppermute(value, 'rcv', [(i, i ^ bit) for i in range(8)])  5.11 us
    pallas_call x1, Pallas kernels, line_on_device(): kernel_call(most_kernel, acc_shape, 3 * block_flops, 7)  3.64 us
    pallas_call x1, Pallas kernels, line_on_device(): kernel_call(first_kernel, out_shape, block_flops * 2 // 3, 6, out_specs=i...  1.54 us
    pallas_call x1, Pallas kernels, line_on_device(): pl.pallas_call(last_kernel, out_shape=out_shape, in_specs=[pl.BlockSpec(m...  1.26 us
  transfers between devices with their start and end apart: 15, of which 8 were waited for; matrix products, arithmetic and copies ran while one was open for 4% of the time, Pallas kernels for 10%

profile of v6, /device:TPU:0, one launch (start us, length us, event | category | flops | bytes accessed | tf_op | source)
XLA Modules:
  0.0 58.3 jit_solution(11192490752048341579)
XLA Ops:
  0.0 0.5 collective-permute-start
  0.5 2.6 %collective-permute-start.6 = (bf16[256,1536]{1,0:T(8,128)(2,1)}, bf16[256,1536]{1,0:T(8,128)(2,1)S(1)}, u32[]{:S(2)}, u32[]{:S(2)}) collective-permute-start(bf16[256,1536]{1,0:T(8,128)(2,1)} %own.1), channel_id=1, source_target_pairs={{0,8},{8,0},{16,24},{24,16},{1,9},{9,1},{17,25},{25,17},{2,10},{10... | collective-permute-start | bytes 2359304 | tf_op jit(solution)/shard_map/ppermute | solution.py:66
  3.1 1.1 %fusion.1 = (bf16[256,512]{1,0:T(8,128)(2,1)S(1)}, bf16[256,512]{1,0:T(8,128)(2,1)S(1)}) fusion(bf16[256,1536]{1,0:T(8,128)(2,1)} %own.1), kind=kLoop, calls=%fused_computation.7 | loop fusion | bytes 1048576 | tf_op jit(solution)/shard_map/slice | solution.py:171
  4.2 0.1 pad_maximum_fusion
  4.2 0.2 collective-permute-start.3
  4.5 1.0 %constant_dynamic-update-slice_fusion.1 = bf16[4,512,128]{2,1,0:T(8,128)(2,1)S(1)} fusion(bf16[2,512,128]{2,1,0:T(8,128)(2,1)} %param.2), kind=kLoop, calls=%fused_computation.5 | loop fusion | bytes 524288
  5.4 0.0 collective-permute-done
  5.5 1.6 %collective-permute-start.1 = (bf16[4,512,128]{2,1,0:T(8,128)(2,1)S(1)}, bf16[4,512,128]{2,1,0:T(8,128)(2,1)S(1)}, u32[]{:S(2)}, u32[]{:S(2)}) collective-permute-start(bf16[4,512,128]{2,1,0:T(8,128)(2,1)S(1)} %constant_dynamic-update-slice_fusion.own), channel_id=1, source_target_pairs={{0,2},{1,3},{2,0},{3,1},{4,6},{5,7},{6,4},{7,5},{8,10},{9,11},{10,... | collective-permute-start | bytes 1572872 | tf_op jit(solution)/shard_map/ppermute | solution.py:62
  7.0 0.1 fusion
  7.1 1.6 %collective-permute-start.2 = (bf16[4,512,128]{2,1,0:T(8,128)(2,1)S(1)}, bf16[4,512,128]{2,1,0:T(8,128)(2,1)S(1)}, u32[]{:S(2)}, u32[]{:S(2)}) collective-permute-start(bf16[4,512,128]{2,1,0:T(8,128)(2,1)S(1)} %constant_dynamic-update-slice_fusion.own), channel_id=1, source_target_pairs={{0,4},{1,5},{2,6},{3,7},{4,0},{5,1},{6,2},{7,3},{8,12},{9,13},{10,... | collective-permute-start | bytes 1572872 | tf_op jit(solution)/shard_map/ppermute | solution.py:62
  8.7 0.1 collective-permute-start.4
  8.8 1.3 %collective-permute-start.7 = (bf16[256,1024]{1,0:T(8,128)(2,1)S(1)}, bf16[256,1024]{1,0:T(8,128)(2,1)S(1)}, u32[]{:S(2)}, u32[]{:S(2)}) collective-permute-start(bf16[256,1024]{1,0:T(8,128)(2,1)S(1)} %collective-permute-done.3.inner_a), channel_id=1, source_target_pairs={{8,0},{16,24},{9,1},{17,25},{10,2},{18,26},{11,3},{19,27},{12,4},{... | collective-permute-start | bytes 1572872 | tf_op jit(solution)/shard_map/ppermute | solution.py:66
  10.1 0.2 collective-permute-done.4.inner_b
  10.3 9.4 %collective-permute-done.1.x = bf16[4,512,128]{2,1,0:T(8,128)(2,1)S(1)} collective-permute-done((bf16[4,512,128]{2,1,0:T(8,128)(2,1)S(1)}, bf16[4,512,128]{2,1,0:T(8,128)(2,1)S(1)}, u32[]{:S(2)}, u32[]{:S(2)}) %collective-permute-start.1) | collective-permute-done | bytes 524320 | tf_op jit(solution)/shard_map/ppermute | solution.py:62
  19.7 1.5 %collective-permute-start.5 = (bf16[4,512,128]{2,1,0:T(8,128)(2,1)S(1)}, bf16[4,512,128]{2,1,0:T(8,128)(2,1)S(1)}, u32[]{:S(2)}, u32[]{:S(2)}) collective-permute-start(bf16[4,512,128]{2,1,0:T(8,128)(2,1)S(1)} %collective-permute-done.1.x), channel_id=1, source_target_pairs={{0,4},{1,5},{2,6},{3,7},{4,0},{5,1},{6,2},{7,3},{8,12},{9,13},{10,... | collective-permute-start | bytes 1572872 | tf_op jit(solution)/shard_map/ppermute | solution.py:62
  21.3 0.2 collective-permute-done.6.near
  21.5 8.6 %collective-permute-start.11 = (bf16[256,512]{1,0:T(8,128)(2,1)S(1)}, bf16[256,512]{1,0:T(8,128)(2,1)S(1)}, u32[]{:S(2)}, u32[]{:S(2)}) collective-permute-start(bf16[256,512]{1,0:T(8,128)(2,1)S(1)} %get-tuple-element.15), channel_id=1, source_target_pairs={{0,16},{24,8},{1,17},{25,9},{2,18},{26,10},{3,19},{27,11},{4,20},{... | collective-permute-start | bytes 786440 | tf_op jit(solution)/shard_map/ppermute | solution.py:66
  30.0 1.3 %collective-permute-start.13 = (bf16[256,512]{1,0:T(8,128)(2,1)S(1)}, bf16[256,512]{1,0:T(8,128)(2,1)S(1)}, u32[]{:S(2)}, u32[]{:S(2)}) collective-permute-start(bf16[256,512]{1,0:T(8,128)(2,1)S(1)} %get-tuple-element.16), channel_id=1, source_target_pairs={{0,16},{24,8},{1,17},{25,9},{2,18},{26,10},{3,19},{27,11},{4,20},{... | collective-permute-start | bytes 786440 | tf_op jit(solution)/shard_map/ppermute | solution.py:66
  31.3 1.3 %collective-permute-start.8 = (bf16[256,512]{1,0:T(8,128)(2,1)S(1)}, bf16[256,512]{1,0:T(8,128)(2,1)S(1)}, u32[]{:S(2)}, u32[]{:S(2)}) collective-permute-start(bf16[256,512]{1,0:T(8,128)(2,1)S(1)} %collective-permute-done.4.inner_b), channel_id=1, source_target_pairs={{8,0},{16,24},{9,1},{17,25},{10,2},{18,26},{11,3},{19,27},{12,4},{... | collective-permute-start | bytes 786440 | tf_op jit(solution)/shard_map/ppermute | solution.py:66
  32.6 0.1 collective-permute-done.7.outer_a
  32.7 4.2 %collective-permute-start.9 = (bf16[256,512]{1,0:T(8,128)(2,1)S(1)}, bf16[256,512]{1,0:T(8,128)(2,1)S(1)}, u32[]{:S(2)}, u32[]{:S(2)}) collective-permute-start(bf16[256,512]{1,0:T(8,128)(2,1)S(1)} %pad_maximum_fusion.1), channel_id=1, source_target_pairs={{0,16},{24,8},{1,17},{25,9},{2,18},{26,10},{3,19},{27,11},{4,20},{... | collective-permute-start | bytes 786440 | tf_op jit(solution)/shard_map/ppermute | solution.py:66
  36.9 1.3 %collective-permute-start.12 = (bf16[256,512]{1,0:T(8,128)(2,1)S(1)}, bf16[256,512]{1,0:T(8,128)(2,1)S(1)}, u32[]{:S(2)}, u32[]{:S(2)}) collective-permute-start(bf16[256,512]{1,0:T(8,128)(2,1)S(1)} %collective-permute-done.11.inner_a), channel_id=1, source_target_pairs={{8,0},{16,24},{9,1},{17,25},{10,2},{18,26},{11,3},{19,27},{12,4},{... | collective-permute-start | bytes 786440 | tf_op jit(solution)/shard_map/ppermute | solution.py:66
  38.2 4.1 %collective-permute-done.13.inner_b = bf16[256,512]{1,0:T(8,128)(2,1)S(1)} collective-permute-done((bf16[256,512]{1,0:T(8,128)(2,1)S(1)}, bf16[256,512]{1,0:T(8,128)(2,1)S(1)}, u32[]{:S(2)}, u32[]{:S(2)}) %collective-permute-start.13) | collective-permute-done | bytes 262176 | tf_op jit(solution)/shard_map/ppermute | solution.py:66
  42.4 1.3 %collective-permute-start.14 = (bf16[256,512]{1,0:T(8,128)(2,1)S(1)}, bf16[256,512]{1,0:T(8,128)(2,1)S(1)}, u32[]{:S(2)}, u32[]{:S(2)}) collective-permute-start(bf16[256,512]{1,0:T(8,128)(2,1)S(1)} %collective-permute-done.13.inner_b), channel_id=1, source_target_pairs={{8,0},{16,24},{9,1},{17,25},{10,2},{18,26},{11,3},{19,27},{12,4},{... | collective-permute-start | bytes 786440 | tf_op jit(solution)/shard_map/ppermute | solution.py:66
  43.7 2.3 %collective-permute-done.9.from_inner = bf16[256,512]{1,0:T(8,128)(2,1)S(1)} collective-permute-done((bf16[256,512]{1,0:T(8,128)(2,1)S(1)}, bf16[256,512]{1,0:T(8,128)(2,1)S(1)}, u32[]{:S(2)}, u32[]{:S(2)}) %collective-permute-start.9) | collective-permute-done | bytes 262176 | tf_op jit(solution)/shard_map/ppermute | solution.py:66
  46.0 1.3 %collective-permute-start.10 = (bf16[256,512]{1,0:T(8,128)(2,1)S(1)}, bf16[256,512]{1,0:T(8,128)(2,1)S(1)}, u32[]{:S(2)}, u32[]{:S(2)}) collective-permute-start(bf16[256,512]{1,0:T(8,128)(2,1)S(1)} %collective-permute-done.9.from_inner), channel_id=1, source_target_pairs={{8,0},{16,24},{9,1},{17,25},{10,2},{18,26},{11,3},{19,27},{12,4},{... | collective-permute-start | bytes 786440 | tf_op jit(solution)/shard_map/ppermute | solution.py:66
  47.3 0.6 %shard_map.28.left = bf16[4,2,512,512]{3,2,1,0:T(8,128)(2,1)S(1)} custom-call(bf16[4,512,128]{2,1,0:T(8,128)(2,1)S(1)} %constant_dynamic-update-slice_fusion.own, bf16[4,512,128]{2,1,0:T(8,128)(2,1)S(1)} %collective-permute-done.1.x, bf16[4,512,128]{2,1,0:T(8,128)(2,1)S(1)} %collective-permute-done.2.y, bf16[4,512,128]{2,1,0:T(8,128)(2,1)S(1)} %collective-permute-done.5.d), custom_call_target="tpu_custom_call" | custom-call | flops 1 | bytes 4194304 | tf_op jit(solution)/shard_map/pallas_call | solution.py:198
  47.9 3.6 %shard_map.29.acc = f32[6,512,256]{2,1,0:T(8,128)S(1)} custom-call(bf16[4,2,512,512]{3,2,1,0:T(8,128)(2,1)S(1)} %shard_map.28.left, bf16[256,1536]{1,0:T(8,128)(2,1)S(1)} %copy-done, bf16[256,1536]{1,0:T(8,128)(2,1)S(1)} %collective-permute-done.6.near, bf16[256,1024]{1,0:T(8,128)(2,1)S(1)} %collective-permute-done.3.inner_a, ...), custom_call_target="tpu_custom_call" | custom-call | flops 2415919104 | bytes 4194304 | tf_op jit(solution)/shard_map/pallas_call | solution.py:201
  51.5 2.2 %collective-permute-done.14.outer_b = bf16[256,512]{1,0:T(8,128)(2,1)S(1)} collective-permute-done((bf16[256,512]{1,0:T(8,128)(2,1)S(1)}, bf16[256,512]{1,0:T(8,128)(2,1)S(1)}, u32[]{:S(2)}, u32[]{:S(2)}) %collective-permute-start.14) | collective-permute-done | bytes 262176 | tf_op jit(solution)/shard_map/ppermute | solution.py:66
  53.7 1.5 %shard_map.30._ = bf16[512,1536]{1,0:T(8,128)(2,1)} custom-call(bf16[4,2,512,512]{3,2,1,0:T(8,128)(2,1)S(1)} %shard_map.28.left, f32[6,512,256]{2,1,0:T(8,128)S(1)} %shard_map.29.acc, bf16[256,512]{1,0:T(8,128)(2,1)S(1)} %collective-permute-done.11.inner_a, bf16[256,512]{1,0:T(8,128)(2,1)S(1)} %collective-permute-done.12.outer_a, ...), custom_call_target="tpu_custom_call" | custom-call | flops 536870912 | bytes 4194304 | tf_op jit(solution)/shard_map/pallas_call | solution.py:208
  55.3 1.8 %collective-permute-done.10.from_outer = bf16[256,512]{1,0:T(8,128)(2,1)S(1)} collective-permute-done((bf16[256,512]{1,0:T(8,128)(2,1)S(1)}, bf16[256,512]{1,0:T(8,128)(2,1)S(1)}, u32[]{:S(2)}, u32[]{:S(2)}) %collective-permute-start.10) | collective-permute-done | bytes 262176 | tf_op jit(solution)/shard_map/ppermute | solution.py:66
  57.1 1.3 %shard_map.31 = bf16[512,1536]{1,0:T(8,128)(2,1)} custom-call(bf16[4,2,512,512]{3,2,1,0:T(8,128)(2,1)S(1)} %shard_map.28.left, f32[6,512,256]{2,1,0:T(8,128)S(1)} %shard_map.29.acc, bf16[256,512]{1,0:T(8,128)(2,1)S(1)} %collective-permute-done.9.from_inner, bf16[256,512]{1,0:T(8,128)(2,1)S(1)} %collective-permute-done.10.from_outer, ...), custom_call_target="tpu_custom_call", output_to_operand_aliasing={{}: (4, {})} | custom-call | flops 268435456 | bytes 1048576 | tf_op jit(solution)/shard_map/pallas_call | solution.py:211
  (11 shorter events, 0.1 us)
Async XLA Ops:
  0.0 7.0 %copy-start = (bf16[256,1536]{1,0:T(8,128)(2,1)S(1)}, bf16[256,1536]{1,0:T(8,128)(2,1)}, u32[]{:S(2)}) copy-start(bf16[256,1536]{1,0:T(8,128)(2,1)} %own.1) | copy-start | bytes 2359300
  0.0 5.4 %collective-permute-start = (bf16[2,512,128]{2,1,0:T(8,128)(2,1)}, bf16[2,512,128]{2,1,0:T(8,128)(2,1)S(1)}, u32[]{:S(2)}, u32[]{:S(2)}) collective-permute-start(bf16[2,512,128]{2,1,0:T(8,128)(2,1)} %param.2), channel_id=1, source_target_pairs={{0,1},{1,0},{2,3},{3,2},{4,5},{5,4},{6,7},{7,6},{8,9},{9,8},{10,11... | collective-permute-start | bytes 786440 | tf_op jit(solution)/shard_map/ppermute | solution.py:62
  0.5 21.0 %collective-permute-start.6 = (bf16[256,1536]{1,0:T(8,128)(2,1)}, bf16[256,1536]{1,0:T(8,128)(2,1)S(1)}, u32[]{:S(2)}, u32[]{:S(2)}) collective-permute-start(bf16[256,1536]{1,0:T(8,128)(2,1)} %own.1), channel_id=1, source_target_pairs={{0,8},{8,0},{16,24},{24,16},{1,9},{9,1},{17,25},{25,17},{2,10},{10... | collective-permute-start | bytes 2359304 | tf_op jit(solution)/shard_map/ppermute | solution.py:66
  4.2 4.6 %collective-permute-start.3 = (bf16[256,1024]{1,0:T(8,128)(2,1)S(1)}, bf16[256,1024]{1,0:T(8,128)(2,1)S(1)}, u32[]{:S(2)}, u32[]{:S(2)}) collective-permute-start(bf16[256,1024]{1,0:T(8,128)(2,1)S(1)} %pad_maximum_fusion), channel_id=1, source_target_pairs={{0,1},{1,0},{2,3},{3,2},{4,5},{5,4},{6,7},{7,6},{8,16},{9,17},{10,... | collective-permute-start | bytes 1572872 | tf_op jit(solution)/shard_map/ppermute | solution.py:181
  5.5 14.2 %collective-permute-start.1 = (bf16[4,512,128]{2,1,0:T(8,128)(2,1)S(1)}, bf16[4,512,128]{2,1,0:T(8,128)(2,1)S(1)}, u32[]{:S(2)}, u32[]{:S(2)}) collective-permute-start(bf16[4,512,128]{2,1,0:T(8,128)(2,1)S(1)} %constant_dynamic-update-slice_fusion.own), channel_id=1, source_target_pairs={{0,2},{1,3},{2,0},{3,1},{4,6},{5,7},{6,4},{7,5},{8,10},{9,11},{10,... | collective-permute-start | bytes 1572872 | tf_op jit(solution)/shard_map/ppermute | solution.py:62
  7.1 14.2 %collective-permute-start.2 = (bf16[4,512,128]{2,1,0:T(8,128)(2,1)S(1)}, bf16[4,512,128]{2,1,0:T(8,128)(2,1)S(1)}, u32[]{:S(2)}, u32[]{:S(2)}) collective-permute-start(bf16[4,512,128]{2,1,0:T(8,128)(2,1)S(1)} %constant_dynamic-update-slice_fusion.own), channel_id=1, source_target_pairs={{0,4},{1,5},{2,6},{3,7},{4,0},{5,1},{6,2},{7,3},{8,12},{9,13},{10,... | collective-permute-start | bytes 1572872 | tf_op jit(solution)/shard_map/ppermute | solution.py:62
  8.7 1.6 %collective-permute-start.4 = (bf16[256,512]{1,0:T(8,128)(2,1)S(1)}, bf16[256,512]{1,0:T(8,128)(2,1)S(1)}, u32[]{:S(2)}, u32[]{:S(2)}) collective-permute-start(bf16[256,512]{1,0:T(8,128)(2,1)S(1)} %pad_maximum_fusion.1), channel_id=1, source_target_pairs={{0,1},{1,0},{2,3},{3,2},{4,5},{5,4},{6,7},{7,6},{8,16},{9,17},{10,... | collective-permute-start | bytes 786440 | tf_op jit(solution)/shard_map/ppermute | solution.py:181
  8.8 23.9 %collective-permute-start.7 = (bf16[256,1024]{1,0:T(8,128)(2,1)S(1)}, bf16[256,1024]{1,0:T(8,128)(2,1)S(1)}, u32[]{:S(2)}, u32[]{:S(2)}) collective-permute-start(bf16[256,1024]{1,0:T(8,128)(2,1)S(1)} %collective-permute-done.3.inner_a), channel_id=1, source_target_pairs={{8,0},{16,24},{9,1},{17,25},{10,2},{18,26},{11,3},{19,27},{12,4},{... | collective-permute-start | bytes 1572872 | tf_op jit(solution)/shard_map/ppermute | solution.py:66
  19.7 26.3 %collective-permute-start.5 = (bf16[4,512,128]{2,1,0:T(8,128)(2,1)S(1)}, bf16[4,512,128]{2,1,0:T(8,128)(2,1)S(1)}, u32[]{:S(2)}, u32[]{:S(2)}) collective-permute-start(bf16[4,512,128]{2,1,0:T(8,128)(2,1)S(1)} %collective-permute-done.1.x), channel_id=1, source_target_pairs={{0,4},{1,5},{2,6},{3,7},{4,0},{5,1},{6,2},{7,3},{8,12},{9,13},{10,... | collective-permute-start | bytes 1572872 | tf_op jit(solution)/shard_map/ppermute | solution.py:62
  21.5 15.5 %collective-permute-start.11 = (bf16[256,512]{1,0:T(8,128)(2,1)S(1)}, bf16[256,512]{1,0:T(8,128)(2,1)S(1)}, u32[]{:S(2)}, u32[]{:S(2)}) collective-permute-start(bf16[256,512]{1,0:T(8,128)(2,1)S(1)} %get-tuple-element.15), channel_id=1, source_target_pairs={{0,16},{24,8},{1,17},{25,9},{2,18},{26,10},{3,19},{27,11},{4,20},{... | collective-permute-start | bytes 786440 | tf_op jit(solution)/shard_map/ppermute | solution.py:66
  30.0 12.3 %collective-permute-start.13 = (bf16[256,512]{1,0:T(8,128)(2,1)S(1)}, bf16[256,512]{1,0:T(8,128)(2,1)S(1)}, u32[]{:S(2)}, u32[]{:S(2)}) collective-permute-start(bf16[256,512]{1,0:T(8,128)(2,1)S(1)} %get-tuple-element.16), channel_id=1, source_target_pairs={{0,16},{24,8},{1,17},{25,9},{2,18},{26,10},{3,19},{27,11},{4,20},{... | collective-permute-start | bytes 786440 | tf_op jit(solution)/shard_map/ppermute | solution.py:66
  31.3 12.3 %collective-permute-start.8 = (bf16[256,512]{1,0:T(8,128)(2,1)S(1)}, bf16[256,512]{1,0:T(8,128)(2,1)S(1)}, u32[]{:S(2)}, u32[]{:S(2)}) collective-permute-start(bf16[256,512]{1,0:T(8,128)(2,1)S(1)} %collective-permute-done.4.inner_b), channel_id=1, source_target_pairs={{8,0},{16,24},{9,1},{17,25},{10,2},{18,26},{11,3},{19,27},{12,4},{... | collective-permute-start | bytes 786440 | tf_op jit(solution)/shard_map/ppermute | solution.py:66
  32.7 13.3 %collective-permute-start.9 = (bf16[256,512]{1,0:T(8,128)(2,1)S(1)}, bf16[256,512]{1,0:T(8,128)(2,1)S(1)}, u32[]{:S(2)}, u32[]{:S(2)}) collective-permute-start(bf16[256,512]{1,0:T(8,128)(2,1)S(1)} %pad_maximum_fusion.1), channel_id=1, source_target_pairs={{0,16},{24,8},{1,17},{25,9},{2,18},{26,10},{3,19},{27,11},{4,20},{... | collective-permute-start | bytes 786440 | tf_op jit(solution)/shard_map/ppermute | solution.py:66
  36.9 14.6 %collective-permute-start.12 = (bf16[256,512]{1,0:T(8,128)(2,1)S(1)}, bf16[256,512]{1,0:T(8,128)(2,1)S(1)}, u32[]{:S(2)}, u32[]{:S(2)}) collective-permute-start(bf16[256,512]{1,0:T(8,128)(2,1)S(1)} %collective-permute-done.11.inner_a), channel_id=1, source_target_pairs={{8,0},{16,24},{9,1},{17,25},{10,2},{18,26},{11,3},{19,27},{12,4},{... | collective-permute-start | bytes 786440 | tf_op jit(solution)/shard_map/ppermute | solution.py:66
  42.4 11.3 %collective-permute-start.14 = (bf16[256,512]{1,0:T(8,128)(2,1)S(1)}, bf16[256,512]{1,0:T(8,128)(2,1)S(1)}, u32[]{:S(2)}, u32[]{:S(2)}) collective-permute-start(bf16[256,512]{1,0:T(8,128)(2,1)S(1)} %collective-permute-done.13.inner_b), channel_id=1, source_target_pairs={{8,0},{16,24},{9,1},{17,25},{10,2},{18,26},{11,3},{19,27},{12,4},{... | collective-permute-start | bytes 786440 | tf_op jit(solution)/shard_map/ppermute | solution.py:66
  46.0 11.1 %collective-permute-start.10 = (bf16[256,512]{1,0:T(8,128)(2,1)S(1)}, bf16[256,512]{1,0:T(8,128)(2,1)S(1)}, u32[]{:S(2)}, u32[]{:S(2)}) collective-permute-start(bf16[256,512]{1,0:T(8,128)(2,1)S(1)} %collective-permute-done.9.from_inner), channel_id=1, source_target_pairs={{8,0},{16,24},{9,1},{17,25},{10,2},{18,26},{11,3},{19,27},{12,4},{... | collective-permute-start | bytes 786440 | tf_op jit(solution)/shard_map/ppermute | solution.py:66

commit v7 on v6

--- a/solution.py
+++ b/solution.py
@@ -193,7 +193,7 @@
     inner_c = over_shot(after(across[2], mid_b, near, y), ACROSS)
     outer_a = over_shot(inner_a, OUTWARD)
     outer_b = over_shot(inner_b, OUTWARD)
-    outer_c = over_shot(after(inner_c, diag, mid_a, outer_mid_a, outer_mid_b), OUTWARD)
+    outer_c = over_shot(after(inner_c, outer_mid_a, outer_mid_b), OUTWARD)
 
     left = kernel_call(stack_kernel, jax.ShapeDtypeStruct((4, 2, shots, 512), jnp.bfloat16), 1, 4)(chip, x, y, diag)
     block_flops = 8 * shots * 256 * (cols // 2)

time: 58.6 us -> 60.4 us (1.031)
  starting transfers between devices: 28.6 us -> 29.5 us
  waiting for transfers between devices: 20.3 us -> 21.2 us
    ppermute x4, waiting for transfers between devices: 9.42 us -> 7.67 us  [flipped(): return lax.ppermute(value, 'rcv', [(i, i ^ bit) for i in range(8)])]
    ppermute x9, waiting for transfers between devices: 10.6 us -> 12 us  [over_shot(): return lax.ppermute(value, 'shot', pairs)]
    ppermute x2, waiting for transfers between devices: 0.21 us -> 1.52 us  [line_on_device(): lax.ppermute(piece, ('shot', 'rcv'), SWAP_INNER)]
    ppermute x9, starting transfers between devices: 23.2 us -> 24.1 us  [over_shot(): return lax.ppermute(value, 'shot', pairs)]
where the time goes in v7:
time: 60.4 us; the launch traced here: 60.1 us
  starting transfers between devices  29.5 us (49%)
  waiting for transfers between devices  21.2 us (35%)
  Pallas kernels  7.04 us (12%)
  local copies, waits for them, and re-layouts  2.12 us (4%)
    ppermute x9, starting transfers between devices, over_shot(): return lax.ppermute(value, 'shot', pairs)  24.1 us
    ppermute x9, waiting for transfers between devices, over_shot(): return lax.ppermute(value, 'shot', pairs)  12 us
    ppermute x4, waiting for transfers between devices, flipped(): return lax.ppermute(value, 'rcv', [(i, i ^ bit) for i in range(8)])  7.67 us
    ppermute x4, starting transfers between devices, flipped(): return lax.ppermute(value, 'rcv', [(i, i ^ bit) for i in range(8)])  5.11 us
    pallas_call x1, Pallas kernels, line_on_device(): kernel_call(most_kernel, acc_shape, 3 * block_flops, 7)  3.64 us
    pallas_call x1, Pallas kernels, line_on_device(): kernel_call(first_kernel, out_shape, block_flops * 2 // 3, 6, out_specs=i...  1.54 us
    ppermute x2, waiting for transfers between devices, line_on_device(): lax.ppermute(piece, ('shot', 'rcv'), SWAP_INNER)  1.52 us
    pallas_call x1, Pallas kernels, line_on_device(): pl.pallas_call(last_kernel, out_shape=out_shape, in_specs=[pl.BlockSpec(m...  1.26 us
  transfers between devices with their start and end apart: 15, of which 8 were waited for; matrix products, arithmetic and copies ran while one was open for 4% of the time, Pallas kernels for 10%

profile of v7, /device:TPU:0, one launch (start us, length us, event | category | flops | bytes accessed | tf_op | source)
XLA Modules:
  0.0 60.1 jit_solution(8524479320298162615)
XLA Ops:
  0.0 0.5 collective-permute-start
  0.5 1.1 %fusion.1 = (bf16[256,512]{1,0:T(8,128)(2,1)S(1)}, bf16[256,512]{1,0:T(8,128)(2,1)S(1)}) fusion(bf16[256,1536]{1,0:T(8,128)(2,1)} %own.1), kind=kLoop, calls=%fused_computation.7 | loop fusion | bytes 1048576 | tf_op jit(solution)/shard_map/slice | solution.py:171
  1.5 0.1 pad_maximum_fusion
  1.6 0.2 collective-permute-start.3
  1.8 4.1 %collective-permute-start.6 = (bf16[256,1536]{1,0:T(8,128)(2,1)}, bf16[256,1536]{1,0:T(8,128)(2,1)S(1)}, u32[]{:S(2)}, u32[]{:S(2)}) collective-permute-start(bf16[256,1536]{1,0:T(8,128)(2,1)} %own.1), channel_id=1, source_target_pairs={{0,8},{8,0},{16,24},{24,16},{1,9},{9,1},{17,25},{25,17},{2,10},{10... | collective-permute-start | bytes 2359304 | tf_op jit(solution)/shard_map/ppermute | solution.py:66
  5.9 1.0 %constant_dynamic-update-slice_fusion.1 = bf16[4,512,128]{2,1,0:T(8,128)(2,1)S(1)} fusion(bf16[2,512,128]{2,1,0:T(8,128)(2,1)} %param.2), kind=kLoop, calls=%fused_computation.5 | loop fusion | bytes 524288
  6.9 0.0 collective-permute-done
  6.9 1.6 %collective-permute-start.1 = (bf16[4,512,128]{2,1,0:T(8,128)(2,1)S(1)}, bf16[4,512,128]{2,1,0:T(8,128)(2,1)S(1)}, u32[]{:S(2)}, u32[]{:S(2)}) collective-permute-start(bf16[4,512,128]{2,1,0:T(8,128)(2,1)S(1)} %constant_dynamic-update-slice_fusion.own), channel_id=1, source_target_pairs={{0,2},{1,3},{2,0},{3,1},{4,6},{5,7},{6,4},{7,5},{8,10},{9,11},{10,... | collective-permute-start | bytes 1572872 | tf_op jit(solution)/shard_map/ppermute | solution.py:62
  8.5 0.1 fusion
  8.5 1.6 %collective-permute-start.2 = (bf16[4,512,128]{2,1,0:T(8,128)(2,1)S(1)}, bf16[4,512,128]{2,1,0:T(8,128)(2,1)S(1)}, u32[]{:S(2)}, u32[]{:S(2)}) collective-permute-start(bf16[4,512,128]{2,1,0:T(8,128)(2,1)S(1)} %constant_dynamic-update-slice_fusion.own), channel_id=1, source_target_pairs={{0,4},{1,5},{2,6},{3,7},{4,0},{5,1},{6,2},{7,3},{8,12},{9,13},{10,... | collective-permute-start | bytes 1572872 | tf_op jit(solution)/shard_map/ppermute | solution.py:62
  10.1 1.3 %collective-permute-start.7 = (bf16[256,1024]{1,0:T(8,128)(2,1)S(1)}, bf16[256,1024]{1,0:T(8,128)(2,1)S(1)}, u32[]{:S(2)}, u32[]{:S(2)}) collective-permute-start(bf16[256,1024]{1,0:T(8,128)(2,1)S(1)} %collective-permute-done.3.inner_a), channel_id=1, source_target_pairs={{8,0},{16,24},{9,1},{17,25},{10,2},{18,26},{11,3},{19,27},{12,4},{... | collective-permute-start | bytes 1572872 | tf_op jit(solution)/shard_map/ppermute | solution.py:66
  11.4 0.1 collective-permute-start.4
  11.5 1.5 %collective-permute-done.4.inner_b = bf16[256,512]{1,0:T(8,128)(2,1)S(1)} collective-permute-done((bf16[256,512]{1,0:T(8,128)(2,1)S(1)}, bf16[256,512]{1,0:T(8,128)(2,1)S(1)}, u32[]{:S(2)}, u32[]{:S(2)}) %collective-permute-start.4) | collective-permute-done | bytes 262176 | tf_op jit(solution)/shard_map/ppermute | solution.py:181
  13.0 7.7 %collective-permute-done.1.x = bf16[4,512,128]{2,1,0:T(8,128)(2,1)S(1)} collective-permute-done((bf16[4,512,128]{2,1,0:T(8,128)(2,1)S(1)}, bf16[4,512,128]{2,1,0:T(8,128)(2,1)S(1)}, u32[]{:S(2)}, u32[]{:S(2)}) %collective-permute-start.1) | collective-permute-done | bytes 524320 | tf_op jit(solution)/shard_map/ppermute | solution.py:62
  20.7 1.5 %collective-permute-start.5 = (bf16[4,512,128]{2,1,0:T(8,128)(2,1)S(1)}, bf16[4,512,128]{2,1,0:T(8,128)(2,1)S(1)}, u32[]{:S(2)}, u32[]{:S(2)}) collective-permute-start(bf16[4,512,128]{2,1,0:T(8,128)(2,1)S(1)} %collective-permute-done.1.x), channel_id=1, source_target_pairs={{0,4},{1,5},{2,6},{3,7},{4,0},{5,1},{6,2},{7,3},{8,12},{9,13},{10,... | collective-permute-start | bytes 1572872 | tf_op jit(solution)/shard_map/ppermute | solution.py:62
  22.3 2.2 %collective-permute-done.6.near = bf16[256,1536]{1,0:T(8,128)(2,1)S(1)} collective-permute-done((bf16[256,1536]{1,0:T(8,128)(2,1)}, bf16[256,1536]{1,0:T(8,128)(2,1)S(1)}, u32[]{:S(2)}, u32[]{:S(2)}) %collective-permute-start.6) | collective-permute-done | bytes 786464 | tf_op jit(solution)/shard_map/ppermute | solution.py:66
  24.4 8.0 %collective-permute-start.11 = (bf16[256,512]{1,0:T(8,128)(2,1)S(1)}, bf16[256,512]{1,0:T(8,128)(2,1)S(1)}, u32[]{:S(2)}, u32[]{:S(2)}) collective-permute-start(bf16[256,512]{1,0:T(8,128)(2,1)S(1)} %get-tuple-element.15), channel_id=1, source_target_pairs={{0,16},{24,8},{1,17},{25,9},{2,18},{26,10},{3,19},{27,11},{4,20},{... | collective-permute-start | bytes 786440 | tf_op jit(solution)/shard_map/ppermute | solution.py:66
  32.4 1.3 %collective-permute-start.13 = (bf16[256,512]{1,0:T(8,128)(2,1)S(1)}, bf16[256,512]{1,0:T(8,128)(2,1)S(1)}, u32[]{:S(2)}, u32[]{:S(2)}) collective-permute-start(bf16[256,512]{1,0:T(8,128)(2,1)S(1)} %get-tuple-element.16), channel_id=1, source_target_pairs={{0,16},{24,8},{1,17},{25,9},{2,18},{26,10},{3,19},{27,11},{4,20},{... | collective-permute-start | bytes 786440 | tf_op jit(solution)/shard_map/ppermute | solution.py:66
  33.7 1.3 %collective-permute-start.8 = (bf16[256,512]{1,0:T(8,128)(2,1)S(1)}, bf16[256,512]{1,0:T(8,128)(2,1)S(1)}, u32[]{:S(2)}, u32[]{:S(2)}) collective-permute-start(bf16[256,512]{1,0:T(8,128)(2,1)S(1)} %collective-permute-done.4.inner_b), channel_id=1, source_target_pairs={{8,0},{16,24},{9,1},{17,25},{10,2},{18,26},{11,3},{19,27},{12,4},{... | collective-permute-start | bytes 786440 | tf_op jit(solution)/shard_map/ppermute | solution.py:66
  35.0 0.2 collective-permute-done.7.outer_a
  35.2 4.3 %collective-permute-start.9 = (bf16[256,512]{1,0:T(8,128)(2,1)S(1)}, bf16[256,512]{1,0:T(8,128)(2,1)S(1)}, u32[]{:S(2)}, u32[]{:S(2)}) collective-permute-start(bf16[256,512]{1,0:T(8,128)(2,1)S(1)} %pad_maximum_fusion.1), channel_id=1, source_target_pairs={{0,16},{24,8},{1,17},{25,9},{2,18},{26,10},{3,19},{27,11},{4,20},{... | collective-permute-start | bytes 786440 | tf_op jit(solution)/shard_map/ppermute | solution.py:66
  39.5 1.3 %collective-permute-start.12 = (bf16[256,512]{1,0:T(8,128)(2,1)S(1)}, bf16[256,512]{1,0:T(8,128)(2,1)S(1)}, u32[]{:S(2)}, u32[]{:S(2)}) collective-permute-start(bf16[256,512]{1,0:T(8,128)(2,1)S(1)} %collective-permute-done.11.inner_a), channel_id=1, source_target_pairs={{8,0},{16,24},{9,1},{17,25},{10,2},{18,26},{11,3},{19,27},{12,4},{... | collective-permute-start | bytes 786440 | tf_op jit(solution)/shard_map/ppermute | solution.py:66
  40.8 3.9 %collective-permute-done.13.inner_b = bf16[256,512]{1,0:T(8,128)(2,1)S(1)} collective-permute-done((bf16[256,512]{1,0:T(8,128)(2,1)S(1)}, bf16[256,512]{1,0:T(8,128)(2,1)S(1)}, u32[]{:S(2)}, u32[]{:S(2)}) %collective-permute-start.13) | collective-permute-done | bytes 262176 | tf_op jit(solution)/shard_map/ppermute | solution.py:66
  44.7 1.3 %collective-permute-start.14 = (bf16[256,512]{1,0:T(8,128)(2,1)S(1)}, bf16[256,512]{1,0:T(8,128)(2,1)S(1)}, u32[]{:S(2)}, u32[]{:S(2)}) collective-permute-start(bf16[256,512]{1,0:T(8,128)(2,1)S(1)} %collective-permute-done.13.inner_b), channel_id=1, source_target_pairs={{8,0},{16,24},{9,1},{17,25},{10,2},{18,26},{11,3},{19,27},{12,4},{... | collective-permute-start | bytes 786440 | tf_op jit(solution)/shard_map/ppermute | solution.py:66
  46.0 1.8 %collective-permute-done.9.from_inner = bf16[256,512]{1,0:T(8,128)(2,1)S(1)} collective-permute-done((bf16[256,512]{1,0:T(8,128)(2,1)S(1)}, bf16[256,512]{1,0:T(8,128)(2,1)S(1)}, u32[]{:S(2)}, u32[]{:S(2)}) %collective-permute-start.9) | collective-permute-done | bytes 262176 | tf_op jit(solution)/shard_map/ppermute | solution.py:66
  47.8 1.3 %collective-permute-start.10 = (bf16[256,512]{1,0:T(8,128)(2,1)S(1)}, bf16[256,512]{1,0:T(8,128)(2,1)S(1)}, u32[]{:S(2)}, u32[]{:S(2)}) collective-permute-start(bf16[256,512]{1,0:T(8,128)(2,1)S(1)} %collective-permute-done.9.from_inner), channel_id=1, source_target_pairs={{8,0},{16,24},{9,1},{17,25},{10,2},{18,26},{11,3},{19,27},{12,4},{... | collective-permute-start | bytes 786440 | tf_op jit(solution)/shard_map/ppermute | solution.py:66
  49.1 0.6 shard_map.28.left
  49.7 3.6 %shard_map.29.acc = f32[6,512,256]{2,1,0:T(8,128)S(1)} custom-call(bf16[4,2,512,512]{3,2,1,0:T(8,128)(2,1)S(1)} %shard_map.28.left, bf16[256,1536]{1,0:T(8,128)(2,1)S(1)} %copy-done, bf16[256,1536]{1,0:T(8,128)(2,1)S(1)} %collective-permute-done.6.near, bf16[256,1024]{1,0:T(8,128)(2,1)S(1)} %collective-permute-done.3.inner_a, ...), custom_call_target="tpu_custom_call" | custom-call | flops 2415919104 | bytes 4194304 | tf_op jit(solution)/shard_map/pallas_call | solution.py:201
  53.4 2.7 %collective-permute-done.14.outer_b = bf16[256,512]{1,0:T(8,128)(2,1)S(1)} collective-permute-done((bf16[256,512]{1,0:T(8,128)(2,1)S(1)}, bf16[256,512]{1,0:T(8,128)(2,1)S(1)}, u32[]{:S(2)}, u32[]{:S(2)}) %collective-permute-start.14) | collective-permute-done | bytes 262176 | tf_op jit(solution)/shard_map/ppermute | solution.py:66
  56.1 1.5 %shard_map.30._ = bf16[512,1536]{1,0:T(8,128)(2,1)} custom-call(bf16[4,2,512,512]{3,2,1,0:T(8,128)(2,1)S(1)} %shard_map.28.left, f32[6,512,256]{2,1,0:T(8,128)S(1)} %shard_map.29.acc, bf16[256,512]{1,0:T(8,128)(2,1)S(1)} %collective-permute-done.11.inner_a, bf16[256,512]{1,0:T(8,128)(2,1)S(1)} %collective-permute-done.12.outer_a, ...), custom_call_target="tpu_custom_call" | custom-call | flops 536870912 | bytes 4194304 | tf_op jit(solution)/shard_map/pallas_call | solution.py:208
  57.6 1.3 %collective-permute-done.10.from_outer = bf16[256,512]{1,0:T(8,128)(2,1)S(1)} collective-permute-done((bf16[256,512]{1,0:T(8,128)(2,1)S(1)}, bf16[256,512]{1,0:T(8,128)(2,1)S(1)}, u32[]{:S(2)}, u32[]{:S(2)}) %collective-permute-start.10) | collective-permute-done | bytes 262176 | tf_op jit(solution)/shard_map/ppermute | solution.py:66
  58.9 1.3 %shard_map.31 = bf16[512,1536]{1,0:T(8,128)(2,1)} custom-call(bf16[4,2,512,512]{3,2,1,0:T(8,128)(2,1)S(1)} %shard_map.28.left, f32[6,512,256]{2,1,0:T(8,128)S(1)} %shard_map.29.acc, bf16[256,512]{1,0:T(8,128)(2,1)S(1)} %collective-permute-done.9.from_inner, bf16[256,512]{1,0:T(8,128)(2,1)S(1)} %collective-permute-done.10.from_outer, ...), custom_call_target="tpu_custom_call", output_to_operand_aliasing={{}: (4, {})} | custom-call | flops 268435456 | bytes 1048576 | tf_op jit(solution)/shard_map/pallas_call | solution.py:211
  (11 shorter events, 0.1 us)
Async XLA Ops:
  0.0 8.5 %copy-start = (bf16[256,1536]{1,0:T(8,128)(2,1)S(1)}, bf16[256,1536]{1,0:T(8,128)(2,1)}, u32[]{:S(2)}) copy-start(bf16[256,1536]{1,0:T(8,128)(2,1)} %own.1) | copy-start | bytes 2359300
  0.0 6.9 %collective-permute-start = (bf16[2,512,128]{2,1,0:T(8,128)(2,1)}, bf16[2,512,128]{2,1,0:T(8,128)(2,1)S(1)}, u32[]{:S(2)}, u32[]{:S(2)}) collective-permute-start(bf16[2,512,128]{2,1,0:T(8,128)(2,1)} %param.2), channel_id=1, source_target_pairs={{0,1},{1,0},{2,3},{3,2},{4,5},{5,4},{6,7},{7,6},{8,9},{9,8},{10,11... | collective-permute-start | bytes 786440 | tf_op jit(solution)/shard_map/ppermute | solution.py:62
  1.6 8.5 %collective-permute-start.3 = (bf16[256,1024]{1,0:T(8,128)(2,1)S(1)}, bf16[256,1024]{1,0:T(8,128)(2,1)S(1)}, u32[]{:S(2)}, u32[]{:S(2)}) collective-permute-start(bf16[256,1024]{1,0:T(8,128)(2,1)S(1)} %pad_maximum_fusion), channel_id=1, source_target_pairs={{0,1},{1,0},{2,3},{3,2},{4,5},{5,4},{6,7},{7,6},{8,16},{9,17},{10,... | collective-permute-start | bytes 1572872 | tf_op jit(solution)/shard_map/ppermute | solution.py:181
  1.8 22.6 %collective-permute-start.6 = (bf16[256,1536]{1,0:T(8,128)(2,1)}, bf16[256,1536]{1,0:T(8,128)(2,1)S(1)}, u32[]{:S(2)}, u32[]{:S(2)}) collective-permute-start(bf16[256,1536]{1,0:T(8,128)(2,1)} %own.1), channel_id=1, source_target_pairs={{0,8},{8,0},{16,24},{24,16},{1,9},{9,1},{17,25},{25,17},{2,10},{10... | collective-permute-start | bytes 2359304 | tf_op jit(solution)/shard_map/ppermute | solution.py:66
  6.9 13.8 %collective-permute-start.1 = (bf16[4,512,128]{2,1,0:T(8,128)(2,1)S(1)}, bf16[4,512,128]{2,1,0:T(8,128)(2,1)S(1)}, u32[]{:S(2)}, u32[]{:S(2)}) collective-permute-start(bf16[4,512,128]{2,1,0:T(8,128)(2,1)S(1)} %constant_dynamic-update-slice_fusion.own), channel_id=1, source_target_pairs={{0,2},{1,3},{2,0},{3,1},{4,6},{5,7},{6,4},{7,5},{8,10},{9,11},{10,... | collective-permute-start | bytes 1572872 | tf_op jit(solution)/shard_map/ppermute | solution.py:62
  8.5 13.7 %collective-permute-start.2 = (bf16[4,512,128]{2,1,0:T(8,128)(2,1)S(1)}, bf16[4,512,128]{2,1,0:T(8,128)(2,1)S(1)}, u32[]{:S(2)}, u32[]{:S(2)}) collective-permute-start(bf16[4,512,128]{2,1,0:T(8,128)(2,1)S(1)} %constant_dynamic-update-slice_fusion.own), channel_id=1, source_target_pairs={{0,4},{1,5},{2,6},{3,7},{4,0},{5,1},{6,2},{7,3},{8,12},{9,13},{10,... | collective-permute-start | bytes 1572872 | tf_op jit(solution)/shard_map/ppermute | solution.py:62
  10.1 25.1 %collective-permute-start.7 = (bf16[256,1024]{1,0:T(8,128)(2,1)S(1)}, bf16[256,1024]{1,0:T(8,128)(2,1)S(1)}, u32[]{:S(2)}, u32[]{:S(2)}) collective-permute-start(bf16[256,1024]{1,0:T(8,128)(2,1)S(1)} %collective-permute-done.3.inner_a), channel_id=1, source_target_pairs={{8,0},{16,24},{9,1},{17,25},{10,2},{18,26},{11,3},{19,27},{12,4},{... | collective-permute-start | bytes 1572872 | tf_op jit(solution)/shard_map/ppermute | solution.py:66
  11.4 1.6 %collective-permute-start.4 = (bf16[256,512]{1,0:T(8,128)(2,1)S(1)}, bf16[256,512]{1,0:T(8,128)(2,1)S(1)}, u32[]{:S(2)}, u32[]{:S(2)}) collective-permute-start(bf16[256,512]{1,0:T(8,128)(2,1)S(1)} %pad_maximum_fusion.1), channel_id=1, source_target_pairs={{0,1},{1,0},{2,3},{3,2},{4,5},{5,4},{6,7},{7,6},{8,16},{9,17},{10,... | collective-permute-start | bytes 786440 | tf_op jit(solution)/shard_map/ppermute | solution.py:181
  20.7 28.4 %collective-permute-start.5 = (bf16[4,512,128]{2,1,0:T(8,128)(2,1)S(1)}, bf16[4,512,128]{2,1,0:T(8,128)(2,1)S(1)}, u32[]{:S(2)}, u32[]{:S(2)}) collective-permute-start(bf16[4,512,128]{2,1,0:T(8,128)(2,1)S(1)} %collective-permute-done.1.x), channel_id=1, source_target_pairs={{0,4},{1,5},{2,6},{3,7},{4,0},{5,1},{6,2},{7,3},{8,12},{9,13},{10,... | collective-permute-start | bytes 1572872 | tf_op jit(solution)/shard_map/ppermute | solution.py:62
  24.4 15.1 %collective-permute-start.11 = (bf16[256,512]{1,0:T(8,128)(2,1)S(1)}, bf16[256,512]{1,0:T(8,128)(2,1)S(1)}, u32[]{:S(2)}, u32[]{:S(2)}) collective-permute-start(bf16[256,512]{1,0:T(8,128)(2,1)S(1)} %get-tuple-element.15), channel_id=1, source_target_pairs={{0,16},{24,8},{1,17},{25,9},{2,18},{26,10},{3,19},{27,11},{4,20},{... | collective-permute-start | bytes 786440 | tf_op jit(solution)/shard_map/ppermute | solution.py:66
  32.4 12.3 %collective-permute-start.13 = (bf16[256,512]{1,0:T(8,128)(2,1)S(1)}, bf16[256,512]{1,0:T(8,128)(2,1)S(1)}, u32[]{:S(2)}, u32[]{:S(2)}) collective-permute-start(bf16[256,512]{1,0:T(8,128)(2,1)S(1)} %get-tuple-element.16), channel_id=1, source_target_pairs={{0,16},{24,8},{1,17},{25,9},{2,18},{26,10},{3,19},{27,11},{4,20},{... | collective-permute-start | bytes 786440 | tf_op jit(solution)/shard_map/ppermute | solution.py:66
  33.7 12.3 %collective-permute-start.8 = (bf16[256,512]{1,0:T(8,128)(2,1)S(1)}, bf16[256,512]{1,0:T(8,128)(2,1)S(1)}, u32[]{:S(2)}, u32[]{:S(2)}) collective-permute-start(bf16[256,512]{1,0:T(8,128)(2,1)S(1)} %collective-permute-done.4.inner_b), channel_id=1, source_target_pairs={{8,0},{16,24},{9,1},{17,25},{10,2},{18,26},{11,3},{19,27},{12,4},{... | collective-permute-start | bytes 786440 | tf_op jit(solution)/shard_map/ppermute | solution.py:66
  35.2 12.6 %collective-permute-start.9 = (bf16[256,512]{1,0:T(8,128)(2,1)S(1)}, bf16[256,512]{1,0:T(8,128)(2,1)S(1)}, u32[]{:S(2)}, u32[]{:S(2)}) collective-permute-start(bf16[256,512]{1,0:T(8,128)(2,1)S(1)} %pad_maximum_fusion.1), channel_id=1, source_target_pairs={{0,16},{24,8},{1,17},{25,9},{2,18},{26,10},{3,19},{27,11},{4,20},{... | collective-permute-start | bytes 786440 | tf_op jit(solution)/shard_map/ppermute | solution.py:66
  39.5 13.9 %collective-permute-start.12 = (bf16[256,512]{1,0:T(8,128)(2,1)S(1)}, bf16[256,512]{1,0:T(8,128)(2,1)S(1)}, u32[]{:S(2)}, u32[]{:S(2)}) collective-permute-start(bf16[256,512]{1,0:T(8,128)(2,1)S(1)} %collective-permute-done.11.inner_a), channel_id=1, source_target_pairs={{8,0},{16,24},{9,1},{17,25},{10,2},{18,26},{11,3},{19,27},{12,4},{... | collective-permute-start | bytes 786440 | tf_op jit(solution)/shard_map/ppermute | solution.py:66
  44.7 11.3 %collective-permute-start.14 = (bf16[256,512]{1,0:T(8,128)(2,1)S(1)}, bf16[256,512]{1,0:T(8,128)(2,1)S(1)}, u32[]{:S(2)}, u32[]{:S(2)}) collective-permute-start(bf16[256,512]{1,0:T(8,128)(2,1)S(1)} %collective-permute-done.13.inner_b), channel_id=1, source_target_pairs={{8,0},{16,24},{9,1},{17,25},{10,2},{18,26},{11,3},{19,27},{12,4},{... | collective-permute-start | bytes 786440 | tf_op jit(solution)/shard_map/ppermute | solution.py:66
  47.8 11.1 %collective-permute-start.10 = (bf16[256,512]{1,0:T(8,128)(2,1)S(1)}, bf16[256,512]{1,0:T(8,128)(2,1)S(1)}, u32[]{:S(2)}, u32[]{:S(2)}) collective-permute-start(bf16[256,512]{1,0:T(8,128)(2,1)S(1)} %collective-permute-done.9.from_inner), channel_id=1, source_target_pairs={{8,0},{16,24},{9,1},{17,25},{10,2},{18,26},{11,3},{19,27},{12,4},{... | collective-permute-start | bytes 786440 | tf_op jit(solution)/shard_map/ppermute | solution.py:66
